TPU v7x, 512 devices: a whole 4x8x8 slice. The times are simulated.
512 devices in a mesh: rep: 4 (over x), ep: 128 (over z, y, core).
Axes of the slice: x: 4, y: 8, z: 8, core: 2. Of those that a mesh axis runs over, the one named last changes fastest.
Arguments:
- tokens: bfloat16 [16384, 2048], P('ep', 'rep'), may hold values from -6 to 6
- out_grad: bfloat16 [16384, 2048], P('ep', 'rep'), may hold values from -6 to 6
- expert_ids: int32 [16384, 8], P('ep'), may hold values from 0 to 127, all different within a row; in each aligned block of 128 rows (0 to 127, 128 to 255, ...) at most 9 rows name the same one
- route_weight: bfloat16 [16384, 8], P('ep'), may hold values from 0.019897461 to 0.29882812
- w_gate: bfloat16 [128, 2048, 640], P('ep', 'rep'), may hold values from -0.125 to 0.125
- w_up: bfloat16 [128, 2048, 640], P('ep', 'rep'), may hold values from -0.125 to 0.125
- w_down: bfloat16 [128, 640, 2048], P('ep', None, 'rep'), may hold values from -0.25 to 0.25
Outputs:
- token_grad: bfloat16 [16384, 2048], P('ep', 'rep')
- grad_gate: bfloat16 [128, 2048, 640], P('ep', 'rep')
- grad_up: bfloat16 [128, 2048, 640], P('ep', 'rep')
- grad_down: bfloat16 [128, 640, 2048], P('ep', None, 'rep')
Inputs may be any that keep to these rules, and one draw needn't show every extreme that they name: `expert_ids`: each token picks 8 different experts. Among the 128 tokens of one index of ep no expert is picked by more than 9 tokens, and in every draw some expert is picked by exactly 9 tokens of some such index.
All inputs are finite; a program needn't handle non-finite values.
Results may differ from a plain program's by a relative error of at most 0.024.
Values may be sent and summed in bfloat16 or wider, within the bound.
No kernel may reach another device: no remote copies, remote signals or barrier semaphores. Data moves between devices by JAX's collectives and lax.ppermute only.
A program may use at most 64 MiB of HBM per device.

v0:
```python
import jax
import jax.numpy as jnp
from jax import lax
from jax.sharding import PartitionSpec as P

CAP = 9


def hidden_terms(pre_gate, pre_up, pre_back, weight):
    sigmoid_gate = jax.nn.sigmoid(pre_gate)
    silu_gate = pre_gate * sigmoid_gate
    d_hidden = weight[..., None] * pre_back
    hidden = (silu_gate * pre_up).astype(jnp.bfloat16)
    gate_delta = (
        d_hidden * pre_up * sigmoid_gate * (1.0 + pre_gate * (1.0 - sigmoid_gate))
    ).astype(jnp.bfloat16)
    up_delta = (d_hidden * silu_gate).astype(jnp.bfloat16)
    return (hidden, gate_delta, up_delta)


def body(tokens, out_grad, expert_ids, route_weight, w_gate, w_up, w_down):
    ep_ranks = lax.axis_size("ep")
    local_count = w_gate.shape[0]
    experts = local_count * ep_ranks
    quarter = tokens.shape[1]
    slot_rows = ep_ranks * CAP
    slot_total = experts * CAP
    expert_range = jnp.arange(experts, dtype=jnp.int32)
    matches = expert_ids[:, :, None] == expert_range[None, None, :]
    picked = jnp.sum(matches.astype(jnp.int32), axis=1)
    before = jnp.cumsum(picked, axis=0) - picked
    position = jnp.sum(jnp.where(matches, before[:, None, :], 0), axis=2)
    owner_col = expert_ids // local_count
    within = expert_ids % local_count
    slot_index = (within * ep_ranks + owner_col) * CAP + position
    select = slot_index[:, :, None] == jnp.arange(slot_total, dtype=jnp.int32)[None, None, :]
    placing = jnp.any(select, axis=1).astype(jnp.bfloat16)
    send_tokens = jnp.einsum("ts,td->sd", placing, tokens, preferred_element_type=jnp.float32)
    send_tokens = send_tokens.astype(jnp.bfloat16).reshape(local_count, ep_ranks, CAP, quarter)
    send_grads = jnp.einsum("ts,td->sd", placing, out_grad, preferred_element_type=jnp.float32)
    send_grads = send_grads.astype(jnp.bfloat16).reshape(local_count, ep_ranks, CAP, quarter)
    send_weight = jnp.sum(
        jnp.where(select, route_weight.astype(jnp.float32)[:, :, None], 0.0), axis=(0, 1)
    )
    send_weight = send_weight.astype(jnp.bfloat16).reshape(local_count, ep_ranks, CAP)
    routed_tokens, routed_grads, routed_weight = (
        lax.all_to_all(send_tokens, "ep", split_axis=1, concat_axis=1, tiled=True),
        lax.all_to_all(send_grads, "ep", split_axis=1, concat_axis=1, tiled=True),
        lax.all_to_all(send_weight, "ep", split_axis=1, concat_axis=1, tiled=True),
    )
    routed_tokens = routed_tokens.reshape(local_count, slot_rows, quarter)
    part_gate = jnp.einsum(
        "erd,edf->erf", routed_tokens, w_gate, preferred_element_type=jnp.float32
    )
    part_up = jnp.einsum("erd,edf->erf", routed_tokens, w_up, preferred_element_type=jnp.float32)
    routed_grads = routed_grads.reshape(local_count, slot_rows, quarter)
    part_back = jnp.einsum("erd,efd->erf", routed_grads, w_down, preferred_element_type=jnp.float32)
    weight = routed_weight.reshape(local_count, slot_rows).astype(jnp.float32)
    pre_gate, pre_up, pre_back = (
        lax.psum(part_gate.astype(jnp.bfloat16), "rep").astype(jnp.float32),
        lax.psum(part_up.astype(jnp.bfloat16), "rep").astype(jnp.float32),
        lax.psum(part_back.astype(jnp.bfloat16), "rep").astype(jnp.float32),
    )
    hidden, gate_delta, up_delta = hidden_terms(pre_gate, pre_up, pre_back, weight)
    scaled_grad = (weight[:, :, None] * routed_grads.astype(jnp.float32)).astype(jnp.bfloat16)
    back_rows = jnp.einsum("erf,edf->erd", gate_delta, w_gate, preferred_element_type=jnp.float32)
    back_rows = back_rows + jnp.einsum(
        "erf,edf->erd", up_delta, w_up, preferred_element_type=jnp.float32
    )
    back_rows = back_rows.astype(jnp.bfloat16).reshape(local_count, ep_ranks, CAP, quarter)
    returned = lax.all_to_all(back_rows, "ep", split_axis=1, concat_axis=1, tiled=True)
    grad_gate = jnp.einsum(
        "erd,erf->edf", routed_tokens, gate_delta, preferred_element_type=jnp.float32
    ).astype(jnp.bfloat16)
    grad_up = jnp.einsum(
        "erd,erf->edf", routed_tokens, up_delta, preferred_element_type=jnp.float32
    ).astype(jnp.bfloat16)
    grad_down = jnp.einsum(
        "erf,erd->efd", hidden, scaled_grad, preferred_element_type=jnp.float32
    ).astype(jnp.bfloat16)
    token_grad = jnp.einsum(
        "ts,sd->td",
        placing,
        returned.reshape(slot_total, quarter),
        preferred_element_type=jnp.float32,
    )
    return (token_grad.astype(jnp.bfloat16), grad_gate, grad_up, grad_down)


def solution(mesh):
    placed = (
        P("ep", "rep"),
        P("ep", "rep"),
        P("ep", None),
        P("ep", None),
        P("ep", "rep", None),
        P("ep", "rep", None),
        P("ep", None, "rep"),
    )
    return jax.shard_map(
        body,
        mesh=mesh,
        in_specs=placed,
        out_specs=(
            P("ep", "rep"),
            P("ep", "rep", None),
            P("ep", "rep", None),
            P("ep", None, "rep"),
        ),
        check_vma=False,
    )
```

profile of v0, /device:TPU:1, one launch (start us, length us, event | category | flops | bytes accessed | tf_op | source)
XLA Modules:
  0.0 343.4 jit_solution(13522083225533455690)
XLA Ops:
  7.2 0.0 copy-start
  7.2 0.9 copy.35
  8.0 0.2 convert_reduce_fusion
  8.3 0.2 reduce_window_sum.11
  8.4 2.4 select_reduce_fusion.1
  10.9 0.7 multiply_add_fusion
  11.6 0.1 copy.37
  11.7 0.6 copy-done.11
  12.3 1.5 fusion
  13.8 1.4 convolution_convert_fusion.3
  15.2 1.6 reshape.170
  16.8 18.6 %all-to-all-start.2 = ((bf16[1,128,9,512]{3,2,0,1:T(8,128)(2,1)}), bf16[1,128,9,512]{3,2,0,1:T(8,128)(2,1)S(1)}, u32[]{:S(2)}, u32[]{:S(2)}) async-start(bf16[1,128,9,512]{3,2,0,1:T(8,128)(2,1)} %bitcast.72), calls=%async_computation.2 | async-start | bytes 4194304 | tf_op jit(solution)/shard_map/all_to_all | solution.py:47
  35.4 1.5 convolution_convert_fusion.4
  36.9 3.3 reshape.167
  40.2 46.4 %all-to-all-done.2 = bf16[1,128,9,512]{3,2,0,1:T(8,128)(2,1)S(1)} async-done(((bf16[1,128,9,512]{3,2,0,1:T(8,128)(2,1)}), bf16[1,128,9,512]{3,2,0,1:T(8,128)(2,1)S(1)}, u32[]{:S(2)}, u32[]{:S(2)}) %all-to-all-start.2) | async-done | bytes 1179680 | tf_op jit(solution)/shard_map/all_to_all | solution.py:47
  86.6 1.3 copy-done.1
  87.9 8.8 %all-to-all-start.1 = ((bf16[1,128,9,512]{3,2,0,1:T(8,128)(2,1)}), bf16[1,128,9,512]{3,2,0,1:T(8,128)(2,1)S(1)}, u32[]{:S(2)}, u32[]{:S(2)}) async-start(bf16[1,128,9,512]{3,2,0,1:T(8,128)(2,1)} %bitcast.71), calls=%async_computation.1 | async-start | bytes 4194304 | tf_op jit(solution)/shard_map/all_to_all | solution.py:48
  96.8 0.0 copy-start.10
  96.8 0.2 all-reduce.3.cloned.1.call-start
  97.0 3.6 %reshape.171 = bf16[1152,512]{1,0:T(8,128)(2,1)} reshape(bf16[1,128,9,512]{3,2,0,1:T(8,128)(2,1)} %copy-done.1) | data formatting | bytes 2359296 | tf_op jit(solution)/shard_map/reshape.4
  100.6 3.6 %fusion.11 = bf16[1,1152,640]{2,1,0:T(8,128)(2,1)} fusion(bf16[1152,512]{1,0:T(8,128)(2,1)} %reshape.171, bf16[1,512,640]{2,1,0:T(8,128)(2,1)S(1)} %copy-done.10), kind=kOutput, calls=%fused_computation.26 | convolution fusion | flops 755712000 | bytes 3309568 | tf_op jit(solution)/shard_map/erd,edf->erf/dot_general | solution.py:55
  104.2 2.2 fusion.12
  106.4 41.6 %all-to-all-done.1 = bf16[1,128,9,512]{3,2,0,1:T(8,128)(2,1)S(1)} async-done(((bf16[1,128,9,512]{3,2,0,1:T(8,128)(2,1)}), bf16[1,128,9,512]{3,2,0,1:T(8,128)(2,1)S(1)}, u32[]{:S(2)}, u32[]{:S(2)}) %all-to-all-start.1) | async-done | bytes 1179680 | tf_op jit(solution)/shard_map/all_to_all | solution.py:48
  148.1 1.3 reshape.168
  149.4 3.7 %fusion.10 = bf16[1,1152,640]{2,1,0:T(8,128)(2,1)} fusion(bf16[1152,512]{1,0:T(8,128)(2,1)} %reshape.168, bf16[1,640,512]{2,1,0:T(8,128)(2,1)} %param.13), kind=kOutput, calls=%fused_computation.25 | convolution fusion | flops 755712000 | bytes 3309568 | tf_op jit(solution)/shard_map/erd,efd->erf/dot_general | solution.py:57
  153.1 0.0 all-reduce.3.cloned.1.call-update
  153.2 1.4 copy.38
  154.6 2.1 select_reduce_fusion
  156.6 1.6 convert_element_type.176
  158.2 20.2 %all_to_all.20 = bf16[1,128,9]{2,0,1:T(2,128)(2,1)S(1)} all-to-all(bf16[1,128,9]{2,0,1:T(2,128)(2,1)} %convert_element_type.176), channel_id=1, replica_groups=mesh['rep'=4,'ep'=128] {'ep'}, dimensions={1} | all-to-all | bytes 4608 | tf_op jit(solution)/shard_map/all_to_all | solution.py:49
  178.4 0.8 convert_reduce_fusion.1
  179.2 1.6 reshape.179
  180.9 75.9 %all-reduce.3.cloned.1.call-done = (bf16[1,1152,640]{2,1,0:T(8,128)(2,1)}, bf16[1,1152,640]{2,1,0:T(8,128)(2,1)}, bf16[1,1152,640]{2,1,0:T(8,128)(2,1)}) async-done(((bf16[1,1152,640]{2,1,0:T(8,128)(2,1)}, bf16[1,1152,640]{2,1,0:T(8,128)(2,1)}, bf16[1,1152,640]{2,1,0:T(8,128)(2,1)}), (bf16[1,1152,640]{2,1,0:T(8,128)(2,1)}, bf16[1,1152,640]{2,1,0:T(8,128)(2,1)}, ...) | async-done | bytes 4423696 | tf_op jit(solution)/shard_map/psum | solution.py:61
  256.8 3.5 %fusion.13 = (bf16[1152,640]{1,0:T(8,128)(2,1)S(1)}, bf16[1,1152,640]{2,1,0:T(8,128)(2,1)S(1)}) fusion(bf16[1,1152,640]{2,1,0:T(8,128)(2,1)} %get-tuple-element.6, f32[1152]{0:T(1024)} %reshape.179, bf16[1,1152,640]{2,1,0:T(8,128)(2,1)} %get-tuple-element.5, bf16[1,1152,640]{2,1,0:T(8,128)(2,1)} %get-tuple-element.4), kind=kLoop, calls=%fused_computation.29 | loop fusion | flops 12533760 | bytes 7377408 | tf_op jit(solution)/shard_map/reshape.25
  260.3 1.1 fusion.19
  261.4 0.4 copy-done.2
  261.9 2.2 fusion.1
  264.0 3.3 reshape.176
  267.3 14.8 %all-to-all-start.3 = ((bf16[1,128,9,512]{3,2,0,1:T(8,128)(2,1)}), bf16[1,128,9,512]{3,2,0,1:T(8,128)(2,1)}, u32[]{:S(2)}, u32[]{:S(2)}) async-start(bf16[1,128,9,512]{3,2,0,1:T(8,128)(2,1)} %bitcast.70), calls=%async_computation.3 | async-start | bytes 4194304 | tf_op jit(solution)/shard_map/all_to_all | solution.py:71
  282.1 0.0 copy-start.13
  282.1 4.2 %reshape.180 = f32[1,1152,1,1,1,1,512]{6,0,1,5,4,3,2:T(1,128)} reshape(bf16[1,128,9,512]{3,2,0,1:T(8,128)(2,1)S(1)} %all-to-all-done.1) | data formatting | bytes 3538944 | tf_op jit(solution)/shard_map/convert_element_type | solution.py:65
  286.4 5.4 %multiply_convert_fusion.1 = bf16[1,1152,1,1,1,1,512]{6,0,1,5,4,3,2:T(2,128)(2,1)S(1)} fusion(f32[1,1152,1,1,1,1,512]{6,0,1,5,4,3,2:T(1,128)} %reshape.180, f32[1152]{0:T(1024)S(1)} %copy-done.13), kind=kLoop, calls=%fused_computation.28 | loop fusion | flops 1179648 | bytes 3543552 | tf_op jit(solution)/shard_map/convert_element_type | solution.py:65
  291.8 2.0 fusion.27
  293.8 2.0 fusion.28
  295.9 2.2 fusion.31
  298.1 34.9 %all-to-all-done.3 = bf16[1,128,9,512]{3,2,0,1:T(8,128)(2,1)} async-done(((bf16[1,128,9,512]{3,2,0,1:T(8,128)(2,1)}), bf16[1,128,9,512]{3,2,0,1:T(8,128)(2,1)}, u32[]{:S(2)}, u32[]{:S(2)}) %all-to-all-start.3) | async-done | bytes 1179680 | tf_op jit(solution)/shard_map/all_to_all | solution.py:71
  333.0 2.5 reshape.177
  335.6 1.0 convolution_convert_fusion.6
  (24 shorter events, 0.1 us)
Async XLA Ops:
  7.2 97.0 %copy-start = (bf16[1,512,640]{2,1,0:T(8,128)(2,1)S(1)}, bf16[1,512,640]{2,1,0:T(8,128)(2,1)}, u32[]{:S(2)}) copy-start(bf16[1,512,640]{2,1,0:T(8,128)(2,1)} %param.11) | copy-start | bytes 1966084
  11.7 0.6 copy-start.11
  16.8 18.6 %copy-start.12 = (bf16[128,512]{1,0:T(8,128)(2,1)S(1)}, bf16[128,512]{1,0:T(8,128)(2,1)}, u32[]{:S(2)}) copy-start(bf16[128,512]{1,0:T(8,128)(2,1)} %param.8) | copy-start | bytes 393220
  16.8 69.8 %all-to-all-start.2 = ((bf16[1,128,9,512]{3,2,0,1:T(8,128)(2,1)}), bf16[1,128,9,512]{3,2,0,1:T(8,128)(2,1)S(1)}, u32[]{:S(2)}, u32[]{:S(2)}) async-start(bf16[1,128,9,512]{3,2,0,1:T(8,128)(2,1)} %bitcast.72), calls=%async_computation.2 | async-start | bytes 4194304 | tf_op jit(solution)/shard_map/all_to_all | solution.py:47
  86.6 1.3 copy-start.1
  87.9 60.1 %all-to-all-start.1 = ((bf16[1,128,9,512]{3,2,0,1:T(8,128)(2,1)}), bf16[1,128,9,512]{3,2,0,1:T(8,128)(2,1)S(1)}, u32[]{:S(2)}, u32[]{:S(2)}) async-start(bf16[1,128,9,512]{3,2,0,1:T(8,128)(2,1)} %bitcast.71), calls=%async_computation.1 | async-start | bytes 4194304 | tf_op jit(solution)/shard_map/all_to_all | solution.py:48
  96.8 3.8 %copy-start.10 = (bf16[1,512,640]{2,1,0:T(8,128)(2,1)S(1)}, bf16[1,512,640]{2,1,0:T(8,128)(2,1)}, u32[]{:S(2)}) copy-start(bf16[1,512,640]{2,1,0:T(8,128)(2,1)} %param.12) | copy-start | bytes 1966084
  96.8 160.0 %all-reduce.3.cloned.1.call-start = ((), (), s32[]{:S(2)}) async-start(), calls=%async_computation.4 | async-start | bytes 8847360 | tf_op jit(solution)/shard_map/psum | solution.py:61
  100.6 3.6 %copy-start.8 = (bf16[1152,512]{1,0:T(8,128)(2,1)S(1)}, bf16[1152,512]{1,0:T(8,128)(2,1)}, u32[]{:S(2)}) copy-start(bf16[1152,512]{1,0:T(8,128)(2,1)} %reshape.171) | copy-start | bytes 3538948
  260.3 1.1 copy-start.6
  260.3 1.6 copy-start.2
  267.3 65.7 %all-to-all-start.3 = ((bf16[1,128,9,512]{3,2,0,1:T(8,128)(2,1)}), bf16[1,128,9,512]{3,2,0,1:T(8,128)(2,1)}, u32[]{:S(2)}, u32[]{:S(2)}) async-start(bf16[1,128,9,512]{3,2,0,1:T(8,128)(2,1)} %bitcast.70), calls=%async_computation.3 | async-start | bytes 4194304 | tf_op jit(solution)/shard_map/all_to_all | solution.py:71
  282.1 4.3 %copy-start.13 = (f32[1152]{0:T(1024)S(1)}, f32[1152]{0:T(1024)}, u32[]{:S(2)}) copy-start(f32[1152]{0:T(1024)} %reshape.179) | copy-start | bytes 13828
  286.4 5.4 %copy-start.3 = (bf16[1152,640]{1,0:T(8,128)(2,1)S(1)}, bf16[1152,640]{1,0:T(8,128)(2,1)}, u32[]{:S(2)}) copy-start(bf16[1152,640]{1,0:T(8,128)(2,1)} %copy-done.2) | copy-start | bytes 4423684
  286.4 5.4 %copy-start.9 = (bf16[1152,512]{1,0:T(8,128)(2,1)S(1)}, bf16[1152,512]{1,0:T(8,128)(2,1)}, u32[]{:S(2)}) copy-start(bf16[1152,512]{1,0:T(8,128)(2,1)} %reshape.171) | copy-start | bytes 3538948
  291.8 2.1 copy-start.7
  293.8 2.1 copy-start.4
  293.8 2.1 copy-start.5
Sparse Core Ops, SparseCore 0:
  153.3 103.4 all-reduce.2
where the time goes:
time: 346 us; the launch traced here: 343 us
  waiting for transfers between devices  199 us (58%)
  starting transfers between devices  42.4 us (12%)
  local copies, waits for them, and re-layouts  27.9 us (8%)
  matrix products  23.1 us (7%)
  blocking collectives  20.2 us (6%)
  other arithmetic  16.7 us (5%)
  between operations  14.2 us (4%)
    psum x1, waiting for transfers between devices, body(): lax.psum(part_up.astype(jnp.bfloat16), 'rep').astype(jnp.float32)  75.9 us
    all_to_all x1, waiting for transfers between devices, body(): lax.all_to_all(send_tokens, 'ep', split_axis=1, concat_axis=1, tiled=True)  46.4 us
    all_to_all x1, waiting for transfers between devices, body(): lax.all_to_all(send_grads, 'ep', split_axis=1, concat_axis=1, tiled=True)  41.6 us
    all_to_all x1, waiting for transfers between devices, body(): lax.all_to_all(back_rows, 'ep', split_axis=1, concat_axis=1, tiled=True)  34.9 us
    all_to_all x1, blocking collectives, body(): lax.all_to_all(send_weight, 'ep', split_axis=1, concat_axis=1, tiled=True)  20.2 us
    all_to_all x1, starting transfers between devices, body(): lax.all_to_all(send_tokens, 'ep', split_axis=1, concat_axis=1, tiled=True)  18.6 us
    all_to_all x1, starting transfers between devices, body(): lax.all_to_all(back_rows, 'ep', split_axis=1, concat_axis=1, tiled=True)  14.8 us
    all_to_all x1, starting transfers between devices, body(): lax.all_to_all(send_grads, 'ep', split_axis=1, concat_axis=1, tiled=True)  8.85 us
  transfers between devices with their start and end apart: 4, of which 4 were waited for; matrix products, arithmetic and copies ran while one was open for 11% of the time, Pallas kernels for 0%

commit v1 on v0

v1 whole, which is shorter than its diff:
```python
import jax
import jax.numpy as jnp
from jax import lax
from jax.experimental import pallas as pl
from jax.experimental.pallas import tpu as pltpu
from jax.sharding import PartitionSpec as P

MAIN = 8
LANES = 128
BF = jnp.bfloat16
F32 = jnp.float32
CONTRACT_LAST = (((1,), (1,)), ((), ()))
CONTRACT_FIRST = (((0,), (0,)), ((), ()))


def dot(a, b, dims=(((1,), (0,)), ((), ()))):
    return lax.dot_general(a, b, dims, preferred_element_type=F32)


def kernel_call(body, out_shape, args, flops, scratch=()):
    moved = sum(a.size * a.dtype.itemsize for a in args)
    outs = out_shape if isinstance(out_shape, tuple) else (out_shape,)
    moved += sum(o.size * o.dtype.itemsize for o in outs)
    return pl.pallas_call(
        body,
        out_shape=out_shape,
        in_specs=[pl.BlockSpec(memory_space=pltpu.VMEM)] * len(args),
        out_specs=jax.tree.map(lambda _: pl.BlockSpec(memory_space=pltpu.VMEM), out_shape),
        scratch_shapes=list(scratch),
        compiler_params=pltpu.CompilerParams(vmem_limit_bytes=48 << 20),
        cost_estimate=pl.CostEstimate(flops=flops, bytes_accessed=moved, transcendentals=0),
    )(*args)


def routing(ids_ref, experts):
    top, count = ids_ref.shape
    expert = lax.broadcasted_iota(jnp.int32, (experts, count), 0)
    matches = [expert == ids_ref[k : k + 1, :] for k in range(top)]
    picked = sum(m.astype(F32) for m in matches)
    earlier = lax.broadcasted_iota(jnp.int32, (count, count), 0) < lax.broadcasted_iota(
        jnp.int32, (count, count), 1
    )
    before = dot(picked.astype(BF), earlier.astype(F32).astype(BF))
    return jnp.where(picked > 0.0, before, -1.0), matches


def spread(per_expert):
    experts, count = per_expert.shape
    wide = jnp.broadcast_to(per_expert[:, None, :], (experts, MAIN, count))
    return wide.reshape(experts * MAIN, count)


def main_slots(slot):
    experts, count = slot.shape
    number = lax.broadcasted_iota(jnp.int32, (experts * MAIN, count), 0) % MAIN
    return spread(slot) == number.astype(F32)


def dispatch_kernel(ids_ref, weight_ref, tokens_ref, grads_ref, first_ref, second_ref, packed):
    experts = first_ref.shape[0] // MAIN
    quarter = tokens_ref.shape[1]
    slot, matches = routing(ids_ref, experts)
    weight = sum(
        jnp.where(m, weight_ref[k : k + 1, :], 0.0) for k, m in enumerate(matches)
    )
    here = main_slots(slot)
    first_ref[...] = dot(jnp.where(here, 1.0, 0.0).astype(BF), tokens_ref[...]).astype(BF)
    second_ref[:, :quarter] = dot(
        jnp.where(here, spread(weight), 0.0).astype(BF), grads_ref[...]
    ).astype(BF)
    last = slot == float(MAIN)
    extra_tokens = dot(jnp.where(last, 1.0, 0.0).astype(BF), tokens_ref[...])
    extra_grads = dot(jnp.where(last, weight, 0.0).astype(BF), grads_ref[...])
    pieces = quarter // LANES
    for j in range(pieces):
        packed[:, j, :] = extra_tokens[:, j * LANES : (j + 1) * LANES]
        packed[:, pieces + j, :] = extra_grads[:, j * LANES : (j + 1) * LANES]
    second_ref[:, quarter:] = packed[...].reshape(experts * MAIN, LANES).astype(BF)


def token_products_kernel(rows_ref, gate_ref, up_ref, out_ref):
    ffw = gate_ref.shape[1]
    for r in range(4):
        n = rows_ref.shape[0] // 4
        rows = rows_ref[r * n : (r + 1) * n, :]
        out_ref[r * n : (r + 1) * n, :ffw] = dot(rows, gate_ref[...]).astype(BF)
        out_ref[r * n : (r + 1) * n, ffw:] = dot(rows, up_ref[...]).astype(BF)


def grad_products_kernel(
    rows_ref, gate_ref, up_ref, down_ref, out_ref, extra_tokens_ref, extra_grads_ref, packed
):
    quarter = gate_ref.shape[0]
    sources = rows_ref.shape[0] // MAIN
    pieces = quarter // LANES
    packed[...] = rows_ref[:, quarter:].astype(F32).reshape(sources, MAIN, LANES)
    for j in range(pieces):
        extra_tokens_ref[:, j * LANES : (j + 1) * LANES] = packed[:, j, :].astype(BF)
        extra_grads_ref[:, j * LANES : (j + 1) * LANES] = packed[:, pieces + j, :].astype(BF)
    extra = (
        dot(extra_tokens_ref[...], gate_ref[...]).astype(BF),
        dot(extra_tokens_ref[...], up_ref[...]).astype(BF),
        dot(extra_grads_ref[...], down_ref[...], CONTRACT_LAST).astype(BF),
    )
    n = rows_ref.shape[0] // 4
    m = sources // 4
    for r in range(4):
        at = r * (n + 3 * m)
        rows = rows_ref[r * n : (r + 1) * n, :quarter]
        out_ref[at : at + n, :] = dot(rows, down_ref[...], CONTRACT_LAST).astype(BF)
        for i in range(3):
            out_ref[at + n + i * m : at + n + (i + 1) * m, :] = extra[i][r * m : (r + 1) * m, :]


def hidden_kernel(tokens_side_ref, grads_side_ref, delta_ref, hidden_ref):
    n = tokens_side_ref.shape[0]
    ffw = grads_side_ref.shape[1]
    m = (grads_side_ref.shape[0] - n) // 3

    def terms(gate, up, back, at, size):
        gate, up, back = gate.astype(F32), up.astype(F32), back.astype(F32)
        sigmoid = 1.0 / (1.0 + jnp.exp(-gate))
        silu = gate * sigmoid
        hidden_ref[at : at + size, :] = (silu * up).astype(BF)
        delta_ref[at : at + size, :ffw] = (
            back * up * sigmoid * (1.0 + gate * (1.0 - sigmoid))
        ).astype(BF)
        delta_ref[at : at + size, ffw:] = (back * silu).astype(BF)

    terms(tokens_side_ref[:, :ffw], tokens_side_ref[:, ffw:], grads_side_ref[:n, :], 0, n)
    terms(
        grads_side_ref[n : n + m, :],
        grads_side_ref[n + m : n + 2 * m, :],
        grads_side_ref[n + 2 * m :, :],
        n,
        m,
    )


def back_kernel(delta_ref, gate_ref, up_ref, out_ref, packed):
    quarter, ffw = gate_ref.shape
    n = out_ref.shape[0] // 4
    m = n // MAIN
    for r in range(4):
        at = r * (n + m)
        rows = dot(delta_ref[at : at + n + m, :ffw], gate_ref[...], CONTRACT_LAST)
        rows = rows + dot(delta_ref[at : at + n + m, ffw:], up_ref[...], CONTRACT_LAST)
        out_ref[r * n : (r + 1) * n, :quarter] = rows[:n, :].astype(BF)
        for j in range(quarter // LANES):
            packed[r * m : (r + 1) * m, j, :] = rows[n:, j * LANES : (j + 1) * LANES]
    for j in range(quarter // LANES, MAIN):
        packed[:, j, :] = jnp.zeros((4 * m, LANES), F32)
    out_ref[:, quarter:] = packed[...].reshape(4 * n, LANES).astype(BF)


def token_weights_kernel(rows_ref, extra_ref, delta_ref, gate_ref, up_ref):
    ffw = gate_ref.shape[1]
    n = rows_ref.shape[0] // 4
    m = extra_ref.shape[0] // 4
    total = None
    for r in range(4):
        at = r * (n + m)
        part = dot(rows_ref[r * n : (r + 1) * n, :], delta_ref[at : at + n, :], CONTRACT_FIRST)
        part = part + dot(
            extra_ref[r * m : (r + 1) * m, :], delta_ref[at + n : at + n + m, :], CONTRACT_FIRST
        )
        total = part if total is None else total + part
    gate_ref[...] = total[:, :ffw].astype(BF)
    up_ref[...] = total[:, ffw:].astype(BF)


def down_weights_kernel(rows_ref, extra_ref, hidden_ref, down_ref):
    quarter = extra_ref.shape[1]
    n = rows_ref.shape[0] // 4
    m = extra_ref.shape[0] // 4
    total = None
    for r in range(4):
        at = r * (n + m)
        part = dot(
            hidden_ref[at : at + n, :], rows_ref[r * n : (r + 1) * n, :quarter], CONTRACT_FIRST
        )
        part = part + dot(
            hidden_ref[at + n : at + n + m, :], extra_ref[r * m : (r + 1) * m, :], CONTRACT_FIRST
        )
        total = part if total is None else total + part
    down_ref[...] = total.astype(BF)


def combine_kernel(ids_ref, rows_ref, out_ref, packed):
    experts = rows_ref.shape[0] // MAIN
    quarter = out_ref.shape[1]
    slot, _ = routing(ids_ref, experts)
    here = jnp.where(main_slots(slot), 1.0, 0.0).astype(BF)
    last = jnp.where(slot == float(MAIN), 1.0, 0.0).astype(BF)
    packed[...] = rows_ref[:, quarter:].astype(F32).reshape(experts, MAIN, LANES)
    total = dot(here, rows_ref[:, :quarter], CONTRACT_FIRST)
    for j in range(quarter // LANES):
        at = slice(j * LANES, (j + 1) * LANES)
        extra = dot(last, packed[:, j, :].astype(BF), CONTRACT_FIRST)
        out_ref[:, at] = (total[:, at] + extra).astype(BF)


def body(tokens, out_grad, expert_ids, route_weight, w_gate, w_up, w_down):
    experts = lax.axis_size("ep")
    count, quarter = tokens.shape
    w_gate, w_up, w_down = w_gate[0], w_up[0], w_down[0]
    ffw = w_gate.shape[1]
    main = experts * MAIN
    local = main // 4
    extra = experts // 4
    shape = jax.ShapeDtypeStruct
    packed = pltpu.VMEM((experts, MAIN, LANES), F32)

    def exchange(rows):
        blocks = rows.reshape(experts, MAIN, rows.shape[1])
        blocks = lax.all_to_all(blocks, "ep", split_axis=0, concat_axis=0, tiled=True)
        return blocks.reshape(rows.shape)

    ids = expert_ids.T
    first, second = kernel_call(
        dispatch_kernel,
        (shape((main, quarter), BF), shape((main, quarter + LANES), BF)),
        (ids, route_weight.T.astype(F32), tokens, out_grad),
        4 * main * count * quarter,
        (packed,),
    )
    token_rows = exchange(first)
    token_rows, second = lax.optimization_barrier((token_rows, second))
    grad_rows = exchange(second)
    products = kernel_call(
        token_products_kernel,
        shape((main, 2 * ffw), BF),
        (token_rows, w_gate, w_up),
        4 * main * quarter * ffw,
    )
    tokens_side = lax.psum_scatter(products, "rep", scatter_dimension=0, tiled=True)
    products, extra_tokens, extra_grads = kernel_call(
        grad_products_kernel,
        (
            shape((main + 3 * experts, ffw), BF),
            shape((experts, quarter), BF),
            shape((experts, quarter), BF),
        ),
        (grad_rows, w_gate, w_up, w_down),
        2 * (main + 3 * experts) * quarter * ffw,
        (packed,),
    )
    grads_side = lax.psum_scatter(products, "rep", scatter_dimension=0, tiled=True)
    delta, hidden = kernel_call(
        hidden_kernel,
        (shape((local + extra, 2 * ffw), BF), shape((local + extra, ffw), BF)),
        (tokens_side, grads_side),
        20 * (local + extra) * ffw,
    )
    delta = lax.all_gather(delta, "rep", axis=0, tiled=True)
    delta, hidden = lax.optimization_barrier((delta, hidden))
    hidden = lax.all_gather(hidden, "rep", axis=0, tiled=True)
    back = kernel_call(
        back_kernel,
        shape((main, quarter + LANES), BF),
        (delta, w_gate, w_up),
        4 * (main + experts) * quarter * ffw,
        (packed,),
    )
    returned = exchange(back)
    grad_gate, grad_up = kernel_call(
        token_weights_kernel,
        (shape((quarter, ffw), BF), shape((quarter, ffw), BF)),
        (token_rows, extra_tokens, delta),
        4 * (main + experts) * quarter * ffw,
    )
    grad_down = kernel_call(
        down_weights_kernel,
        shape((ffw, quarter), BF),
        (grad_rows, extra_grads, hidden),
        2 * (main + experts) * quarter * ffw,
    )
    token_grad = kernel_call(
        combine_kernel,
        shape((count, quarter), BF),
        (ids, returned),
        2 * main * count * quarter,
        (packed,),
    )
    return token_grad, grad_gate[None], grad_up[None], grad_down[None]


def solution(mesh):
    rows = P("ep", "rep")
    by_width = P("ep", "rep", None)
    last = P("ep", None, "rep")
    return jax.shard_map(
        body,
        mesh=mesh,
        in_specs=(rows, rows, P("ep", None), P("ep", None), by_width, by_width, last),
        out_specs=(rows, by_width, by_width, last),
        check_vma=False,
    )
```

time: 346 us -> 250 us (0.72)
  waiting for transfers between devices: 199 us -> 97.1 us
  blocking collectives: 20.2 us -> 91.6 us
  starting transfers between devices: 42.4 us -> 14.5 us
  matrix products: 23.1 us -> 0 us
  Pallas kernels: 0 us -> 18.7 us
  other arithmetic: 16.7 us -> 0.68 us
  local copies, waits for them, and re-layouts: 27.9 us -> 13 us
    all_to_all x3 -> x1, waiting for transfers between devices: 123 us -> 0.01 us  [exchange(): lax.all_to_all(blocks, 'ep', split_axis=0, concat_axis=0, tiled=True)]
    psum x1 -> x0, waiting for transfers between devices: 75.9 us -> none  [body(): lax.psum(part_up.astype(jnp.bfloat16), 'rep').astype(jnp.float32)]
    all_to_all x1 -> x2, blocking collectives: 20.2 us -> 91.6 us  [exchange(): lax.all_to_all(blocks, 'ep', split_axis=0, concat_axis=0, tiled=True)]
    all_gather x0 -> x2, waiting for transfers between devices: none -> 69.7 us  [the longest x1 43.1 us: body(): delta = lax.all_gather(delta, 'rep', axis=0, tiled=True)]
    all_to_all x3 -> x1, starting transfers between devices: 42.2 us -> 14.3 us  [exchange(): lax.all_to_all(blocks, 'ep', split_axis=0, concat_axis=0, tiled=True)]
    reduce_scatter x0 -> x2, waiting for transfers between devices: none -> 26.8 us  [body(): lax.psum_scatter(products, 'rep', scatter_dimension=0, tiled=True)]
    dot_general x11 -> x0, matrix products: 23.1 us -> none  [the longest x1 3.74 us: body(): jnp.einsum('erd,efd->erf', routed_grads, w_down, preferred_element_type=j...]
    pallas_call x0 -> x8, Pallas kernels: none -> 18.7 us  [kernel_call(): pl.pallas_call(body, out_shape=out_shape, in_specs=[pl.BlockSpec(memory_s...]
  transfers between devices with their start and end apart: 4 -> 5, of which waited for: 4 -> 3; matrix products, arithmetic and copies ran while one was open for 11% -> 0% of each run, Pallas kernels for 0% -> 4%
where the time goes in v1:
time: 250 us; the launch traced here: 249 us
  waiting for transfers between devices  97.1 us (39%)
  blocking collectives  91.6 us (37%)
  Pallas kernels  18.7 us (7%)
  starting transfers between devices  14.5 us (6%)
  between operations  13.8 us (6%)
  local copies, waits for them, and re-layouts  13 us (5%)
    all_to_all x2, blocking collectives, exchange(): lax.all_to_all(blocks, 'ep', split_axis=0, concat_axis=0, tiled=True)  91.6 us
    all_gather x1, waiting for transfers between devices, body(): delta = lax.all_gather(delta, 'rep', axis=0, tiled=True)  43.1 us
    reduce_scatter x2, waiting for transfers between devices, body(): lax.psum_scatter(products, 'rep', scatter_dimension=0, tiled=True)  26.8 us
    all_gather x1, waiting for transfers between devices, body(): hidden = lax.all_gather(hidden, 'rep', axis=0, tiled=True)  26.6 us
    pallas_call x8, Pallas kernels, kernel_call(): pl.pallas_call(body, out_shape=out_shape, in_specs=[pl.BlockSpec(memory_s...  18.7 us
    all_to_all x1, starting transfers between devices, exchange(): lax.all_to_all(blocks, 'ep', split_axis=0, concat_axis=0, tiled=True)  14.3 us
    unnamed x36, local copies, waits for them, and re-layouts  13 us
  transfers between devices with their start and end apart: 5, of which 3 were waited for; matrix products, arithmetic and copies ran while one was open for 0% of the time, Pallas kernels for 4%

profile of v1, /device:TPU:1, one launch (start us, length us, event | category | flops | bytes accessed | tf_op | source)
XLA Modules:
  0.0 249.4 jit_solution(12085989591096041706)
XLA Ops:
  7.2 0.0 reduce-scatter.3.cloned.1.call-start
  7.2 0.7 convert_bitcast_fusion.weight_ref
  7.9 0.7 copy-done.11
  8.6 0.0 copy-start.16
  8.6 0.9 copy-done.16
  9.5 0.9 copy-done.17
  10.4 1.2 shard_map.102
  11.6 49.1 %all_to_all.15 = bf16[128,8,512]{2,1,0:T(8,128)(2,1)S(1)} all-to-all(bf16[128,8,512]{2,1,0:T(8,128)(2,1)S(1)} %bitcast.22), channel_id=1, replica_groups=mesh['rep'=4,'ep'=128] {'ep'}, dimensions={0} | all-to-all | bytes 2097152 | tf_op jit(solution)/shard_map/all_to_all | solution.py:216
  60.7 0.0 copy-done.4
  60.7 0.0 copy-done.5
  60.7 3.3 %shard_map.103 = bf16[1024,1280]{1,0:T(8,128)(2,1)} custom-call(bf16[1024,512]{1,0:T(8,128)(2,1)S(1)} %bitcast.18, bf16[512,640]{1,0:T(8,128)(2,1)S(1)} %bitcast.23, bf16[512,640]{1,0:T(8,128)(2,1)S(1)} %bitcast.26), custom_call_target="tpu_custom_call" | custom-call | flops 1342177280 | bytes 4980736 | tf_op jit(solution)/shard_map/pallas_call | solution.py:24
  64.0 1.0 copy-done
  65.0 0.0 reduce-scatter.3.cloned.1.call-update
  65.1 0.0 reduce-scatter.5.cloned.1.call-start
  65.1 0.0 copy-start.6
  65.1 0.0 copy-start.15
  65.1 42.5 %all_to_all.16 = bf16[128,8,640]{2,1,0:T(8,128)(2,1)S(1)} all-to-all(bf16[128,8,640]{2,1,0:T(8,128)(2,1)S(1)} %bitcast.21), channel_id=1, replica_groups=mesh['rep'=4,'ep'=128] {'ep'}, dimensions={0} | all-to-all | bytes 2621440 | tf_op jit(solution)/shard_map/all_to_all | solution.py:216
  107.6 0.0 copy-done.6
  107.6 0.0 copy-done.15
  107.6 3.0 %shard_map.104 = (bf16[1408,640]{1,0:T(8,128)(2,1)}, bf16[128,512]{1,0:T(8,128)(2,1)S(1)}, bf16[128,512]{1,0:T(8,128)(2,1)S(1)}) custom-call(bf16[1024,640]{1,0:T(8,128)(2,1)S(1)} %bitcast.15, bf16[512,640]{1,0:T(8,128)(2,1)S(1)} %bitcast.24, bf16[512,640]{1,0:T(8,128)(2,1)S(1)} %bitcast.27, bf16[640,512]{1,0:T(8,128)(2,1)S(1)} %bitcast.31), custom_call_target="tpu_custom_call" | custom-call | flops 922746880 | bytes 5341184 | tf_op jit(solution)/shard_map/pallas_call | solution.py:24
  110.7 0.0 reduce-scatter.5.cloned.1.call-update
  110.7 0.0 all-gather.3.cloned.1.call-start
  110.7 0.0 reduce-scatter.3.cloned.1.call-done.tokens_side_ref
  110.8 26.8 %reduce-scatter.5.cloned.1.call-done.grads_side_ref = bf16[352,640]{1,0:T(8,128)(2,1)} async-done(((bf16[1408,640]{1,0:T(8,128)(2,1)}), bf16[352,640]{1,0:T(8,128)(2,1)}) %reduce-scatter.5.cloned.1.call-update) | async-done | bytes 450576 | tf_op jit(solution)/shard_map/reduce_scatter | solution.py:248
  137.6 1.1 copy-done.8
  138.6 1.0 copy-done.9
  139.7 1.3 shard_map.105
  141.0 0.0 all-gather.3.cloned.1.call-update
  141.0 43.1 %all-gather.3.cloned.1.call-done.delta_ref = bf16[1152,1280]{1,0:T(8,128)(2,1)} async-done(((bf16[288,1280]{1,0:T(8,128)(2,1)}), bf16[1152,1280]{1,0:T(8,128)(2,1)}) %all-gather.3.cloned.1.call-update) | async-done | bytes 2949136 | tf_op jit(solution)/shard_map/all_gather | solution.py:255
  184.2 0.0 copy-done.7
  184.2 1.8 copy-done.13
  186.0 2.2 shard_map.106
  188.2 0.0 copy-start.3
  188.2 1.1 copy-done.3
  189.3 0.0 copy-done.10
  189.3 14.3 %all-to-all-start.2 = ((bf16[128,8,640]{2,1,0:T(8,128)(2,1)}), bf16[128,8,640]{2,1,0:T(8,128)(2,1)S(1)}, u32[]{:S(2)}, u32[]{:S(2)}) async-start(bf16[128,8,640]{2,1,0:T(8,128)(2,1)} %bitcast.20), calls=%async_computation.4 | async-start | bytes 2621440 | tf_op jit(solution)/shard_map/all_to_all | solution.py:216
  203.6 0.0 all-gather.5.cloned.1.call-start
  203.7 0.5 all-gather.5.cloned.1.call-update
  204.2 0.0 copy-start.1
  204.2 1.2 copy-done.1
  205.4 1.8 copy-done.14
  207.3 3.8 %shard_map.108 = (bf16[512,640]{1,0:T(8,128)(2,1)}, bf16[512,640]{1,0:T(8,128)(2,1)}) custom-call(bf16[1024,512]{1,0:T(8,128)(2,1)S(1)} %bitcast.19, bf16[128,512]{1,0:T(8,128)(2,1)S(1)} %get-tuple-element.25.extra_ref, bf16[1152,1280]{1,0:T(8,128)(2,1)S(1)} %copy-done.14), custom_call_target="tpu_custom_call" | custom-call | flops 1509949440 | bytes 5439488 | tf_op jit(solution)/shard_map/pallas_call | solution.py:24
  211.1 26.6 %all-gather.5.cloned.1.call-done.hidden_ref = bf16[1152,640]{1,0:T(8,128)(2,1)} async-done(((bf16[288,640]{1,0:T(8,128)(2,1)}), bf16[1152,640]{1,0:T(8,128)(2,1)}) %all-gather.5.cloned.1.call-update) | async-done | bytes 1474576 | tf_op jit(solution)/shard_map/all_gather | solution.py:257
  237.7 1.4 copy-done.2
  239.0 2.4 shard_map.109
  241.4 0.0 all-to-all-done.2
  241.4 0.0 copy-done.12
  241.4 1.4 shard_map.107
  (13 shorter events, 0.0 us)
Async XLA Ops:
  7.2 103.6 %reduce-scatter.3.cloned.1.call-start = ((), (), s32[]{:S(2)}) async-start(), calls=%async_computation.5 | async-start | bytes 3276800 | tf_op jit(solution)/shard_map/reduce_scatter | solution.py:236
  7.9 0.7 copy-start.11
  8.6 0.9 copy-start.16
  9.5 0.9 copy-start.17
  10.4 50.3 %copy-start.4 = (bf16[1,512,640]{2,1,0:T(8,128)(2,1)S(1)}, bf16[1,512,640]{2,1,0:T(8,128)(2,1)}, u32[]{:S(2)}) copy-start(bf16[1,512,640]{2,1,0:T(8,128)(2,1)} %param.11) | copy-start | bytes 1966084
  10.4 50.3 %copy-start.5 = (bf16[1,512,640]{2,1,0:T(8,128)(2,1)S(1)}, bf16[1,512,640]{2,1,0:T(8,128)(2,1)}, u32[]{:S(2)}) copy-start(bf16[1,512,640]{2,1,0:T(8,128)(2,1)} %param.12) | copy-start | bytes 1966084
  64.0 1.0 copy-start
  65.1 72.5 %reduce-scatter.5.cloned.1.call-start = ((), (), s32[]{:S(2)}) async-start(), calls=%async_computation.6 | async-start | bytes 2252800 | tf_op jit(solution)/shard_map/reduce_scatter | solution.py:248
  65.1 42.5 %copy-start.6 = (bf16[1,512,640]{2,1,0:T(8,128)(2,1)S(1)}, bf16[1,512,640]{2,1,0:T(8,128)(2,1)}, u32[]{:S(2)}) copy-start(bf16[1,512,640]{2,1,0:T(8,128)(2,1)} %param.12) | copy-start | bytes 1966084
  65.1 42.5 %copy-start.15 = (bf16[1,640,512]{2,1,0:T(8,128)(2,1)S(1)}, bf16[1,640,512]{2,1,0:T(8,128)(2,1)}, u32[]{:S(2)}) copy-start(bf16[1,640,512]{2,1,0:T(8,128)(2,1)} %param.13) | copy-start | bytes 1966084
  110.7 73.5 %copy-start.7 = (bf16[1,512,640]{2,1,0:T(8,128)(2,1)S(1)}, bf16[1,512,640]{2,1,0:T(8,128)(2,1)}, u32[]{:S(2)}) copy-start(bf16[1,512,640]{2,1,0:T(8,128)(2,1)} %param.12) | copy-start | bytes 1966084
  110.7 73.5 %all-gather.3.cloned.1.call-start = ((), (), s32[]{:S(2)}) async-start(), calls=%async_computation.7 | async-start | bytes 3686400 | tf_op jit(solution)/shard_map/all_gather | solution.py:255
  137.6 1.1 copy-start.8
  138.6 1.0 copy-start.9
  141.0 48.3 %copy-start.10 = (bf16[288,640]{1,0:T(8,128)(2,1)}, bf16[288,640]{1,0:T(8,128)(2,1)S(1)}, u32[]{:S(2)}) copy-start(bf16[288,640]{1,0:T(8,128)(2,1)S(1)} %get-tuple-element.29) | copy-start | bytes 1105924
  184.2 1.8 copy-start.13
  188.2 1.1 copy-start.3
  189.3 52.1 %all-to-all-start.2 = ((bf16[128,8,640]{2,1,0:T(8,128)(2,1)}), bf16[128,8,640]{2,1,0:T(8,128)(2,1)S(1)}, u32[]{:S(2)}, u32[]{:S(2)}) async-start(bf16[128,8,640]{2,1,0:T(8,128)(2,1)} %bitcast.20), calls=%async_computation.4 | async-start | bytes 2621440 | tf_op jit(solution)/shard_map/all_to_all | solution.py:216
  203.6 34.1 %all-gather.5.cloned.1.call-start = ((), (), s32[]{:S(2)}) async-start(), calls=%async_computation.8 | async-start | bytes 1843200 | tf_op jit(solution)/shard_map/all_gather | solution.py:257
  204.2 1.2 copy-start.1
  205.4 1.8 copy-start.14
  237.7 1.4 copy-start.2
  239.0 2.4 copy-start.12
Sparse Core Ops, SparseCore 0:
  65.2 32.8 reduce-scatter.2
  110.8 26.7 reduce-scatter.4
  141.2 42.9 all-gather.2
  207.0 30.5 all-gather.4

commit v2 on v1

v2 whole, which is shorter than its diff:
```python
import jax
import jax.numpy as jnp
from jax import lax
from jax.experimental import pallas as pl
from jax.experimental.pallas import tpu as pltpu
from jax.sharding import PartitionSpec as P

MAIN = 8
LANES = 128
BF = jnp.bfloat16
F32 = jnp.float32
CONTRACT_LAST = (((1,), (1,)), ((), ()))
CONTRACT_FIRST = (((0,), (0,)), ((), ()))


def dot(a, b, dims=(((1,), (0,)), ((), ()))):
    return lax.dot_general(a, b, dims, preferred_element_type=F32)


def kernel_call(body, out_shape, args, flops, scratch=()):
    moved = sum(a.size * a.dtype.itemsize for a in args)
    outs = out_shape if isinstance(out_shape, tuple) else (out_shape,)
    moved += sum(o.size * o.dtype.itemsize for o in outs)
    return pl.pallas_call(
        body,
        out_shape=out_shape,
        in_specs=[pl.BlockSpec(memory_space=pltpu.VMEM)] * len(args),
        out_specs=jax.tree.map(lambda _: pl.BlockSpec(memory_space=pltpu.VMEM), out_shape),
        scratch_shapes=list(scratch),
        compiler_params=pltpu.CompilerParams(vmem_limit_bytes=48 << 20),
        cost_estimate=pl.CostEstimate(flops=flops, bytes_accessed=moved, transcendentals=0),
    )(*args)


def routing(ids_ref, experts):
    top, count = ids_ref.shape
    expert = lax.broadcasted_iota(jnp.int32, (experts, count), 0)
    matches = [expert == ids_ref[k : k + 1, :] for k in range(top)]
    picked = sum(m.astype(F32) for m in matches)
    earlier = lax.broadcasted_iota(jnp.int32, (count, count), 0) < lax.broadcasted_iota(
        jnp.int32, (count, count), 1
    )
    before = dot(picked.astype(BF), earlier.astype(F32).astype(BF))
    return jnp.where(picked > 0.0, before, -1.0), matches


def spread(per_expert):
    experts, count = per_expert.shape
    wide = jnp.broadcast_to(per_expert[:, None, :], (experts, MAIN, count))
    return wide.reshape(experts * MAIN, count)


def main_slots(slot):
    experts, count = slot.shape
    number = lax.broadcasted_iota(jnp.int32, (experts * MAIN, count), 0) % MAIN
    return spread(slot) == number.astype(F32)


def dispatch_kernel(ids_ref, weight_ref, tokens_ref, grads_ref, out_ref, packed):
    experts = out_ref.shape[0] // MAIN
    quarter = tokens_ref.shape[1]
    slot, matches = routing(ids_ref, experts)
    weight = sum(
        jnp.where(m, weight_ref[k : k + 1, :], 0.0) for k, m in enumerate(matches)
    )
    here = main_slots(slot)
    out_ref[:, :quarter] = dot(jnp.where(here, 1.0, 0.0).astype(BF), tokens_ref[...]).astype(BF)
    out_ref[:, quarter : 2 * quarter] = dot(
        jnp.where(here, spread(weight), 0.0).astype(BF), grads_ref[...]
    ).astype(BF)
    last = slot == float(MAIN)
    extra_tokens = dot(jnp.where(last, 1.0, 0.0).astype(BF), tokens_ref[...])
    extra_grads = dot(jnp.where(last, weight, 0.0).astype(BF), grads_ref[...])
    pieces = quarter // LANES
    for j in range(pieces):
        packed[:, j, :] = extra_tokens[:, j * LANES : (j + 1) * LANES]
        packed[:, pieces + j, :] = extra_grads[:, j * LANES : (j + 1) * LANES]
    out_ref[:, 2 * quarter :] = packed[...].reshape(experts * MAIN, LANES).astype(BF)


def expert_kernel(
    rows_ref, gate_ref, up_ref, down_ref, delta_ref, hidden_ref, back_ref, token_rows, grad_rows, packed
):
    groups, n, _ = rows_ref.shape
    quarter, ffw = gate_ref.shape[1:]
    m = n // MAIN
    pieces = quarter // LANES
    for q in range(groups):
        at = q * quarter
        token_rows[:n, at : at + quarter] = rows_ref[q, :, :quarter]
        grad_rows[:n, at : at + quarter] = rows_ref[q, :, quarter : 2 * quarter]
        packed[...] = rows_ref[q, :, 2 * quarter :].astype(F32).reshape(m, MAIN, LANES)
        for j in range(pieces):
            to = slice(at + j * LANES, at + (j + 1) * LANES)
            token_rows[n:, to] = packed[:, j, :].astype(BF)
            grad_rows[n:, to] = packed[:, pieces + j, :].astype(BF)
    full = (groups * quarter, ffw)
    gate = dot(token_rows[...], gate_ref[...].reshape(full))
    up = dot(token_rows[...], up_ref[...].reshape(full))
    back = sum(
        dot(grad_rows[:, q * quarter : (q + 1) * quarter], down_ref[q], CONTRACT_LAST)
        for q in range(groups)
    )
    sigmoid = 1.0 / (1.0 + jnp.exp(-gate))
    silu = gate * sigmoid
    hidden_ref[...] = (silu * up).astype(BF)
    gate_delta = (back * up * sigmoid * (1.0 + gate * (1.0 - sigmoid))).astype(BF)
    up_delta = (back * silu).astype(BF)
    delta_ref[:, :ffw] = gate_delta
    delta_ref[:, ffw:] = up_delta
    for j in range(pieces, MAIN):
        packed[:, j, :] = jnp.zeros((m, LANES), F32)
    for q in range(groups):
        out = dot(gate_delta, gate_ref[q], CONTRACT_LAST) + dot(up_delta, up_ref[q], CONTRACT_LAST)
        back_ref[q, :, :quarter] = out[:n, :].astype(BF)
        for j in range(pieces):
            packed[:, j, :] = out[n:, j * LANES : (j + 1) * LANES]
        back_ref[q, :, quarter:] = packed[...].reshape(n, LANES).astype(BF)


def row_blocks(rows_ref, packed, quarter, which):
    sources = rows_ref.shape[0] // MAIN
    pieces = quarter // LANES
    packed[...] = rows_ref[:, 2 * quarter :].astype(F32).reshape(sources, MAIN, LANES)
    n, m = rows_ref.shape[0] // 4, sources // 4
    columns = slice(which * quarter, (which + 1) * quarter)
    for r in range(4):
        extra = jnp.concatenate(
            [packed[r * m : (r + 1) * m, which * pieces + j, :] for j in range(pieces)], axis=1
        )
        yield r * (n + m), n, m, rows_ref[r * n : (r + 1) * n, columns], extra.astype(BF)


def token_weights_kernel(rows_ref, delta_ref, gate_ref, up_ref, packed):
    quarter, ffw = gate_ref.shape
    total = 0.0
    for at, n, m, rows, extra in row_blocks(rows_ref, packed, quarter, 0):
        total = total + dot(rows, delta_ref[at : at + n, :], CONTRACT_FIRST)
        total = total + dot(extra, delta_ref[at + n : at + n + m, :], CONTRACT_FIRST)
    gate_ref[...] = total[:, :ffw].astype(BF)
    up_ref[...] = total[:, ffw:].astype(BF)


def down_weights_kernel(rows_ref, hidden_ref, down_ref, packed):
    total = 0.0
    for at, n, m, rows, extra in row_blocks(rows_ref, packed, down_ref.shape[1], 1):
        total = total + dot(hidden_ref[at : at + n, :], rows, CONTRACT_FIRST)
        total = total + dot(hidden_ref[at + n : at + n + m, :], extra, CONTRACT_FIRST)
    down_ref[...] = total.astype(BF)


def combine_kernel(ids_ref, rows_ref, out_ref, packed):
    experts = rows_ref.shape[0] // MAIN
    quarter = out_ref.shape[1]
    slot, _ = routing(ids_ref, experts)
    here = jnp.where(main_slots(slot), 1.0, 0.0).astype(BF)
    last = jnp.where(slot == float(MAIN), 1.0, 0.0).astype(BF)
    packed[...] = rows_ref[:, quarter:].astype(F32).reshape(experts, MAIN, LANES)
    total = dot(here, rows_ref[:, :quarter], CONTRACT_FIRST)
    for j in range(quarter // LANES):
        at = slice(j * LANES, (j + 1) * LANES)
        extra = dot(last, packed[:, j, :].astype(BF), CONTRACT_FIRST)
        out_ref[:, at] = (total[:, at] + extra).astype(BF)


def exchange(blocks, axis):
    return lax.all_to_all(blocks, axis, split_axis=0, concat_axis=0, tiled=True)


def body(tokens, out_grad, expert_ids, route_weight, w_gate, w_up, w_down):
    experts = lax.axis_size("ep")
    groups = lax.axis_size("rep")
    count, quarter = tokens.shape
    ffw = w_gate.shape[2]
    main = experts * MAIN
    n, m = main // groups, experts // groups
    shape = jax.ShapeDtypeStruct
    packed = pltpu.VMEM((experts, MAIN, LANES), F32)

    gate_all, up_all, down_all = (
        lax.all_gather(w, "rep", axis=0, tiled=True) for w in (w_gate, w_up, w_down)
    )
    ids = expert_ids.T
    sent = kernel_call(
        dispatch_kernel,
        shape((main, 2 * quarter + LANES), BF),
        (ids, route_weight.T.astype(F32), tokens, out_grad),
        4 * main * count * quarter,
        (packed,),
    )
    rows = exchange(sent.reshape(experts, MAIN, -1), "ep").reshape(main, -1)
    wide_rows = exchange(rows.reshape(groups, n, -1), "rep")
    delta, hidden, back = kernel_call(
        expert_kernel,
        (
            shape((n + m, 2 * ffw), BF),
            shape((n + m, ffw), BF),
            shape((groups, n, quarter + LANES), BF),
        ),
        (wide_rows, gate_all, up_all, down_all),
        10 * (n + m) * groups * quarter * ffw,
        (
            pltpu.VMEM((n + m, groups * quarter), BF),
            pltpu.VMEM((n + m, groups * quarter), BF),
            pltpu.VMEM((m, MAIN, LANES), F32),
        ),
    )
    delta = lax.all_gather(delta, "rep", axis=0, tiled=True)
    hidden = lax.all_gather(hidden, "rep", axis=0, tiled=True)
    back = exchange(back, "rep")
    returned = exchange(back.reshape(experts, MAIN, -1), "ep").reshape(main, -1)
    grad_gate, grad_up = kernel_call(
        token_weights_kernel,
        (shape((quarter, ffw), BF), shape((quarter, ffw), BF)),
        (rows, delta),
        4 * (main + experts) * quarter * ffw,
        (packed,),
    )
    grad_down = kernel_call(
        down_weights_kernel,
        shape((ffw, quarter), BF),
        (rows, hidden),
        2 * (main + experts) * quarter * ffw,
        (packed,),
    )
    token_grad = kernel_call(
        combine_kernel,
        shape((count, quarter), BF),
        (ids, returned),
        2 * main * count * quarter,
        (packed,),
    )
    return token_grad, grad_gate[None], grad_up[None], grad_down[None]


def solution(mesh):
    rows = P("ep", "rep")
    by_width = P("ep", "rep", None)
    last = P("ep", None, "rep")
    return jax.shard_map(
        body,
        mesh=mesh,
        in_specs=(rows, rows, P("ep", None), P("ep", None), by_width, by_width, last),
        out_specs=(rows, by_width, by_width, last),
        check_vma=False,
    )
```

time: 250 us -> 252 us (level)
  blocking collectives: 91.6 us -> 23.8 us
  waiting for transfers between devices: 97.1 us -> 143 us
  starting transfers between devices: 14.5 us -> 40.9 us
  local copies, waits for them, and re-layouts: 13 us -> 6.78 us
  Pallas kernels: 18.7 us -> 22.2 us
    all_to_all x1 -> x3, waiting for transfers between devices: 0.01 us -> 86.3 us  [exchange(): return lax.all_to_all(blocks, axis, split_axis=0, concat_axis=0, tiled=True)]
    all_to_all x2 -> x1, blocking collectives: 91.6 us -> 23.8 us  [exchange(): return lax.all_to_all(blocks, axis, split_axis=0, concat_axis=0, tiled=True)]
    all_gather x0 -> x3, waiting for transfers between devices: none -> 54 us  [body(): lax.all_gather(w, 'rep', axis=0, tiled=True)]
    all_gather x1, waiting for transfers between devices: 43.1 us -> 0.5 us  [body(): delta = lax.all_gather(delta, 'rep', axis=0, tiled=True)]
    reduce_scatter x2 -> x0, waiting for transfers between devices: 26.8 us -> none  [body(): lax.psum_scatter(products, 'rep', scatter_dimension=0, tiled=True)]
    all_gather x1, waiting for transfers between devices: 26.6 us -> 0.02 us  [body(): hidden = lax.all_gather(hidden, 'rep', axis=0, tiled=True)]
    all_to_all x1 -> x3, starting transfers between devices: 14.3 us -> 40.7 us  [exchange(): return lax.all_to_all(blocks, axis, split_axis=0, concat_axis=0, tiled=True)]
    unnamed x36 -> x14, local copies, waits for them, and re-layouts: 13 us -> 6.78 us
  transfers between devices with their start and end apart: 5 -> 8, of which waited for: 3 -> 5; matrix products, arithmetic and copies ran while one was open for 0% -> 0% of each run, Pallas kernels for 4% -> 3%
where the time goes in v2:
time: 252 us; the launch traced here: 251 us
  waiting for transfers between devices  143 us (57%)
  starting transfers between devices  40.9 us (16%)
  blocking collectives  23.8 us (9%)
  Pallas kernels  22.2 us (9%)
  between operations  13.8 us (5%)
  local copies, waits for them, and re-layouts  6.78 us (3%)
    all_to_all x3, waiting for transfers between devices, exchange(): return lax.all_to_all(blocks, axis, split_axis=0, concat_axis=0, tiled=True)  86.3 us
    all_gather x3, waiting for transfers between devices, body(): lax.all_gather(w, 'rep', axis=0, tiled=True)  54 us
    all_to_all x3, starting transfers between devices, exchange(): return lax.all_to_all(blocks, axis, split_axis=0, concat_axis=0, tiled=True)  40.7 us
    all_to_all x1, blocking collectives, exchange(): return lax.all_to_all(blocks, axis, split_axis=0, concat_axis=0, tiled=True)  23.8 us
    pallas_call x5, Pallas kernels, kernel_call(): pl.pallas_call(body, out_shape=out_shape, in_specs=[pl.BlockSpec(memory_s...  22.2 us
    unnamed x14, local copies, waits for them, and re-layouts  6.78 us
  transfers between devices with their start and end apart: 8, of which 5 were waited for; matrix products, arithmetic and copies ran while one was open for 0% of the time, Pallas kernels for 3%

profile of v2, /device:TPU:1, one launch (start us, length us, event | category | flops | bytes accessed | tf_op | source)
XLA Modules:
  0.0 251.5 jit_solution(4548942190202425504)
XLA Ops:
  7.2 0.0 all-gather.6.cloned.1.call-start
  7.2 0.7 all-gather.6.cloned.1.call-update
  7.9 0.0 all-gather.8.cloned.1.call-start
  7.9 0.7 all-gather.8.cloned.1.call-update
  8.6 0.7 convert_bitcast_fusion.weight_ref
  9.3 0.0 copy-start.2
  9.3 0.9 copy-done.2
  10.2 0.0 copy-start.3
  10.2 0.9 copy-done.3
  11.1 0.0 copy-start.4
  11.1 0.7 copy-done.4
  11.8 2.6 %shard_map.102 = bf16[1024,1152]{1,0:T(8,128)(2,1)} custom-call(s32[8,128]{1,0:T(8,128)S(1)} %bitcast.12, f32[8,128]{1,0:T(8,128)S(1)} %convert_bitcast_fusion.weight_ref, bf16[128,512]{1,0:T(8,128)(2,1)S(1)} %copy-done.2, bf16[128,512]{1,0:T(8,128)(2,1)S(1)} %copy-done.3), custom_call_target="tpu_custom_call" | custom-call | flops 268435456 | bytes 2629632 | tf_op jit(solution)/shard_map/pallas_call | solution.py:24
  14.5 18.8 %all-to-all-start = ((bf16[128,8,1152]{2,1,0:T(8,128)(2,1)}), bf16[128,8,1152]{2,1,0:T(8,128)(2,1)}, u32[]{:S(2)}, u32[]{:S(2)}) async-start(bf16[128,8,1152]{2,1,0:T(8,128)(2,1)} %bitcast.2), calls=%async_computation | async-start | bytes 4718592 | tf_op jit(solution)/shard_map/all_to_all | solution.py:167
  33.3 0.0 all-gather.10.cloned.1.call-start
  33.3 0.7 all-gather.10.cloned.1.call-update
  34.0 55.7 %all-to-all-done = bf16[128,8,1152]{2,1,0:T(8,128)(2,1)} async-done(((bf16[128,8,1152]{2,1,0:T(8,128)(2,1)}), bf16[128,8,1152]{2,1,0:T(8,128)(2,1)}, u32[]{:S(2)}, u32[]{:S(2)}) %all-to-all-start) | async-done | bytes 2359328 | tf_op jit(solution)/shard_map/all_to_all | solution.py:167
  89.7 4.0 %all-to-all-start.1 = ((bf16[4,256,1152]{2,1,0:T(8,128)(2,1)}), bf16[4,256,1152]{2,1,0:T(8,128)(2,1)S(1)}, u32[]{:S(2)}, u32[]{:S(2)}) async-start(bf16[4,256,1152]{2,1,0:T(8,128)(2,1)} %bitcast.3), calls=%async_computation.1 | async-start | bytes 4718592 | tf_op jit(solution)/shard_map/all_to_all | solution.py:167
  93.8 0.0 all-gather.14.cloned.1.call-start
  93.8 0.0 all-gather.6.cloned.1.call-done.gate_ref
  93.8 5.6 %all-gather.8.cloned.1.call-done.up_ref = bf16[4,512,640]{2,1,0:T(8,128)(2,1)} async-done(((bf16[1,512,640]{2,1,0:T(8,128)(2,1)}), bf16[4,512,640]{2,1,0:T(8,128)(2,1)}) %all-gather.8.cloned.1.call-update) | async-done | bytes 2621456 | tf_op jit(solution)/shard_map/all_gather | solution.py:181
  99.3 48.4 %all-gather.10.cloned.1.call-done.down_ref = bf16[4,640,512]{2,1,0:T(8,128)(2,1)} async-done(((bf16[1,640,512]{2,1,0:T(8,128)(2,1)}), bf16[4,640,512]{2,1,0:T(8,128)(2,1)}) %all-gather.10.cloned.1.call-update) | async-done | bytes 2621456 | tf_op jit(solution)/shard_map/all_gather | solution.py:181
  147.7 0.0 all-to-all-done.1.rows_ref
  147.7 8.5 %shard_map.103 = (bf16[288,1280]{1,0:T(8,128)(2,1)}, bf16[288,640]{1,0:T(8,128)(2,1)}, bf16[4,256,640]{2,1,0:T(8,128)(2,1)S(1)}) custom-call(bf16[4,256,1152]{2,1,0:T(8,128)(2,1)S(1)} %all-to-all-done.1.rows_ref, bf16[4,512,640]{2,1,0:T(8,128)(2,1)} %all-gather.6.cloned.1.call-done.gate_ref, bf16[4,512,640]{2,1,0:T(8,128)(2,1)} %all-gather.8.cloned.1.call-done.up_ref, ...), custom_call_target="tpu_custom_call" | custom-call | flops 3774873600 | bytes 12640256 | tf_op jit(solution)/shard_map/pallas_call | solution.py:24
  156.3 0.0 copy-start.1
  156.3 1.1 copy-done.1
  157.4 0.0 all-gather.14.cloned.1.call-update
  157.4 0.0 all-gather.12.cloned.1.call-start
  157.4 0.5 all-gather.12.cloned.1.call-update
  158.0 23.8 %all_to_all.20 = bf16[4,256,640]{2,1,0:T(8,128)(2,1)} all-to-all(bf16[4,256,640]{2,1,0:T(8,128)(2,1)} %copy-done.1), channel_id=1, replica_groups=mesh['rep'=4,'ep'=128] {'rep'}, dimensions={0} | all-to-all | bytes 2621440 | tf_op jit(solution)/shard_map/all_to_all | solution.py:167
  181.7 0.0 copy-start.5
  181.7 17.9 %all-to-all-start.3 = ((bf16[128,8,640]{2,1,0:T(8,128)(2,1)}), bf16[128,8,640]{2,1,0:T(8,128)(2,1)S(1)}, u32[]{:S(2)}, u32[]{:S(2)}) async-start(bf16[128,8,640]{2,1,0:T(8,128)(2,1)} %bitcast.4), calls=%async_computation.3 | async-start | bytes 2621440 | tf_op jit(solution)/shard_map/all_to_all | solution.py:167
  199.6 0.0 all-gather.14.cloned.1.call-done.hidden_ref
  199.7 0.0 copy-start
  199.7 1.4 copy-done
  201.0 4.1 %shard_map.106 = bf16[640,512]{1,0:T(8,128)(2,1)} custom-call(bf16[1024,1152]{1,0:T(8,128)(2,1)} %bitcast.6.rows_ref, bf16[1152,640]{1,0:T(8,128)(2,1)S(1)} %copy-done), custom_call_target="tpu_custom_call" | custom-call | flops 754974720 | bytes 4489216 | tf_op jit(solution)/shard_map/pallas_call | solution.py:24
  205.1 30.6 %all-to-all-done.3 = bf16[128,8,640]{2,1,0:T(8,128)(2,1)S(1)} async-done(((bf16[128,8,640]{2,1,0:T(8,128)(2,1)}), bf16[128,8,640]{2,1,0:T(8,128)(2,1)S(1)}, u32[]{:S(2)}, u32[]{:S(2)}) %all-to-all-start.3) | async-done | bytes 1310752 | tf_op jit(solution)/shard_map/all_to_all | solution.py:167
  235.7 0.0 copy-done.5
  235.7 1.4 shard_map.104
  237.1 0.5 all-gather.12.cloned.1.call-done.delta_ref
  237.6 0.0 copy-start.6
  237.6 1.8 copy-done.6
  239.4 5.5 %shard_map.105 = (bf16[512,640]{1,0:T(8,128)(2,1)}, bf16[512,640]{1,0:T(8,128)(2,1)}) custom-call(bf16[1024,1152]{1,0:T(8,128)(2,1)} %bitcast.6.rows_ref, bf16[1152,1280]{1,0:T(8,128)(2,1)S(1)} %copy-done.6), custom_call_target="tpu_custom_call" | custom-call | flops 1509949440 | bytes 6619136 | tf_op jit(solution)/shard_map/pallas_call | solution.py:24
Async XLA Ops:
  7.2 86.6 %all-gather.6.cloned.1.call-start = ((), (), s32[]{:S(2)}) async-start(), calls=%async_computation.4 | async-start | bytes 3276800 | tf_op jit(solution)/shard_map/all_gather | solution.py:181
  7.9 91.4 %all-gather.8.cloned.1.call-start = ((), (), s32[]{:S(2)}) async-start(), calls=%async_computation.5 | async-start | bytes 3276800 | tf_op jit(solution)/shard_map/all_gather | solution.py:181
  9.3 0.9 copy-start.2
  10.2 0.9 copy-start.3
  11.1 0.7 copy-start.4
  14.5 75.3 %all-to-all-start = ((bf16[128,8,1152]{2,1,0:T(8,128)(2,1)}), bf16[128,8,1152]{2,1,0:T(8,128)(2,1)}, u32[]{:S(2)}, u32[]{:S(2)}) async-start(bf16[128,8,1152]{2,1,0:T(8,128)(2,1)} %bitcast.2), calls=%async_computation | async-start | bytes 4718592 | tf_op jit(solution)/shard_map/all_to_all | solution.py:167
  33.3 114.5 %all-gather.10.cloned.1.call-start = ((), (), s32[]{:S(2)}) async-start(), calls=%async_computation.6 | async-start | bytes 3276800 | tf_op jit(solution)/shard_map/all_gather | solution.py:181
  89.7 58.0 %all-to-all-start.1 = ((bf16[4,256,1152]{2,1,0:T(8,128)(2,1)}), bf16[4,256,1152]{2,1,0:T(8,128)(2,1)S(1)}, u32[]{:S(2)}, u32[]{:S(2)}) async-start(bf16[4,256,1152]{2,1,0:T(8,128)(2,1)} %bitcast.3), calls=%async_computation.1 | async-start | bytes 4718592 | tf_op jit(solution)/shard_map/all_to_all | solution.py:167
  93.8 105.9 %all-gather.14.cloned.1.call-start = ((), (), s32[]{:S(2)}) async-start(), calls=%async_computation.8 | async-start | bytes 1843200 | tf_op jit(solution)/shard_map/all_gather | solution.py:209
  156.3 1.1 copy-start.1
  157.4 80.2 %all-gather.12.cloned.1.call-start = ((), (), s32[]{:S(2)}) async-start(), calls=%async_computation.7 | async-start | bytes 3686400 | tf_op jit(solution)/shard_map/all_gather | solution.py:208
  181.7 54.0 %copy-start.5 = (s32[128,8]{0,1:T(8,128)S(1)}, s32[128,8]{0,1:T(8,128)}, u32[]{:S(2)}) copy-start(s32[128,8]{0,1:T(8,128)} %param.9) | copy-start | bytes 12292
  181.7 53.9 %all-to-all-start.3 = ((bf16[128,8,640]{2,1,0:T(8,128)(2,1)}), bf16[128,8,640]{2,1,0:T(8,128)(2,1)S(1)}, u32[]{:S(2)}, u32[]{:S(2)}) async-start(bf16[128,8,640]{2,1,0:T(8,128)(2,1)} %bitcast.4), calls=%async_computation.3 | async-start | bytes 2621440 | tf_op jit(solution)/shard_map/all_to_all | solution.py:167
  199.7 1.4 copy-start
  237.6 1.8 copy-start.6
Sparse Core Ops, SparseCore 0:
  10.1 45.9 all-gather.5
  58.2 41.0 all-gather.7
  101.4 46.2 all-gather.9
  157.5 35.0 all-gather.13
  194.6 42.9 all-gather.11

commit v3 on v2

--- a/solution.py
+++ b/solution.py
@@ -17,14 +17,17 @@
     return lax.dot_general(a, b, dims, preferred_element_type=F32)
 
 
-def kernel_call(body, out_shape, args, flops, scratch=()):
+def kernel_call(body, out_shape, args, flops, scratch=(), in_hbm=()):
     moved = sum(a.size * a.dtype.itemsize for a in args)
     outs = out_shape if isinstance(out_shape, tuple) else (out_shape,)
     moved += sum(o.size * o.dtype.itemsize for o in outs)
     return pl.pallas_call(
         body,
         out_shape=out_shape,
-        in_specs=[pl.BlockSpec(memory_space=pltpu.VMEM)] * len(args),
+        in_specs=[
+            pl.BlockSpec(memory_space=pltpu.HBM if i in in_hbm else pltpu.VMEM)
+            for i in range(len(args))
+        ],
         out_specs=jax.tree.map(lambda _: pl.BlockSpec(memory_space=pltpu.VMEM), out_shape),
         scratch_shapes=list(scratch),
         compiler_params=pltpu.CompilerParams(vmem_limit_bytes=48 << 20),
@@ -56,18 +59,35 @@
     return spread(slot) == number.astype(F32)
 
 
-def dispatch_kernel(ids_ref, weight_ref, tokens_ref, grads_ref, out_ref, packed):
+def pack_weights_kernel(gate_ref, up_ref, down_ref, out_ref):
+    ffw = gate_ref.shape[1]
+    out_ref[:, :ffw] = gate_ref[...]
+    out_ref[:, ffw : 2 * ffw] = up_ref[...]
+    out_ref[:, 2 * ffw :] = down_ref[...].T
+
+
+def dispatch_kernel(
+    ids_ref, weight_ref, tokens_hbm, grads_hbm, out_ref, packed, tokens_ref, grads_ref, sems
+):
+    loads = (
+        pltpu.make_async_copy(tokens_hbm, tokens_ref, sems.at[0]),
+        pltpu.make_async_copy(grads_hbm, grads_ref, sems.at[1]),
+    )
+    for load in loads:
+        load.start()
     experts = out_ref.shape[0] // MAIN
     quarter = tokens_ref.shape[1]
     slot, matches = routing(ids_ref, experts)
     weight = sum(
-        jnp.where(m, weight_ref[k : k + 1, :], 0.0) for k, m in enumerate(matches)
+        jnp.where(m, weight_ref[k : k + 1, :].astype(F32), 0.0) for k, m in enumerate(matches)
     )
     here = main_slots(slot)
-    out_ref[:, :quarter] = dot(jnp.where(here, 1.0, 0.0).astype(BF), tokens_ref[...]).astype(BF)
-    out_ref[:, quarter : 2 * quarter] = dot(
-        jnp.where(here, spread(weight), 0.0).astype(BF), grads_ref[...]
-    ).astype(BF)
+    placing = jnp.where(here, 1.0, 0.0).astype(BF)
+    weighing = jnp.where(here, spread(weight), 0.0).astype(BF)
+    loads[0].wait()
+    out_ref[:, :quarter] = dot(placing, tokens_ref[...]).astype(BF)
+    loads[1].wait()
+    out_ref[:, quarter : 2 * quarter] = dot(weighing, grads_ref[...]).astype(BF)
     last = slot == float(MAIN)
     extra_tokens = dot(jnp.where(last, 1.0, 0.0).astype(BF), tokens_ref[...])
     extra_grads = dot(jnp.where(last, weight, 0.0).astype(BF), grads_ref[...])
@@ -78,11 +98,10 @@
     out_ref[:, 2 * quarter :] = packed[...].reshape(experts * MAIN, LANES).astype(BF)
 
 
-def expert_kernel(
-    rows_ref, gate_ref, up_ref, down_ref, delta_ref, hidden_ref, back_ref, token_rows, grad_rows, packed
-):
+def expert_kernel(rows_ref, weights_ref, terms_ref, back_ref, token_rows, grad_rows, packed):
     groups, n, _ = rows_ref.shape
-    quarter, ffw = gate_ref.shape[1:]
+    quarter = weights_ref.shape[1]
+    ffw = weights_ref.shape[2] // 3
     m = n // MAIN
     pieces = quarter // LANES
     for q in range(groups):
@@ -94,24 +113,24 @@
             to = slice(at + j * LANES, at + (j + 1) * LANES)
             token_rows[n:, to] = packed[:, j, :].astype(BF)
             grad_rows[n:, to] = packed[:, pieces + j, :].astype(BF)
-    full = (groups * quarter, ffw)
-    gate = dot(token_rows[...], gate_ref[...].reshape(full))
-    up = dot(token_rows[...], up_ref[...].reshape(full))
-    back = sum(
-        dot(grad_rows[:, q * quarter : (q + 1) * quarter], down_ref[q], CONTRACT_LAST)
-        for q in range(groups)
-    )
+
+    def product(rows, part):
+        weights = weights_ref[:, :, part * ffw : (part + 1) * ffw]
+        return dot(rows[...], weights.reshape(groups * quarter, ffw))
+
+    gate, up, back = product(token_rows, 0), product(token_rows, 1), product(grad_rows, 2)
     sigmoid = 1.0 / (1.0 + jnp.exp(-gate))
     silu = gate * sigmoid
-    hidden_ref[...] = (silu * up).astype(BF)
     gate_delta = (back * up * sigmoid * (1.0 + gate * (1.0 - sigmoid))).astype(BF)
     up_delta = (back * silu).astype(BF)
-    delta_ref[:, :ffw] = gate_delta
-    delta_ref[:, ffw:] = up_delta
+    terms_ref[:, :ffw] = gate_delta
+    terms_ref[:, ffw : 2 * ffw] = up_delta
+    terms_ref[:, 2 * ffw :] = (silu * up).astype(BF)
     for j in range(pieces, MAIN):
         packed[:, j, :] = jnp.zeros((m, LANES), F32)
     for q in range(groups):
-        out = dot(gate_delta, gate_ref[q], CONTRACT_LAST) + dot(up_delta, up_ref[q], CONTRACT_LAST)
+        out = dot(gate_delta, weights_ref[q, :, :ffw], CONTRACT_LAST)
+        out = out + dot(up_delta, weights_ref[q, :, ffw : 2 * ffw], CONTRACT_LAST)
         back_ref[q, :, :quarter] = out[:n, :].astype(BF)
         for j in range(pieces):
             packed[:, j, :] = out[n:, j * LANES : (j + 1) * LANES]
@@ -131,21 +150,22 @@
         yield r * (n + m), n, m, rows_ref[r * n : (r + 1) * n, columns], extra.astype(BF)
 
 
-def token_weights_kernel(rows_ref, delta_ref, gate_ref, up_ref, packed):
+def token_weights_kernel(rows_ref, terms_ref, gate_ref, up_ref, packed):
     quarter, ffw = gate_ref.shape
     total = 0.0
     for at, n, m, rows, extra in row_blocks(rows_ref, packed, quarter, 0):
-        total = total + dot(rows, delta_ref[at : at + n, :], CONTRACT_FIRST)
-        total = total + dot(extra, delta_ref[at + n : at + n + m, :], CONTRACT_FIRST)
+        total = total + dot(rows, terms_ref[at : at + n, : 2 * ffw], CONTRACT_FIRST)
+        total = total + dot(extra, terms_ref[at + n : at + n + m, : 2 * ffw], CONTRACT_FIRST)
     gate_ref[...] = total[:, :ffw].astype(BF)
     up_ref[...] = total[:, ffw:].astype(BF)
 
 
-def down_weights_kernel(rows_ref, hidden_ref, down_ref, packed):
+def down_weights_kernel(rows_ref, terms_ref, down_ref, packed):
+    ffw, quarter = down_ref.shape
     total = 0.0
-    for at, n, m, rows, extra in row_blocks(rows_ref, packed, down_ref.shape[1], 1):
-        total = total + dot(hidden_ref[at : at + n, :], rows, CONTRACT_FIRST)
-        total = total + dot(hidden_ref[at + n : at + n + m, :], extra, CONTRACT_FIRST)
+    for at, n, m, rows, extra in row_blocks(rows_ref, packed, quarter, 1):
+        total = total + dot(terms_ref[at : at + n, 2 * ffw :], rows, CONTRACT_FIRST)
+        total = total + dot(terms_ref[at + n : at + n + m, 2 * ffw :], extra, CONTRACT_FIRST)
     down_ref[...] = total.astype(BF)
 
 
@@ -177,27 +197,33 @@
     shape = jax.ShapeDtypeStruct
     packed = pltpu.VMEM((experts, MAIN, LANES), F32)
 
-    gate_all, up_all, down_all = (
-        lax.all_gather(w, "rep", axis=0, tiled=True) for w in (w_gate, w_up, w_down)
-    )
+    weights = kernel_call(
+        pack_weights_kernel,
+        shape((quarter, 3 * ffw), BF),
+        (w_gate[0], w_up[0], w_down[0]),
+        0,
+    )
+    weights = lax.all_gather(weights, "rep", axis=0)
     ids = expert_ids.T
     sent = kernel_call(
         dispatch_kernel,
         shape((main, 2 * quarter + LANES), BF),
-        (ids, route_weight.T.astype(F32), tokens, out_grad),
+        (ids, route_weight.T, tokens, out_grad),
         4 * main * count * quarter,
-        (packed,),
+        (
+            packed,
+            pltpu.VMEM((count, quarter), BF),
+            pltpu.VMEM((count, quarter), BF),
+            pltpu.SemaphoreType.DMA((2,)),
+        ),
+        in_hbm=(2, 3),
     )
     rows = exchange(sent.reshape(experts, MAIN, -1), "ep").reshape(main, -1)
     wide_rows = exchange(rows.reshape(groups, n, -1), "rep")
-    delta, hidden, back = kernel_call(
+    terms, back = kernel_call(
         expert_kernel,
-        (
-            shape((n + m, 2 * ffw), BF),
-            shape((n + m, ffw), BF),
-            shape((groups, n, quarter + LANES), BF),
-        ),
-        (wide_rows, gate_all, up_all, down_all),
+        (shape((n + m, 3 * ffw), BF), shape((groups, n, quarter + LANES), BF)),
+        (wide_rows, weights),
         10 * (n + m) * groups * quarter * ffw,
         (
             pltpu.VMEM((n + m, groups * quarter), BF),
@@ -205,21 +231,20 @@
             pltpu.VMEM((m, MAIN, LANES), F32),
         ),
     )
-    delta = lax.all_gather(delta, "rep", axis=0, tiled=True)
-    hidden = lax.all_gather(hidden, "rep", axis=0, tiled=True)
+    terms = lax.all_gather(terms, "rep", axis=0, tiled=True)
     back = exchange(back, "rep")
     returned = exchange(back.reshape(experts, MAIN, -1), "ep").reshape(main, -1)
     grad_gate, grad_up = kernel_call(
         token_weights_kernel,
         (shape((quarter, ffw), BF), shape((quarter, ffw), BF)),
-        (rows, delta),
+        (rows, terms),
         4 * (main + experts) * quarter * ffw,
         (packed,),
     )
     grad_down = kernel_call(
         down_weights_kernel,
         shape((ffw, quarter), BF),
-        (rows, hidden),
+        (rows, terms),
         2 * (main + experts) * quarter * ffw,
         (packed,),
     )

time: 252 us -> 231 us (0.917)
  blocking collectives: 23.8 us -> 186 us
  waiting for transfers between devices: 143 us -> 0.04 us
  starting transfers between devices: 40.9 us -> 0.08 us
    all_to_all x1 -> x4, blocking collectives: 23.8 us -> 186 us  [exchange(): return lax.all_to_all(blocks, axis, split_axis=0, concat_axis=0, tiled=True)]
    all_to_all x3 -> x0, waiting for transfers between devices: 86.3 us -> none  [exchange(): return lax.all_to_all(blocks, axis, split_axis=0, concat_axis=0, tiled=True)]
    all_gather x5 -> x2, waiting for transfers between devices: 54.5 us -> 0.01 us  [the longest x1 0.01 us: body(): weights = lax.all_gather(weights, 'rep', axis=0)]
    all_to_all x3 -> x0, starting transfers between devices: 40.7 us -> none  [exchange(): return lax.all_to_all(blocks, axis, split_axis=0, concat_axis=0, tiled=True)]
    unnamed x5 -> x2, waiting for transfers between devices: 2.61 us -> 0.03 us
    pallas_call x5 -> x6, Pallas kernels: 22.2 us -> 24 us  [kernel_call(): pl.pallas_call(body, out_shape=out_shape, in_specs=[pl.BlockSpec(memory_s...]
    unnamed x14 -> x18, local copies, waits for them, and re-layouts: 6.78 us -> 6.04 us
  transfers between devices with their start and end apart: 8 -> 2, of which waited for: 5 -> 0; matrix products, arithmetic and copies ran while one was open for 0% -> 0% of each run, Pallas kernels for 3% -> 1%
where the time goes in v3:
time: 231 us; the launch traced here: 230 us
  blocking collectives  186 us (81%)
  Pallas kernels  24 us (10%)
  between operations  14.1 us (6%)
  local copies, waits for them, and re-layouts  6.04 us (3%)
    all_to_all x4, blocking collectives, exchange(): return lax.all_to_all(blocks, axis, split_axis=0, concat_axis=0, tiled=True)  186 us
    pallas_call x6, Pallas kernels, kernel_call(): pl.pallas_call(body, out_shape=out_shape, in_specs=[pl.BlockSpec(memory_s...  24 us
    unnamed x18, local copies, waits for them, and re-layouts  6.04 us
  transfers between devices with their start and end apart: 2, of which 0 were waited for; matrix products, arithmetic and copies ran while one was open for 0% of the time, Pallas kernels for 1%

profile of v3, /device:TPU:1, one launch (start us, length us, event | category | flops | bytes accessed | tf_op | source)
XLA Modules:
  0.0 229.9 jit_solution(12157112375309226936)
XLA Ops:
  7.2 0.0 all-gather.6.cloned.1.call-start
  7.2 0.0 copy-start.2
  7.2 1.1 copy-done.2
  8.3 0.0 copy-start.3
  8.3 1.1 copy-done.3
  9.4 0.0 copy-start.4
  9.4 1.1 copy-done.4
  10.5 0.0 copy-start.5
  10.5 0.0 copy-start.6
  10.5 0.0 copy-start.7
  10.5 0.0 copy-start.8
  10.5 1.5 shard_map.103
  12.0 0.0 all-gather.6.cloned.1.call-update
  12.0 0.0 all-gather.4.cloned.1.call-start
  12.1 0.0 copy-done.5
  12.1 0.0 copy-done.6
  12.1 0.0 copy-done.7
  12.1 0.0 copy-done.8
  12.1 1.9 shard_map.102
  14.0 74.9 %all_to_all.20 = bf16[128,8,1152]{2,1,0:T(8,128)(2,1)S(1)} all-to-all(bf16[128,8,1152]{2,1,0:T(8,128)(2,1)S(1)} %bitcast.17), channel_id=1, replica_groups=mesh['rep'=4,'ep'=128] {'ep'}, dimensions={0} | all-to-all | bytes 4718592 | tf_op jit(solution)/shard_map/all_to_all | solution.py:187
  89.0 37.5 %all_to_all.21.rows_ref = bf16[4,256,1152]{2,1,0:T(8,128)(2,1)} all-to-all(bf16[4,256,1152]{2,1,0:T(8,128)(2,1)S(1)} %bitcast.14), channel_id=1, replica_groups=mesh['rep'=4,'ep'=128] {'rep'}, dimensions={0} | all-to-all | bytes 4718592 | tf_op jit(solution)/shard_map/all_to_all | solution.py:187
  126.4 0.0 all-gather.6.cloned.1.call-done
  126.4 0.0 copy-start
  126.4 1.7 copy-done
  128.1 8.5 %shard_map.104 = (bf16[288,1920]{1,0:T(8,128)(2,1)}, bf16[4,256,640]{2,1,0:T(8,128)(2,1)S(1)}) custom-call(bf16[4,256,1152]{2,1,0:T(8,128)(2,1)S(1)} %copy-done, bf16[4,512,1920]{2,1,0:T(8,128)(2,1)} %bitcast.27), custom_call_target="tpu_custom_call" | custom-call | flops 3774873600 | bytes 12640256 | tf_op jit(solution)/shard_map/pallas_call | solution.py:24
  136.5 0.0 copy-start.1
  136.6 1.1 copy-done.1
  137.7 0.0 all-gather.4.cloned.1.call-update
  137.7 19.7 %all_to_all.22 = bf16[4,256,640]{2,1,0:T(8,128)(2,1)S(1)} all-to-all(bf16[4,256,640]{2,1,0:T(8,128)(2,1)} %copy-done.1), channel_id=1, replica_groups=mesh['rep'=4,'ep'=128] {'rep'}, dimensions={0} | all-to-all | bytes 2621440 | tf_op jit(solution)/shard_map/all_to_all | solution.py:187
  157.4 53.5 %all_to_all.23 = bf16[128,8,640]{2,1,0:T(8,128)(2,1)S(1)} all-to-all(bf16[128,8,640]{2,1,0:T(8,128)(2,1)S(1)} %bitcast.25), channel_id=1, replica_groups=mesh['rep'=4,'ep'=128] {'ep'}, dimensions={0} | all-to-all | bytes 2621440 | tf_op jit(solution)/shard_map/all_to_all | solution.py:187
  210.9 1.4 shard_map.105
  212.3 0.0 all-gather.4.cloned.1.call-done.terms_ref
  212.3 4.7 %shard_map.107 = bf16[640,512]{1,0:T(8,128)(2,1)} custom-call(bf16[1024,1152]{1,0:T(8,128)(2,1)S(1)} %bitcast.15, bf16[1152,1920]{1,0:T(8,128)(2,1)} %all-gather.4.cloned.1.call-done.terms_ref), custom_call_target="tpu_custom_call" | custom-call | flops 754974720 | bytes 7438336 | tf_op jit(solution)/shard_map/pallas_call | solution.py:24
  217.0 6.1 %shard_map.106 = (bf16[512,640]{1,0:T(8,128)(2,1)}, bf16[512,640]{1,0:T(8,128)(2,1)}) custom-call(bf16[1024,1152]{1,0:T(8,128)(2,1)S(1)} %bitcast.16, bf16[1152,1920]{1,0:T(8,128)(2,1)} %all-gather.4.cloned.1.call-done.terms_ref), custom_call_target="tpu_custom_call" | custom-call | flops 1509949440 | bytes 8093696 | tf_op jit(solution)/shard_map/pallas_call | solution.py:24
Async XLA Ops:
  7.2 119.2 %all-gather.6.cloned.1.call-start = ((), (), s32[]{:S(2)}) async-start(), calls=%async_computation.5 | async-start | bytes 9830400 | tf_op jit(solution)/shard_map/all_gather | solution.py:206
  7.2 1.1 copy-start.2
  8.3 1.1 copy-start.3
  9.4 1.1 copy-start.4
  10.5 1.6 copy-start.5
  10.5 1.6 copy-start.6
  10.5 1.6 copy-start.7
  10.5 1.6 copy-start.8
  12.0 200.3 %all-gather.4.cloned.1.call-start = ((), (), s32[]{:S(2)}) async-start(), calls=%async_computation.4 | async-start | bytes 5529600 | tf_op jit(solution)/shard_map/all_gather | solution.py:234
  126.4 1.7 copy-start
  136.5 1.1 copy-start.1
Sparse Core Ops, SparseCore 0:
  12.2 96.2 all-gather.5
  137.8 57.2 all-gather.3

commit v4 on v3

--- a/solution.py
+++ b/solution.py
@@ -17,7 +17,7 @@
     return lax.dot_general(a, b, dims, preferred_element_type=F32)
 
 
-def kernel_call(body, out_shape, args, flops, scratch=(), in_hbm=()):
+def kernel_call(body, out_shape, args, flops, scratch=(), in_hbm=(), vmem=48):
     moved = sum(a.size * a.dtype.itemsize for a in args)
     outs = out_shape if isinstance(out_shape, tuple) else (out_shape,)
     moved += sum(o.size * o.dtype.itemsize for o in outs)
@@ -25,12 +25,12 @@
         body,
         out_shape=out_shape,
         in_specs=[
-            pl.BlockSpec(memory_space=pltpu.HBM if i in in_hbm else pltpu.VMEM)
+            pl.BlockSpec(memory_space=pl.ANY if i in in_hbm else pltpu.VMEM)
             for i in range(len(args))
         ],
         out_specs=jax.tree.map(lambda _: pl.BlockSpec(memory_space=pltpu.VMEM), out_shape),
         scratch_shapes=list(scratch),
-        compiler_params=pltpu.CompilerParams(vmem_limit_bytes=48 << 20),
+        compiler_params=pltpu.CompilerParams(vmem_limit_bytes=vmem << 20),
         cost_estimate=pl.CostEstimate(flops=flops, bytes_accessed=moved, transcendentals=0),
     )(*args)
 
@@ -98,27 +98,37 @@
     out_ref[:, 2 * quarter :] = packed[...].reshape(experts * MAIN, LANES).astype(BF)
 
 
-def expert_kernel(rows_ref, weights_ref, terms_ref, back_ref, token_rows, grad_rows, packed):
+def expert_kernel(
+    rows_hbm, weights_hbm, terms_ref, back_ref, rows_ref, weights_ref, packed, row_sems, weight_sems
+):
     groups, n, _ = rows_ref.shape
     quarter = weights_ref.shape[1]
     ffw = weights_ref.shape[2] // 3
     m = n // MAIN
     pieces = quarter // LANES
+    loads = []
     for q in range(groups):
-        at = q * quarter
-        token_rows[:n, at : at + quarter] = rows_ref[q, :, :quarter]
-        grad_rows[:n, at : at + quarter] = rows_ref[q, :, quarter : 2 * quarter]
+        rows = pltpu.make_async_copy(rows_hbm.at[q], rows_ref.at[q], row_sems.at[q])
+        weights = pltpu.make_async_copy(weights_hbm.at[q], weights_ref.at[q], weight_sems.at[q])
+        rows.start()
+        weights.start()
+        loads.append((rows, weights))
+
+    gate, up, back = 0.0, 0.0, 0.0
+    for q, (rows, weights) in enumerate(loads):
+        rows.wait()
         packed[...] = rows_ref[q, :, 2 * quarter :].astype(F32).reshape(m, MAIN, LANES)
-        for j in range(pieces):
-            to = slice(at + j * LANES, at + (j + 1) * LANES)
-            token_rows[n:, to] = packed[:, j, :].astype(BF)
-            grad_rows[n:, to] = packed[:, pieces + j, :].astype(BF)
-
-    def product(rows, part):
-        weights = weights_ref[:, :, part * ffw : (part + 1) * ffw]
-        return dot(rows[...], weights.reshape(groups * quarter, ffw))
-
-    gate, up, back = product(token_rows, 0), product(token_rows, 1), product(grad_rows, 2)
+        extra = [packed[:, j, :].astype(BF) for j in range(2 * pieces)]
+        token_rows = jnp.concatenate(
+            [rows_ref[q, :, :quarter], jnp.concatenate(extra[:pieces], axis=1)], axis=0
+        )
+        grad_rows = jnp.concatenate(
+            [rows_ref[q, :, quarter : 2 * quarter], jnp.concatenate(extra[pieces:], axis=1)], axis=0
+        )
+        weights.wait()
+        gate = gate + dot(token_rows, weights_ref[q, :, :ffw])
+        up = up + dot(token_rows, weights_ref[q, :, ffw : 2 * ffw])
+        back = back + dot(grad_rows, weights_ref[q, :, 2 * ffw :])
     sigmoid = 1.0 / (1.0 + jnp.exp(-gate))
     silu = gate * sigmoid
     gate_delta = (back * up * sigmoid * (1.0 + gate * (1.0 - sigmoid))).astype(BF)
@@ -202,6 +212,7 @@
         shape((quarter, 3 * ffw), BF),
         (w_gate[0], w_up[0], w_down[0]),
         0,
+        vmem=60,
     )
     weights = lax.all_gather(weights, "rep", axis=0)
     ids = expert_ids.T
@@ -226,10 +237,14 @@
         (wide_rows, weights),
         10 * (n + m) * groups * quarter * ffw,
         (
-            pltpu.VMEM((n + m, groups * quarter), BF),
-            pltpu.VMEM((n + m, groups * quarter), BF),
+            pltpu.VMEM((groups, n, 2 * quarter + LANES), BF),
+            pltpu.VMEM((groups, quarter, 3 * ffw), BF),
             pltpu.VMEM((m, MAIN, LANES), F32),
+            pltpu.SemaphoreType.DMA((groups,)),
+            pltpu.SemaphoreType.DMA((groups,)),
         ),
+        in_hbm=(0, 1),
+        vmem=60,
     )
     terms = lax.all_gather(terms, "rep", axis=0, tiled=True)
     back = exchange(back, "rep")
@@ -247,6 +262,9 @@
         (rows, terms),
         2 * (main + experts) * quarter * ffw,
         (packed,),
+    )
+    ids, grad_gate, grad_up, grad_down = lax.optimization_barrier(
+        (ids, grad_gate, grad_up, grad_down)
     )
     token_grad = kernel_call(
         combine_kernel,

time: 231 us -> 220 us (0.952)
  blocking collectives: 186 us -> 133 us
  waiting for transfers between devices: 0.04 us -> 25 us
  starting transfers between devices: 0.08 us -> 19.5 us
  local copies, waits for them, and re-layouts: 6.04 us -> 0.02 us
  Pallas kernels: 24 us -> 27.9 us
    all_to_all x4 -> x3, blocking collectives: 186 us -> 133 us  [exchange(): return lax.all_to_all(blocks, axis, split_axis=0, concat_axis=0, tiled=True)]
    all_to_all x0 -> x1, starting transfers between devices: none -> 19.5 us  [exchange(): return lax.all_to_all(blocks, axis, split_axis=0, concat_axis=0, tiled=True)]
    all_gather x1, waiting for transfers between devices: 0.01 us -> 18.2 us  [body(): terms = lax.all_gather(terms, 'rep', axis=0, tiled=True)]
    all_to_all x0 -> x1, waiting for transfers between devices: none -> 6.77 us  [exchange(): return lax.all_to_all(blocks, axis, split_axis=0, concat_axis=0, tiled=True)]
    unnamed x18 -> x8, local copies, waits for them, and re-layouts: 6.04 us -> 0.02 us
    pallas_call x6, Pallas kernels: 24 us -> 27.9 us  [kernel_call(): pl.pallas_call(body, out_shape=out_shape, in_specs=[pl.BlockSpec(memory_s...]
  transfers between devices with their start and end apart: 2 -> 3, of which waited for: 0 -> 2; matrix products, arithmetic and copies ran while one was open for 0% -> 0% of each run, Pallas kernels for 1% -> 6%
where the time goes in v4:
time: 220 us
  blocking collectives  133 us (60%)
  Pallas kernels  27.9 us (13%)
  waiting for transfers between devices  25 us (11%)
  starting transfers between devices  19.5 us (9%)
  between operations  14.1 us (6%)
    all_to_all x3, blocking collectives, exchange(): return lax.all_to_all(blocks, axis, split_axis=0, concat_axis=0, tiled=True)  133 us
    pallas_call x6, Pallas kernels, kernel_call(): pl.pallas_call(body, out_shape=out_shape, in_specs=[pl.BlockSpec(memory_s...  27.9 us
    all_to_all x1, starting transfers between devices, exchange(): return lax.all_to_all(blocks, axis, split_axis=0, concat_axis=0, tiled=True)  19.5 us
    all_gather x1, waiting for transfers between devices, body(): terms = lax.all_gather(terms, 'rep', axis=0, tiled=True)  18.2 us
    all_to_all x1, waiting for transfers between devices, exchange(): return lax.all_to_all(blocks, axis, split_axis=0, concat_axis=0, tiled=True)  6.77 us
  transfers between devices with their start and end apart: 3, of which 2 were waited for; matrix products, arithmetic and copies ran while one was open for 0% of the time, Pallas kernels for 6%

profile of v4, /device:TPU:1, one launch (start us, length us, event | category | flops | bytes accessed | tf_op | source)
XLA Modules:
  0.0 219.7 jit_solution(11103937820575777464)
XLA Ops:
  7.2 0.0 all-gather.6.cloned.1.call-start
  7.2 0.0 copy-start
  7.2 0.0 copy-start.1
  7.2 0.0 copy-start.2
  7.2 0.0 copy-start.3
  7.3 3.1 %shard_map.103 = bf16[512,1920]{1,0:T(8,128)(2,1)} custom-call(bf16[512,640]{1,0:T(8,128)(2,1)} %bitcast.23, bf16[512,640]{1,0:T(8,128)(2,1)} %bitcast.24, bf16[640,512]{1,0:T(8,128)(2,1)} %bitcast.25), custom_call_target="tpu_custom_call" | custom-call | bytes 3932160 | tf_op jit(solution)/shard_map/pallas_call | solution.py:24
  10.3 0.0 all-gather.6.cloned.1.call-update
  10.3 0.0 all-gather.4.cloned.1.call-start
  10.4 0.0 copy-done
  10.4 0.0 copy-done.1
  10.4 0.0 copy-done.2
  10.4 0.0 copy-done.3
  10.4 1.9 shard_map.102
  12.3 74.9 %all_to_all.20 = bf16[128,8,1152]{2,1,0:T(8,128)(2,1)S(1)} all-to-all(bf16[128,8,1152]{2,1,0:T(8,128)(2,1)S(1)} %bitcast.17), channel_id=1, replica_groups=mesh['rep'=4,'ep'=128] {'ep'}, dimensions={0} | all-to-all | bytes 4718592 | tf_op jit(solution)/shard_map/all_to_all | solution.py:197
  87.2 37.5 %all_to_all.21.rows_hbm = bf16[4,256,1152]{2,1,0:T(8,128)(2,1)} all-to-all(bf16[4,256,1152]{2,1,0:T(8,128)(2,1)S(1)} %bitcast.14), channel_id=1, replica_groups=mesh['rep'=4,'ep'=128] {'rep'}, dimensions={0} | all-to-all | bytes 4718592 | tf_op jit(solution)/shard_map/all_to_all | solution.py:197
  124.7 0.0 all-gather.6.cloned.1.call-done
  124.7 9.5 %shard_map.104 = (bf16[288,1920]{1,0:T(8,128)(2,1)}, bf16[4,256,640]{2,1,0:T(8,128)(2,1)}) custom-call(bf16[4,256,1152]{2,1,0:T(8,128)(2,1)} %all_to_all.21.rows_hbm, bf16[4,512,1920]{2,1,0:T(8,128)(2,1)} %bitcast.26), custom_call_target="tpu_custom_call" | custom-call | flops 3774873600 | bytes 12640256 | tf_op jit(solution)/shard_map/pallas_call | solution.py:24
  134.2 0.0 all-gather.4.cloned.1.call-update
  134.2 20.7 %all_to_all.22 = bf16[4,256,640]{2,1,0:T(8,128)(2,1)} all-to-all(bf16[4,256,640]{2,1,0:T(8,128)(2,1)} %get-tuple-element.16), channel_id=1, replica_groups=mesh['rep'=4,'ep'=128] {'rep'}, dimensions={0} | all-to-all | bytes 2621440 | tf_op jit(solution)/shard_map/all_to_all | solution.py:197
  154.9 19.5 %all-to-all-start.3 = ((bf16[128,8,640]{2,1,0:T(8,128)(2,1)}), bf16[128,8,640]{2,1,0:T(8,128)(2,1)}, u32[]{:S(2)}, u32[]{:S(2)}) async-start(bf16[128,8,640]{2,1,0:T(8,128)(2,1)} %bitcast.21), calls=%async_computation.3 | async-start | bytes 2621440 | tf_op jit(solution)/shard_map/all_to_all | solution.py:197
  174.4 18.2 %all-gather.4.cloned.1.call-done.terms_ref = bf16[1152,1920]{1,0:T(8,128)(2,1)} async-done(((bf16[288,1920]{1,0:T(8,128)(2,1)}), bf16[1152,1920]{1,0:T(8,128)(2,1)}) %all-gather.4.cloned.1.call-update) | async-done | bytes 4423696 | tf_op jit(solution)/shard_map/all_gather | solution.py:249
  192.6 4.7 %shard_map.106 = bf16[640,512]{1,0:T(8,128)(2,1)} custom-call(bf16[1024,1152]{1,0:T(8,128)(2,1)S(1)} %bitcast.15, bf16[1152,1920]{1,0:T(8,128)(2,1)} %all-gather.4.cloned.1.call-done.terms_ref), custom_call_target="tpu_custom_call" | custom-call | flops 754974720 | bytes 7438336 | tf_op jit(solution)/shard_map/pallas_call | solution.py:24
  197.3 6.1 %shard_map.105 = (bf16[512,640]{1,0:T(8,128)(2,1)}, bf16[512,640]{1,0:T(8,128)(2,1)}) custom-call(bf16[1024,1152]{1,0:T(8,128)(2,1)S(1)} %bitcast.16, bf16[1152,1920]{1,0:T(8,128)(2,1)} %all-gather.4.cloned.1.call-done.terms_ref), custom_call_target="tpu_custom_call" | custom-call | flops 1509949440 | bytes 8093696 | tf_op jit(solution)/shard_map/pallas_call | solution.py:24
  203.4 6.8 %all-to-all-done.3 = bf16[128,8,640]{2,1,0:T(8,128)(2,1)} async-done(((bf16[128,8,640]{2,1,0:T(8,128)(2,1)}), bf16[128,8,640]{2,1,0:T(8,128)(2,1)}, u32[]{:S(2)}, u32[]{:S(2)}) %all-to-all-start.3) | async-done | bytes 1310752 | tf_op jit(solution)/shard_map/all_to_all | solution.py:197
  210.2 2.7 %shard_map.107 = bf16[128,512]{1,0:T(8,128)(2,1)} custom-call(s32[8,128]{1,0:T(8,128)S(1)} %bitcast.19, bf16[1024,640]{1,0:T(8,128)(2,1)} %bitcast.10.rows_ref), custom_call_target="tpu_custom_call" | custom-call | flops 134217728 | bytes 1445888 | tf_op jit(solution)/shard_map/pallas_call | solution.py:24
Async XLA Ops:
  7.2 117.5 %all-gather.6.cloned.1.call-start = ((), (), s32[]{:S(2)}) async-start(), calls=%async_computation.5 | async-start | bytes 9830400 | tf_op jit(solution)/shard_map/all_gather | solution.py:217
  7.2 3.2 %copy-start = (bf16[128,512]{1,0:T(8,128)(2,1)S(1)}, bf16[128,512]{1,0:T(8,128)(2,1)}, u32[]{:S(2)}) copy-start(bf16[128,512]{1,0:T(8,128)(2,1)} %tokens_hbm.1) | copy-start | bytes 393220
  7.2 3.2 %copy-start.1 = (bf16[128,512]{1,0:T(8,128)(2,1)S(1)}, bf16[128,512]{1,0:T(8,128)(2,1)}, u32[]{:S(2)}) copy-start(bf16[128,512]{1,0:T(8,128)(2,1)} %grads_hbm.1) | copy-start | bytes 393220
  7.2 3.2 %copy-start.2 = (s32[128,8]{0,1:T(8,128)S(1)}, s32[128,8]{0,1:T(8,128)}, u32[]{:S(2)}) copy-start(s32[128,8]{0,1:T(8,128)} %param.9) | copy-start | bytes 12292
  7.2 3.2 %copy-start.3 = (bf16[128,8]{0,1:T(8,128)(2,1)S(1)}, bf16[128,8]{0,1:T(8,128)(2,1)}, u32[]{:S(2)}) copy-start(bf16[128,8]{0,1:T(8,128)(2,1)} %param.10) | copy-start | bytes 6148
  10.3 182.2 %all-gather.4.cloned.1.call-start = ((), (), s32[]{:S(2)}) async-start(), calls=%async_computation.4 | async-start | bytes 5529600 | tf_op jit(solution)/shard_map/all_gather | solution.py:249
  154.9 55.2 %all-to-all-start.3 = ((bf16[128,8,640]{2,1,0:T(8,128)(2,1)}), bf16[128,8,640]{2,1,0:T(8,128)(2,1)}, u32[]{:S(2)}, u32[]{:S(2)}) async-start(bf16[128,8,640]{2,1,0:T(8,128)(2,1)} %bitcast.21), calls=%async_computation.3 | async-start | bytes 2621440 | tf_op jit(solution)/shard_map/all_to_all | solution.py:197
Sparse Core Ops, SparseCore 0:
  10.5 96.2 all-gather.5
  134.4 58.1 all-gather.3

commit v5 on v4

--- a/solution.py
+++ b/solution.py
@@ -17,7 +17,7 @@
     return lax.dot_general(a, b, dims, preferred_element_type=F32)
 
 
-def kernel_call(body, out_shape, args, flops, scratch=(), in_hbm=(), vmem=48):
+def kernel_call(body, out_shape, args, flops, scratch=(), in_hbm=(), in_smem=(), out_hbm=False, vmem=48):
     moved = sum(a.size * a.dtype.itemsize for a in args)
     outs = out_shape if isinstance(out_shape, tuple) else (out_shape,)
     moved += sum(o.size * o.dtype.itemsize for o in outs)
@@ -25,10 +25,14 @@
         body,
         out_shape=out_shape,
         in_specs=[
-            pl.BlockSpec(memory_space=pl.ANY if i in in_hbm else pltpu.VMEM)
+            pl.BlockSpec(
+                memory_space=pl.ANY if i in in_hbm else pltpu.SMEM if i in in_smem else pltpu.VMEM
+            )
             for i in range(len(args))
         ],
-        out_specs=jax.tree.map(lambda _: pl.BlockSpec(memory_space=pltpu.VMEM), out_shape),
+        out_specs=jax.tree.map(
+            lambda _: pl.BlockSpec(memory_space=pl.ANY if out_hbm else pltpu.VMEM), out_shape
+        ),
         scratch_shapes=list(scratch),
         compiler_params=pltpu.CompilerParams(vmem_limit_bytes=vmem << 20),
         cost_estimate=pl.CostEstimate(flops=flops, bytes_accessed=moved, transcendentals=0),
@@ -59,11 +63,16 @@
     return spread(slot) == number.astype(F32)
 
 
-def pack_weights_kernel(gate_ref, up_ref, down_ref, out_ref):
-    ffw = gate_ref.shape[1]
-    out_ref[:, :ffw] = gate_ref[...]
-    out_ref[:, ffw : 2 * ffw] = up_ref[...]
-    out_ref[:, 2 * ffw :] = down_ref[...].T
+def pack_weights_kernel(gate_hbm, up_hbm, out_hbm, sems):
+    ffw = gate_hbm.shape[1]
+    copies = (
+        pltpu.make_async_copy(gate_hbm, out_hbm.at[:, :ffw], sems.at[0]),
+        pltpu.make_async_copy(up_hbm, out_hbm.at[:, ffw:], sems.at[1]),
+    )
+    for copy in copies:
+        copy.start()
+    for copy in copies:
+        copy.wait()
 
 
 def dispatch_kernel(
@@ -99,20 +108,28 @@
 
 
 def expert_kernel(
-    rows_hbm, weights_hbm, terms_ref, back_ref, rows_ref, weights_ref, packed, row_sems, weight_sems
+    rank_ref, rows_hbm, weights_hbm, *refs
 ):
+    *downs_hbm, terms_ref, back_ref, rows_ref, weights_ref, downs_ref, grad_rows, packed, sems = refs
     groups, n, _ = rows_ref.shape
     quarter = weights_ref.shape[1]
-    ffw = weights_ref.shape[2] // 3
+    ffw = weights_ref.shape[2] // 2
     m = n // MAIN
     pieces = quarter // LANES
     loads = []
     for q in range(groups):
-        rows = pltpu.make_async_copy(rows_hbm.at[q], rows_ref.at[q], row_sems.at[q])
-        weights = pltpu.make_async_copy(weights_hbm.at[q], weights_ref.at[q], weight_sems.at[q])
-        rows.start()
-        weights.start()
-        loads.append((rows, weights))
+        load = (
+            pltpu.make_async_copy(rows_hbm.at[q], rows_ref.at[q], sems.at[0, q]),
+            pltpu.make_async_copy(weights_hbm.at[q], weights_ref.at[q], sems.at[1, q]),
+        )
+        load[0].start()
+        load[1].start()
+        loads.append(load)
+    down_loads = [
+        pltpu.make_async_copy(downs_hbm[k], downs_ref.at[k], sems.at[2, k]) for k in range(groups)
+    ]
+    for load in down_loads:
+        load.start()
 
     gate, up, back = 0.0, 0.0, 0.0
     for q, (rows, weights) in enumerate(loads):
@@ -122,13 +139,15 @@
         token_rows = jnp.concatenate(
             [rows_ref[q, :, :quarter], jnp.concatenate(extra[:pieces], axis=1)], axis=0
         )
-        grad_rows = jnp.concatenate(
-            [rows_ref[q, :, quarter : 2 * quarter], jnp.concatenate(extra[pieces:], axis=1)], axis=0
-        )
+        grad_rows[q, :n, :] = rows_ref[q, :, quarter : 2 * quarter]
+        grad_rows[q, n:, :] = jnp.concatenate(extra[pieces:], axis=1)
         weights.wait()
         gate = gate + dot(token_rows, weights_ref[q, :, :ffw])
-        up = up + dot(token_rows, weights_ref[q, :, ffw : 2 * ffw])
-        back = back + dot(grad_rows, weights_ref[q, :, 2 * ffw :])
+        up = up + dot(token_rows, weights_ref[q, :, ffw:])
+    for k, load in enumerate(down_loads):
+        load.wait()
+        source = lax.rem(rank_ref[0] - k + groups, groups)
+        back = back + dot(grad_rows[source], downs_ref[k], CONTRACT_LAST)
     sigmoid = 1.0 / (1.0 + jnp.exp(-gate))
     silu = gate * sigmoid
     gate_delta = (back * up * sigmoid * (1.0 + gate * (1.0 - sigmoid))).astype(BF)
@@ -140,7 +159,7 @@
         packed[:, j, :] = jnp.zeros((m, LANES), F32)
     for q in range(groups):
         out = dot(gate_delta, weights_ref[q, :, :ffw], CONTRACT_LAST)
-        out = out + dot(up_delta, weights_ref[q, :, ffw : 2 * ffw], CONTRACT_LAST)
+        out = out + dot(up_delta, weights_ref[q, :, ffw:], CONTRACT_LAST)
         back_ref[q, :, :quarter] = out[:n, :].astype(BF)
         for j in range(pieces):
             packed[:, j, :] = out[n:, j * LANES : (j + 1) * LANES]
@@ -209,9 +228,12 @@
 
     weights = kernel_call(
         pack_weights_kernel,
-        shape((quarter, 3 * ffw), BF),
-        (w_gate[0], w_up[0], w_down[0]),
+        shape((quarter, 2 * ffw), BF),
+        (w_gate[0], w_up[0]),
         0,
+        (pltpu.SemaphoreType.DMA((2,)),),
+        in_hbm=(0, 1),
+        out_hbm=True,
         vmem=60,
     )
     weights = lax.all_gather(weights, "rep", axis=0)
@@ -229,21 +251,29 @@
         ),
         in_hbm=(2, 3),
     )
+    down, sent = lax.optimization_barrier((w_down[0], sent))
+    downs = [down] + [
+        lax.ppermute(down, "rep", [(i, (i + k) % groups) for i in range(groups)])
+        for k in range(1, groups)
+    ]
     rows = exchange(sent.reshape(experts, MAIN, -1), "ep").reshape(main, -1)
+    rows, *downs = lax.optimization_barrier((rows, *downs))
     wide_rows = exchange(rows.reshape(groups, n, -1), "rep")
     terms, back = kernel_call(
         expert_kernel,
         (shape((n + m, 3 * ffw), BF), shape((groups, n, quarter + LANES), BF)),
-        (wide_rows, weights),
+        (lax.axis_index("rep").astype(jnp.int32).reshape(1), wide_rows, weights, *downs),
         10 * (n + m) * groups * quarter * ffw,
         (
             pltpu.VMEM((groups, n, 2 * quarter + LANES), BF),
-            pltpu.VMEM((groups, quarter, 3 * ffw), BF),
+            pltpu.VMEM((groups, quarter, 2 * ffw), BF),
+            pltpu.VMEM((groups, ffw, quarter), BF),
+            pltpu.VMEM((groups, n + m, quarter), BF),
             pltpu.VMEM((m, MAIN, LANES), F32),
-            pltpu.SemaphoreType.DMA((groups,)),
-            pltpu.SemaphoreType.DMA((groups,)),
+            pltpu.SemaphoreType.DMA((3, groups)),
         ),
-        in_hbm=(0, 1),
+        in_smem=(0,),
+        in_hbm=range(1, 3 + groups),
         vmem=60,
     )
     terms = lax.all_gather(terms, "rep", axis=0, tiled=True)

time: 220 us -> 262 us (1.19)
  blocking collectives: 133 us -> 20 us
  waiting for transfers between devices: 25 us -> 106 us
  Pallas kernels: 27.9 us -> 67.4 us
  starting transfers between devices: 19.5 us -> 52.9 us
    all_to_all x3 -> x1, blocking collectives: 133 us -> 20 us  [exchange(): return lax.all_to_all(blocks, axis, split_axis=0, concat_axis=0, tiled=True)]
    ppermute x0 -> x3, waiting for transfers between devices: none -> 53.5 us  [body(): lax.ppermute(down, 'rep', [(i, (i + k) % groups) for i in range(groups)])]
    pallas_call x6, Pallas kernels: 27.9 us -> 67.4 us  [kernel_call(): pl.pallas_call(body, out_shape=out_shape, in_specs=[pl.BlockSpec(memory_s...]
    all_to_all x1 -> x3, waiting for transfers between devices: 6.77 us -> 34 us  [exchange(): return lax.all_to_all(blocks, axis, split_axis=0, concat_axis=0, tiled=True)]
    all_to_all x1 -> x3, starting transfers between devices: 19.5 us -> 43.5 us  [exchange(): return lax.all_to_all(blocks, axis, split_axis=0, concat_axis=0, tiled=True)]
    ppermute x0 -> x3, starting transfers between devices: none -> 9.34 us  [body(): lax.ppermute(down, 'rep', [(i, (i + k) % groups) for i in range(groups)])]
  transfers between devices with their start and end apart: 3 -> 8, of which waited for: 2 -> 6; matrix products, arithmetic and copies ran while one was open for 0% -> 0% of each run, Pallas kernels for 6% -> 6%
where the time goes in v5:
time: 262 us
  waiting for transfers between devices  106 us (40%)
  Pallas kernels  67.4 us (26%)
  starting transfers between devices  52.9 us (20%)
  blocking collectives  20 us (8%)
  between operations  14.2 us (5%)
    pallas_call x6, Pallas kernels, kernel_call(): pl.pallas_call(body, out_shape=out_shape, in_specs=[pl.BlockSpec(memory_s...  67.4 us
    ppermute x3, waiting for transfers between devices, body(): lax.ppermute(down, 'rep', [(i, (i + k) % groups) for i in range(groups)])  53.5 us
    all_to_all x3, starting transfers between devices, exchange(): return lax.all_to_all(blocks, axis, split_axis=0, concat_axis=0, tiled=True)  43.5 us
    all_to_all x3, waiting for transfers between devices, exchange(): return lax.all_to_all(blocks, axis, split_axis=0, concat_axis=0, tiled=True)  34 us
    all_to_all x1, blocking collectives, exchange(): return lax.all_to_all(blocks, axis, split_axis=0, concat_axis=0, tiled=True)  20 us
    all_gather x1, waiting for transfers between devices, body(): terms = lax.all_gather(terms, 'rep', axis=0, tiled=True)  18.6 us
    ppermute x3, starting transfers between devices, body(): lax.ppermute(down, 'rep', [(i, (i + k) % groups) for i in range(groups)])  9.34 us
  transfers between devices with their start and end apart: 8, of which 6 were waited for; matrix products, arithmetic and copies ran while one was open for 0% of the time, Pallas kernels for 6%

profile of v5, /device:TPU:1, one launch (start us, length us, event | category | flops | bytes accessed | tf_op | source)
XLA Modules:
  0.0 261.5 jit_solution(774369521666228820)
XLA Ops:
  7.2 0.0 copy-start.3
  7.2 0.0 copy-start.2
  7.2 0.0 copy-start.1
  7.2 0.0 copy-start
  7.2 0.0 all-gather.6.cloned.1.call-start
  7.3 40.8 %shard_map.103 = bf16[512,1280]{1,0:T(8,128)(2,1)} custom-call(bf16[512,640]{1,0:T(8,128)(2,1)} %bitcast.19, bf16[512,640]{1,0:T(8,128)(2,1)} %bitcast.20), custom_call_target="tpu_custom_call" | custom-call | bytes 2621440 | tf_op jit(solution)/shard_map/pallas_call | solution.py:24
  48.1 0.0 all-gather.6.cloned.1.call-update
  48.1 0.0 copy-done.3
  48.1 0.0 copy-done.2
  48.1 0.0 copy-done.1
  48.1 0.0 copy-done
  48.1 3.3 %shard_map.102 = bf16[1024,1152]{1,0:T(8,128)(2,1)} custom-call(s32[8,128]{1,0:T(8,128)S(1)} %bitcast.16, bf16[8,128]{1,0:T(8,128)(2,1)S(1)} %bitcast.18, bf16[128,512]{1,0:T(8,128)(2,1)S(1)} %copy-done, bf16[128,512]{1,0:T(8,128)(2,1)S(1)} %copy-done.1), custom_call_target="tpu_custom_call" | custom-call | flops 268435456 | bytes 2627584 | tf_op jit(solution)/shard_map/pallas_call | solution.py:24
  51.5 0.0 copy-start.4
  51.5 19.0 %all-to-all-start = ((bf16[128,8,1152]{2,1,0:T(8,128)(2,1)}), bf16[128,8,1152]{2,1,0:T(8,128)(2,1)}, u32[]{:S(2)}, u32[]{:S(2)}) async-start(bf16[128,8,1152]{2,1,0:T(8,128)(2,1)} %bitcast.3), calls=%async_computation | async-start | bytes 4718592 | tf_op jit(solution)/shard_map/all_to_all | solution.py:216
  70.5 0.0 copy-done.4
  70.5 4.4 %collective-permute-start.2 = (bf16[640,512]{1,0:T(8,128)(2,1)S(1)}, bf16[640,512]{1,0:T(8,128)(2,1)S(1)}, u32[]{:S(2)}, u32[]{:S(2)}) collective-permute-start(bf16[640,512]{1,0:T(8,128)(2,1)S(1)} %bitcast.24), channel_id=1, source_target_pairs={{0,384},{128,0},{256,128},{384,256},{1,385},{129,1},{257,129},{385... | collective-permute-start | bytes 1966088 | tf_op jit(solution)/shard_map/ppermute | solution.py:256
  74.9 2.4 collective-permute-start.1
  77.3 2.5 collective-permute-start
  79.8 22.8 %collective-permute-done.2.refs_3_ = bf16[640,512]{1,0:T(8,128)(2,1)S(1)} collective-permute-done((bf16[640,512]{1,0:T(8,128)(2,1)S(1)}, bf16[640,512]{1,0:T(8,128)(2,1)S(1)}, u32[]{:S(2)}, u32[]{:S(2)}) %collective-permute-start.2) | collective-permute-done | bytes 655392 | tf_op jit(solution)/shard_map/ppermute | solution.py:256
  102.7 0.0 copy-start.5
  102.7 5.9 %collective-permute-done.1.refs_2_ = bf16[640,512]{1,0:T(8,128)(2,1)S(1)} collective-permute-done((bf16[640,512]{1,0:T(8,128)(2,1)S(1)}, bf16[640,512]{1,0:T(8,128)(2,1)S(1)}, u32[]{:S(2)}, u32[]{:S(2)}) %collective-permute-start.1) | collective-permute-done | bytes 655392 | tf_op jit(solution)/shard_map/ppermute | solution.py:256
  108.6 0.0 copy-start.6
  108.6 24.8 %collective-permute-done.refs_1_ = bf16[640,512]{1,0:T(8,128)(2,1)S(1)} collective-permute-done((bf16[640,512]{1,0:T(8,128)(2,1)S(1)}, bf16[640,512]{1,0:T(8,128)(2,1)S(1)}, u32[]{:S(2)}, u32[]{:S(2)}) %collective-permute-start) | collective-permute-done | bytes 655392 | tf_op jit(solution)/shard_map/ppermute | solution.py:256
  133.4 0.0 copy-start.7
  133.4 0.0 all-to-all-done
  133.4 0.0 copy-done.5
  133.4 0.0 copy-done.6
  133.4 0.8 copy-done.7
  134.2 4.8 %all-to-all-start.1 = ((bf16[4,256,1152]{2,1,0:T(8,128)(2,1)}), bf16[4,256,1152]{2,1,0:T(8,128)(2,1)}, u32[]{:S(2)}, u32[]{:S(2)}) async-start(bf16[4,256,1152]{2,1,0:T(8,128)(2,1)} %bitcast.6), calls=%async_computation.1 | async-start | bytes 4718592 | tf_op jit(solution)/shard_map/all_to_all | solution.py:216
  139.0 0.0 all-gather.4.cloned.1.call-start
  139.0 28.7 %all-to-all-done.1.rows_hbm = bf16[4,256,1152]{2,1,0:T(8,128)(2,1)} async-done(((bf16[4,256,1152]{2,1,0:T(8,128)(2,1)}), bf16[4,256,1152]{2,1,0:T(8,128)(2,1)}, u32[]{:S(2)}, u32[]{:S(2)}) %all-to-all-start.1) | async-done | bytes 2359328 | tf_op jit(solution)/shard_map/all_to_all | solution.py:216
  167.8 0.0 all-gather.6.cloned.1.call-done
  167.8 9.7 %shard_map.104 = (bf16[288,1920]{1,0:T(8,128)(2,1)}, bf16[4,256,640]{2,1,0:T(8,128)(2,1)}) custom-call(s32[1]{0:T(128)} %bitcast.5.rank_ref, bf16[4,256,1152]{2,1,0:T(8,128)(2,1)} %all-to-all-done.1.rows_hbm, bf16[4,512,1280]{2,1,0:T(8,128)(2,1)} %bitcast.22, bf16[640,512]{1,0:T(8,128)(2,1)} %bitcast.23, bf16[640,512]{1,0:T(8,128)(2,1)} %copy-done.7, ...), custom_call_target="tpu_custom_call" | custom-call | flops 3774873600 | bytes 12640260 | tf_op jit(solution)/shard_map/pallas_call | solution.py:24
  177.4 0.0 all-gather.4.cloned.1.call-update
  177.5 20.0 %all_to_all.20 = bf16[4,256,640]{2,1,0:T(8,128)(2,1)} all-to-all(bf16[4,256,640]{2,1,0:T(8,128)(2,1)} %get-tuple-element.30), channel_id=1, replica_groups=mesh['rep'=4,'ep'=128] {'rep'}, dimensions={0} | all-to-all | bytes 2621440 | tf_op jit(solution)/shard_map/all_to_all | solution.py:216
  197.5 19.7 %all-to-all-start.3 = ((bf16[128,8,640]{2,1,0:T(8,128)(2,1)}), bf16[128,8,640]{2,1,0:T(8,128)(2,1)S(1)}, u32[]{:S(2)}, u32[]{:S(2)}) async-start(bf16[128,8,640]{2,1,0:T(8,128)(2,1)} %bitcast.10), calls=%async_computation.3 | async-start | bytes 2621440 | tf_op jit(solution)/shard_map/all_to_all | solution.py:216
  217.2 18.6 %all-gather.4.cloned.1.call-done.terms_ref = bf16[1152,1920]{1,0:T(8,128)(2,1)} async-done(((bf16[288,1920]{1,0:T(8,128)(2,1)}), bf16[1152,1920]{1,0:T(8,128)(2,1)}) %all-gather.4.cloned.1.call-update) | async-done | bytes 4423696 | tf_op jit(solution)/shard_map/all_gather | solution.py:279
  235.8 5.4 %shard_map.106 = bf16[640,512]{1,0:T(8,128)(2,1)} custom-call(bf16[1024,1152]{1,0:T(8,128)(2,1)} %bitcast.4.rows_ref, bf16[1152,1920]{1,0:T(8,128)(2,1)} %all-gather.4.cloned.1.call-done.terms_ref), custom_call_target="tpu_custom_call" | custom-call | flops 754974720 | bytes 7438336 | tf_op jit(solution)/shard_map/pallas_call | solution.py:24
  241.2 6.8 %shard_map.105 = (bf16[512,640]{1,0:T(8,128)(2,1)}, bf16[512,640]{1,0:T(8,128)(2,1)}) custom-call(bf16[1024,1152]{1,0:T(8,128)(2,1)} %bitcast.4.rows_ref, bf16[1152,1920]{1,0:T(8,128)(2,1)} %all-gather.4.cloned.1.call-done.terms_ref), custom_call_target="tpu_custom_call" | custom-call | flops 1509949440 | bytes 8093696 | tf_op jit(solution)/shard_map/pallas_call | solution.py:24
  248.0 5.2 %all-to-all-done.3 = bf16[128,8,640]{2,1,0:T(8,128)(2,1)S(1)} async-done(((bf16[128,8,640]{2,1,0:T(8,128)(2,1)}), bf16[128,8,640]{2,1,0:T(8,128)(2,1)S(1)}, u32[]{:S(2)}, u32[]{:S(2)}) %all-to-all-start.3) | async-done | bytes 1310752 | tf_op jit(solution)/shard_map/all_to_all | solution.py:216
  253.3 1.4 shard_map.107
Async XLA Ops:
  7.2 40.9 %copy-start.3 = (bf16[128,8]{0,1:T(8,128)(2,1)S(1)}, bf16[128,8]{0,1:T(8,128)(2,1)}, u32[]{:S(2)}) copy-start(bf16[128,8]{0,1:T(8,128)(2,1)} %param.10) | copy-start | bytes 6148
  7.2 40.9 %copy-start.2 = (s32[128,8]{0,1:T(8,128)S(1)}, s32[128,8]{0,1:T(8,128)}, u32[]{:S(2)}) copy-start(s32[128,8]{0,1:T(8,128)} %param.9) | copy-start | bytes 12292
  7.2 40.9 %copy-start.1 = (bf16[128,512]{1,0:T(8,128)(2,1)S(1)}, bf16[128,512]{1,0:T(8,128)(2,1)}, u32[]{:S(2)}) copy-start(bf16[128,512]{1,0:T(8,128)(2,1)} %grads_hbm.1) | copy-start | bytes 393220
  7.2 40.9 %copy-start = (bf16[128,512]{1,0:T(8,128)(2,1)S(1)}, bf16[128,512]{1,0:T(8,128)(2,1)}, u32[]{:S(2)}) copy-start(bf16[128,512]{1,0:T(8,128)(2,1)} %tokens_hbm.1) | copy-start | bytes 393220
  7.2 160.6 %all-gather.6.cloned.1.call-start = ((), (), s32[]{:S(2)}) async-start(), calls=%async_computation.5 | async-start | bytes 6553600 | tf_op jit(solution)/shard_map/all_gather | solution.py:239
  51.5 19.0 %copy-start.4 = (bf16[1,640,512]{2,1,0:T(8,128)(2,1)S(1)}, bf16[1,640,512]{2,1,0:T(8,128)(2,1)}, u32[]{:S(2)}) copy-start(bf16[1,640,512]{2,1,0:T(8,128)(2,1)} %param.13) | copy-start | bytes 1966084
  51.5 81.9 %all-to-all-start = ((bf16[128,8,1152]{2,1,0:T(8,128)(2,1)}), bf16[128,8,1152]{2,1,0:T(8,128)(2,1)}, u32[]{:S(2)}, u32[]{:S(2)}) async-start(bf16[128,8,1152]{2,1,0:T(8,128)(2,1)} %bitcast.3), calls=%async_computation | async-start | bytes 4718592 | tf_op jit(solution)/shard_map/all_to_all | solution.py:216
  70.5 32.2 %collective-permute-start.2 = (bf16[640,512]{1,0:T(8,128)(2,1)S(1)}, bf16[640,512]{1,0:T(8,128)(2,1)S(1)}, u32[]{:S(2)}, u32[]{:S(2)}) collective-permute-start(bf16[640,512]{1,0:T(8,128)(2,1)S(1)} %bitcast.24), channel_id=1, source_target_pairs={{0,384},{128,0},{256,128},{384,256},{1,385},{129,1},{257,129},{385... | collective-permute-start | bytes 1966088 | tf_op jit(solution)/shard_map/ppermute | solution.py:256
  74.9 33.7 %collective-permute-start.1 = (bf16[640,512]{1,0:T(8,128)(2,1)S(1)}, bf16[640,512]{1,0:T(8,128)(2,1)S(1)}, u32[]{:S(2)}, u32[]{:S(2)}) collective-permute-start(bf16[640,512]{1,0:T(8,128)(2,1)S(1)} %bitcast.25), channel_id=1, source_target_pairs={{0,256},{128,384},{256,0},{384,128},{1,257},{129,385},{257,1},{385... | collective-permute-start | bytes 1966088 | tf_op jit(solution)/shard_map/ppermute | solution.py:256
  77.3 56.1 %collective-permute-start = (bf16[640,512]{1,0:T(8,128)(2,1)S(1)}, bf16[640,512]{1,0:T(8,128)(2,1)S(1)}, u32[]{:S(2)}, u32[]{:S(2)}) collective-permute-start(bf16[640,512]{1,0:T(8,128)(2,1)S(1)} %bitcast.26), channel_id=1, source_target_pairs={{0,128},{128,256},{256,384},{384,0},{1,129},{129,257},{257,385},{3... | collective-permute-start | bytes 1966088 | tf_op jit(solution)/shard_map/ppermute | solution.py:256
  102.7 30.7 %copy-start.5 = (bf16[640,512]{1,0:T(8,128)(2,1)}, bf16[640,512]{1,0:T(8,128)(2,1)S(1)}, u32[]{:S(2)}) copy-start(bf16[640,512]{1,0:T(8,128)(2,1)S(1)} %collective-permute-done.2.refs_3_) | copy-start | bytes 1966084
  108.6 24.8 %copy-start.6 = (bf16[640,512]{1,0:T(8,128)(2,1)}, bf16[640,512]{1,0:T(8,128)(2,1)S(1)}, u32[]{:S(2)}) copy-start(bf16[640,512]{1,0:T(8,128)(2,1)S(1)} %collective-permute-done.1.refs_2_) | copy-start | bytes 1966084
  133.4 0.8 copy-start.7
  134.2 33.6 %all-to-all-start.1 = ((bf16[4,256,1152]{2,1,0:T(8,128)(2,1)}), bf16[4,256,1152]{2,1,0:T(8,128)(2,1)}, u32[]{:S(2)}, u32[]{:S(2)}) async-start(bf16[4,256,1152]{2,1,0:T(8,128)(2,1)} %bitcast.6), calls=%async_computation.1 | async-start | bytes 4718592 | tf_op jit(solution)/shard_map/all_to_all | solution.py:216
  139.0 96.8 %all-gather.4.cloned.1.call-start = ((), (), s32[]{:S(2)}) async-start(), calls=%async_computation.4 | async-start | bytes 5529600 | tf_op jit(solution)/shard_map/all_gather | solution.py:279
  197.5 55.8 %all-to-all-start.3 = ((bf16[128,8,640]{2,1,0:T(8,128)(2,1)}), bf16[128,8,640]{2,1,0:T(8,128)(2,1)S(1)}, u32[]{:S(2)}, u32[]{:S(2)}) async-start(bf16[128,8,640]{2,1,0:T(8,128)(2,1)} %bitcast.10), calls=%async_computation.3 | async-start | bytes 2621440 | tf_op jit(solution)/shard_map/all_to_all | solution.py:216
Sparse Core Ops, SparseCore 0:
  48.2 95.9 all-gather.5
  177.6 58.1 all-gather.3

commit v6 on v4

--- a/solution.py
+++ b/solution.py
@@ -59,11 +59,10 @@
     return spread(slot) == number.astype(F32)
 
 
-def pack_weights_kernel(gate_ref, up_ref, down_ref, out_ref):
+def pack_weights_kernel(gate_ref, up_ref, out_ref):
     ffw = gate_ref.shape[1]
     out_ref[:, :ffw] = gate_ref[...]
-    out_ref[:, ffw : 2 * ffw] = up_ref[...]
-    out_ref[:, 2 * ffw :] = down_ref[...].T
+    out_ref[:, ffw:] = up_ref[...]
 
 
 def dispatch_kernel(
@@ -87,7 +86,7 @@
     loads[0].wait()
     out_ref[:, :quarter] = dot(placing, tokens_ref[...]).astype(BF)
     loads[1].wait()
-    out_ref[:, quarter : 2 * quarter] = dot(weighing, grads_ref[...]).astype(BF)
+    out_ref[:, quarter + LANES :] = dot(weighing, grads_ref[...]).astype(BF)
     last = slot == float(MAIN)
     extra_tokens = dot(jnp.where(last, 1.0, 0.0).astype(BF), tokens_ref[...])
     extra_grads = dot(jnp.where(last, weight, 0.0).astype(BF), grads_ref[...])
@@ -95,40 +94,51 @@
     for j in range(pieces):
         packed[:, j, :] = extra_tokens[:, j * LANES : (j + 1) * LANES]
         packed[:, pieces + j, :] = extra_grads[:, j * LANES : (j + 1) * LANES]
-    out_ref[:, 2 * quarter :] = packed[...].reshape(experts * MAIN, LANES).astype(BF)
+    out_ref[:, quarter : quarter + LANES] = (
+        packed[...].reshape(experts * MAIN, LANES).astype(BF)
+    )
+
+
+def grad_products_kernel(rows_ref, down_ref, out_ref, packed):
+    quarter = down_ref.shape[1]
+    for at, n, m, rows, extra in row_blocks(rows_ref, packed, quarter, 1):
+        out_ref[at : at + n, :] = dot(rows, down_ref[...], CONTRACT_LAST).astype(BF)
+        out_ref[at + n : at + n + m, :] = dot(extra, down_ref[...], CONTRACT_LAST).astype(BF)
 
 
 def expert_kernel(
-    rows_hbm, weights_hbm, terms_ref, back_ref, rows_ref, weights_ref, packed, row_sems, weight_sems
+    rows_hbm, weights_hbm, back_hbm, terms_ref, out_back_ref, rows_ref, weights_ref, back_ref, packed, sems
 ):
     groups, n, _ = rows_ref.shape
     quarter = weights_ref.shape[1]
-    ffw = weights_ref.shape[2] // 3
+    ffw = weights_ref.shape[2] // 2
     m = n // MAIN
     pieces = quarter // LANES
     loads = []
     for q in range(groups):
-        rows = pltpu.make_async_copy(rows_hbm.at[q], rows_ref.at[q], row_sems.at[q])
-        weights = pltpu.make_async_copy(weights_hbm.at[q], weights_ref.at[q], weight_sems.at[q])
-        rows.start()
-        weights.start()
-        loads.append((rows, weights))
-
-    gate, up, back = 0.0, 0.0, 0.0
+        load = (
+            pltpu.make_async_copy(rows_hbm.at[q], rows_ref.at[q], sems.at[0, q]),
+            pltpu.make_async_copy(weights_hbm.at[q], weights_ref.at[q], sems.at[1, q]),
+        )
+        load[0].start()
+        load[1].start()
+        loads.append(load)
+    back_load = pltpu.make_async_copy(back_hbm, back_ref, sems.at[0, groups])
+    back_load.start()
+
+    gate, up = 0.0, 0.0
     for q, (rows, weights) in enumerate(loads):
         rows.wait()
-        packed[...] = rows_ref[q, :, 2 * quarter :].astype(F32).reshape(m, MAIN, LANES)
-        extra = [packed[:, j, :].astype(BF) for j in range(2 * pieces)]
+        packed[...] = rows_ref[q, :, quarter:].astype(F32).reshape(m, MAIN, LANES)
+        extra = [packed[:, j, :].astype(BF) for j in range(pieces)]
         token_rows = jnp.concatenate(
-            [rows_ref[q, :, :quarter], jnp.concatenate(extra[:pieces], axis=1)], axis=0
-        )
-        grad_rows = jnp.concatenate(
-            [rows_ref[q, :, quarter : 2 * quarter], jnp.concatenate(extra[pieces:], axis=1)], axis=0
+            [rows_ref[q, :, :quarter], jnp.concatenate(extra, axis=1)], axis=0
         )
         weights.wait()
         gate = gate + dot(token_rows, weights_ref[q, :, :ffw])
-        up = up + dot(token_rows, weights_ref[q, :, ffw : 2 * ffw])
-        back = back + dot(grad_rows, weights_ref[q, :, 2 * ffw :])
+        up = up + dot(token_rows, weights_ref[q, :, ffw:])
+    back_load.wait()
+    back = back_ref[...].astype(F32)
     sigmoid = 1.0 / (1.0 + jnp.exp(-gate))
     silu = gate * sigmoid
     gate_delta = (back * up * sigmoid * (1.0 + gate * (1.0 - sigmoid))).astype(BF)
@@ -140,19 +150,22 @@
         packed[:, j, :] = jnp.zeros((m, LANES), F32)
     for q in range(groups):
         out = dot(gate_delta, weights_ref[q, :, :ffw], CONTRACT_LAST)
-        out = out + dot(up_delta, weights_ref[q, :, ffw : 2 * ffw], CONTRACT_LAST)
-        back_ref[q, :, :quarter] = out[:n, :].astype(BF)
+        out = out + dot(up_delta, weights_ref[q, :, ffw:], CONTRACT_LAST)
+        out_back_ref[q, :, :quarter] = out[:n, :].astype(BF)
         for j in range(pieces):
             packed[:, j, :] = out[n:, j * LANES : (j + 1) * LANES]
-        back_ref[q, :, quarter:] = packed[...].reshape(n, LANES).astype(BF)
+        out_back_ref[q, :, quarter:] = packed[...].reshape(n, LANES).astype(BF)
 
 
 def row_blocks(rows_ref, packed, quarter, which):
     sources = rows_ref.shape[0] // MAIN
     pieces = quarter // LANES
-    packed[...] = rows_ref[:, 2 * quarter :].astype(F32).reshape(sources, MAIN, LANES)
+    packed[...] = (
+        rows_ref[:, quarter : quarter + LANES].astype(F32).reshape(sources, MAIN, LANES)
+    )
     n, m = rows_ref.shape[0] // 4, sources // 4
-    columns = slice(which * quarter, (which + 1) * quarter)
+    first = which * (quarter + LANES)
+    columns = slice(first, first + quarter)
     for r in range(4):
         extra = jnp.concatenate(
             [packed[r * m : (r + 1) * m, which * pieces + j, :] for j in range(pieces)], axis=1
@@ -209,8 +222,8 @@
 
     weights = kernel_call(
         pack_weights_kernel,
-        shape((quarter, 3 * ffw), BF),
-        (w_gate[0], w_up[0], w_down[0]),
+        shape((quarter, 2 * ffw), BF),
+        (w_gate[0], w_up[0]),
         0,
         vmem=60,
     )
@@ -230,20 +243,31 @@
         in_hbm=(2, 3),
     )
     rows = exchange(sent.reshape(experts, MAIN, -1), "ep").reshape(main, -1)
-    wide_rows = exchange(rows.reshape(groups, n, -1), "rep")
+    back_parts = kernel_call(
+        grad_products_kernel,
+        shape((main + experts, ffw), BF),
+        (rows, w_down[0]),
+        2 * (main + experts) * quarter * ffw,
+        (packed,),
+    )
+    token_rows, back_parts, weights = lax.optimization_barrier(
+        (rows[:, : quarter + LANES], back_parts, weights)
+    )
+    back_sums = lax.psum_scatter(back_parts, "rep", scatter_dimension=0, tiled=True)
+    wide_rows = exchange(token_rows.reshape(groups, n, -1), "rep")
     terms, back = kernel_call(
         expert_kernel,
         (shape((n + m, 3 * ffw), BF), shape((groups, n, quarter + LANES), BF)),
-        (wide_rows, weights),
-        10 * (n + m) * groups * quarter * ffw,
+        (wide_rows, weights, back_sums),
+        8 * (n + m) * groups * quarter * ffw,
         (
-            pltpu.VMEM((groups, n, 2 * quarter + LANES), BF),
-            pltpu.VMEM((groups, quarter, 3 * ffw), BF),
+            pltpu.VMEM((groups, n, quarter + LANES), BF),
+            pltpu.VMEM((groups, quarter, 2 * ffw), BF),
+            pltpu.VMEM((n + m, ffw), BF),
             pltpu.VMEM((m, MAIN, LANES), F32),
-            pltpu.SemaphoreType.DMA((groups,)),
-            pltpu.SemaphoreType.DMA((groups,)),
+            pltpu.SemaphoreType.DMA((2, groups + 1)),
         ),
-        in_hbm=(0, 1),
+        in_hbm=(0, 1, 2),
         vmem=60,
     )
     terms = lax.all_gather(terms, "rep", axis=0, tiled=True)

time: 220 us -> 220 us (level)
  waiting for transfers between devices: 25 us -> 34.4 us
  starting transfers between devices: 19.5 us -> 11.2 us
  local copies, waits for them, and re-layouts: 0.02 us -> 3.34 us
  blocking collectives: 133 us -> 130 us
    reduce_scatter x0 -> x1, waiting for transfers between devices: none -> 9.43 us  [body(): lax.psum_scatter(back_parts, 'rep', scatter_dimension=0, tiled=True)]
    all_to_all x1, starting transfers between devices: 19.5 us -> 11.1 us  [exchange(): return lax.all_to_all(blocks, axis, split_axis=0, concat_axis=0, tiled=True)]
    all_to_all x3, blocking collectives: 133 us -> 130 us  [exchange(): return lax.all_to_all(blocks, axis, split_axis=0, concat_axis=0, tiled=True)]
    pallas_call x6 -> x7, Pallas kernels: 27.9 us -> 27.1 us  [kernel_call(): pl.pallas_call(body, out_shape=out_shape, in_specs=[pl.BlockSpec(memory_s...]
  transfers between devices with their start and end apart: 3 -> 4, of which waited for: 2 -> 3; matrix products, arithmetic and copies ran while one was open for 0% -> 1% of each run, Pallas kernels for 6% -> 7%
where the time goes in v6:
time: 220 us; the launch traced here: 219 us
  blocking collectives  130 us (59%)
  waiting for transfers between devices  34.4 us (16%)
  Pallas kernels  27.1 us (12%)
  between operations  13.8 us (6%)
  starting transfers between devices  11.2 us (5%)
  local copies, waits for them, and re-layouts  3.34 us (2%)
    all_to_all x3, blocking collectives, exchange(): return lax.all_to_all(blocks, axis, split_axis=0, concat_axis=0, tiled=True)  130 us
    pallas_call x7, Pallas kernels, kernel_call(): pl.pallas_call(body, out_shape=out_shape, in_specs=[pl.BlockSpec(memory_s...  27.1 us
    all_gather x1, waiting for transfers between devices, body(): terms = lax.all_gather(terms, 'rep', axis=0, tiled=True)  18.6 us
    all_to_all x1, starting transfers between devices, exchange(): return lax.all_to_all(blocks, axis, split_axis=0, concat_axis=0, tiled=True)  11.1 us
    reduce_scatter x1, waiting for transfers between devices, body(): lax.psum_scatter(back_parts, 'rep', scatter_dimension=0, tiled=True)  9.43 us
    all_to_all x1, waiting for transfers between devices, exchange(): return lax.all_to_all(blocks, axis, split_axis=0, concat_axis=0, tiled=True)  6.35 us
  transfers between devices with their start and end apart: 4, of which 3 were waited for; matrix products, arithmetic and copies ran while one was open for 1% of the time, Pallas kernels for 7%

profile of v6, /device:TPU:1, one launch (start us, length us, event | category | flops | bytes accessed | tf_op | source)
XLA Modules:
  0.0 219.4 jit_solution(16537610867469276817)
XLA Ops:
  7.2 0.0 all-gather.6.cloned.1.call-start
  7.2 2.5 %shard_map.104 = bf16[512,1280]{1,0:T(8,128)(2,1)} custom-call(bf16[512,640]{1,0:T(8,128)(2,1)} %bitcast.25, bf16[512,640]{1,0:T(8,128)(2,1)} %bitcast.26), custom_call_target="tpu_custom_call" | custom-call | bytes 2621440 | tf_op jit(solution)/shard_map/pallas_call | solution.py:24
  9.7 0.0 copy-start.2
  9.7 0.0 copy-start.3
  9.7 0.0 copy-start.4
  9.7 0.0 copy-start.5
  9.7 0.0 all-gather.6.cloned.1.call-update
  9.7 0.0 reduce-scatter.2.cloned.1.call-start
  9.8 0.8 copy-done.2
  10.6 0.1 copy-done.3
  10.6 0.0 copy-done.4
  10.6 0.0 copy-done.5
  10.6 1.8 shard_map.102
  12.5 75.0 %all_to_all.20 = bf16[128,8,1152]{2,1,0:T(8,128)(2,1)S(1)} all-to-all(bf16[128,8,1152]{2,1,0:T(8,128)(2,1)S(1)} %bitcast.18), channel_id=1, replica_groups=mesh['rep'=4,'ep'=128] {'ep'}, dimensions={0} | all-to-all | bytes 4718592 | tf_op jit(solution)/shard_map/all_to_all | solution.py:210
  87.5 0.0 copy-start.1
  87.5 1.3 slice.4
  88.8 0.0 copy-done.1
  88.8 1.7 shard_map.103
  90.5 0.0 copy-start
  90.5 1.2 copy-done
  91.6 0.0 all-gather.6.cloned.1.call-done
  91.6 0.0 reduce-scatter.2.cloned.1.call-update
  91.7 0.0 all-gather.4.cloned.1.call-start
  91.7 25.9 %all_to_all.21.rows_hbm = bf16[4,256,640]{2,1,0:T(8,128)(2,1)} all-to-all(bf16[4,256,640]{2,1,0:T(8,128)(2,1)} %bitcast.24), channel_id=1, replica_groups=mesh['rep'=4,'ep'=128] {'rep'}, dimensions={0} | all-to-all | bytes 2621440 | tf_op jit(solution)/shard_map/all_to_all | solution.py:210
  117.6 9.4 %reduce-scatter.2.cloned.1.call-done.back_hbm = bf16[288,640]{1,0:T(8,128)(2,1)} async-done(((bf16[1152,640]{1,0:T(8,128)(2,1)}), bf16[288,640]{1,0:T(8,128)(2,1)}) %reduce-scatter.2.cloned.1.call-update) | async-done | bytes 368656 | tf_op jit(solution)/shard_map/reduce_scatter | solution.py:256
  127.0 7.6 %shard_map.105 = (bf16[288,1920]{1,0:T(8,128)(2,1)}, bf16[4,256,640]{2,1,0:T(8,128)(2,1)}) custom-call(bf16[4,256,640]{2,1,0:T(8,128)(2,1)} %all_to_all.21.rows_hbm, bf16[4,512,1280]{2,1,0:T(8,128)(2,1)} %bitcast.28, bf16[288,640]{1,0:T(8,128)(2,1)} %reduce-scatter.2.cloned.1.call-done.back_hbm), custom_call_target="tpu_custom_call" | custom-call | flops 3019898880 | bytes 9338880 | tf_op jit(solution)/shard_map/pallas_call | solution.py:24
  134.6 0.0 all-gather.4.cloned.1.call-update
  134.7 28.7 %all_to_all.22 = bf16[4,256,640]{2,1,0:T(8,128)(2,1)} all-to-all(bf16[4,256,640]{2,1,0:T(8,128)(2,1)} %get-tuple-element.22), channel_id=1, replica_groups=mesh['rep'=4,'ep'=128] {'rep'}, dimensions={0} | all-to-all | bytes 2621440 | tf_op jit(solution)/shard_map/all_to_all | solution.py:210
  163.3 11.1 %all-to-all-start.3 = ((bf16[128,8,640]{2,1,0:T(8,128)(2,1)}), bf16[128,8,640]{2,1,0:T(8,128)(2,1)}, u32[]{:S(2)}, u32[]{:S(2)}) async-start(bf16[128,8,640]{2,1,0:T(8,128)(2,1)} %bitcast.23), calls=%async_computation.4 | async-start | bytes 2621440 | tf_op jit(solution)/shard_map/all_to_all | solution.py:210
  174.4 18.6 %all-gather.4.cloned.1.call-done.terms_ref = bf16[1152,1920]{1,0:T(8,128)(2,1)} async-done(((bf16[288,1920]{1,0:T(8,128)(2,1)}), bf16[1152,1920]{1,0:T(8,128)(2,1)}) %all-gather.4.cloned.1.call-update) | async-done | bytes 4423696 | tf_op jit(solution)/shard_map/all_gather | solution.py:273
  193.0 4.7 %shard_map.107 = bf16[640,512]{1,0:T(8,128)(2,1)} custom-call(bf16[1024,1152]{1,0:T(8,128)(2,1)S(1)} %bitcast.16, bf16[1152,1920]{1,0:T(8,128)(2,1)} %all-gather.4.cloned.1.call-done.terms_ref), custom_call_target="tpu_custom_call" | custom-call | flops 754974720 | bytes 7438336 | tf_op jit(solution)/shard_map/pallas_call | solution.py:24
  197.7 6.1 %shard_map.106 = (bf16[512,640]{1,0:T(8,128)(2,1)}, bf16[512,640]{1,0:T(8,128)(2,1)}) custom-call(bf16[1024,1152]{1,0:T(8,128)(2,1)S(1)} %bitcast.17, bf16[1152,1920]{1,0:T(8,128)(2,1)} %all-gather.4.cloned.1.call-done.terms_ref), custom_call_target="tpu_custom_call" | custom-call | flops 1509949440 | bytes 8093696 | tf_op jit(solution)/shard_map/pallas_call | solution.py:24
  203.8 6.4 %all-to-all-done.3 = bf16[128,8,640]{2,1,0:T(8,128)(2,1)} async-done(((bf16[128,8,640]{2,1,0:T(8,128)(2,1)}), bf16[128,8,640]{2,1,0:T(8,128)(2,1)}, u32[]{:S(2)}, u32[]{:S(2)}) %all-to-all-start.3) | async-done | bytes 1310752 | tf_op jit(solution)/shard_map/all_to_all | solution.py:210
  210.2 2.7 %shard_map.108 = bf16[128,512]{1,0:T(8,128)(2,1)} custom-call(s32[8,128]{1,0:T(8,128)S(1)} %bitcast.21, bf16[1024,640]{1,0:T(8,128)(2,1)} %bitcast.10.rows_ref), custom_call_target="tpu_custom_call" | custom-call | flops 134217728 | bytes 1445888 | tf_op jit(solution)/shard_map/pallas_call | solution.py:24
Async XLA Ops:
  7.2 84.5 %all-gather.6.cloned.1.call-start = ((), (), s32[]{:S(2)}) async-start(), calls=%async_computation.7 | async-start | bytes 6553600 | tf_op jit(solution)/shard_map/all_gather | solution.py:230
  9.7 0.9 copy-start.2
  9.7 1.0 copy-start.3
  9.7 1.0 copy-start.4
  9.7 1.0 copy-start.5
  9.7 117.3 %reduce-scatter.2.cloned.1.call-start = ((), (), s32[]{:S(2)}) async-start(), calls=%async_computation.5 | async-start | bytes 1843200 | tf_op jit(solution)/shard_map/reduce_scatter | solution.py:256
  87.5 1.3 copy-start.1
  90.5 1.2 copy-start
  91.7 101.3 %all-gather.4.cloned.1.call-start = ((), (), s32[]{:S(2)}) async-start(), calls=%async_computation.6 | async-start | bytes 5529600 | tf_op jit(solution)/shard_map/all_gather | solution.py:273
  163.3 46.8 %all-to-all-start.3 = ((bf16[128,8,640]{2,1,0:T(8,128)(2,1)}), bf16[128,8,640]{2,1,0:T(8,128)(2,1)}, u32[]{:S(2)}, u32[]{:S(2)}) async-start(bf16[128,8,640]{2,1,0:T(8,128)(2,1)} %bitcast.23), calls=%async_computation.4 | async-start | bytes 2621440 | tf_op jit(solution)/shard_map/all_to_all | solution.py:210
Sparse Core Ops, SparseCore 0:
  10.1 67.7 all-gather.5
  91.8 35.1 reduce-scatter.1
  134.8 58.1 all-gather.3

commit v7 on v6

--- a/solution.py
+++ b/solution.py
@@ -106,8 +106,8 @@
         out_ref[at + n : at + n + m, :] = dot(extra, down_ref[...], CONTRACT_LAST).astype(BF)
 
 
-def expert_kernel(
-    rows_hbm, weights_hbm, back_hbm, terms_ref, out_back_ref, rows_ref, weights_ref, back_ref, packed, sems
+def token_products_kernel(
+    rows_hbm, weights_hbm, gate_ref, up_ref, rows_ref, weights_ref, packed, sems
 ):
     groups, n, _ = rows_ref.shape
     quarter = weights_ref.shape[1]
@@ -123,9 +123,6 @@
         load[0].start()
         load[1].start()
         loads.append(load)
-    back_load = pltpu.make_async_copy(back_hbm, back_ref, sems.at[0, groups])
-    back_load.start()
-
     gate, up = 0.0, 0.0
     for q, (rows, weights) in enumerate(loads):
         rows.wait()
@@ -137,8 +134,34 @@
         weights.wait()
         gate = gate + dot(token_rows, weights_ref[q, :, :ffw])
         up = up + dot(token_rows, weights_ref[q, :, ffw:])
-    back_load.wait()
-    back = back_ref[...].astype(F32)
+    gate_ref[...] = gate
+    up_ref[...] = up
+
+
+def expert_kernel(
+    weights_hbm, gate_hbm, up_hbm, back_hbm, terms_ref, out_back_ref, *scratch
+):
+    weights_ref, gate_ref, up_ref, back_ref, packed, sems = scratch
+    groups, n, _ = out_back_ref.shape
+    quarter = weights_ref.shape[1]
+    ffw = weights_ref.shape[2] // 2
+    m = n // MAIN
+    pieces = quarter // LANES
+    small = [
+        pltpu.make_async_copy(src, dst, sems.at[1, i])
+        for i, (src, dst) in enumerate(
+            ((gate_hbm, gate_ref), (up_hbm, up_ref), (back_hbm, back_ref))
+        )
+    ]
+    loads = [
+        pltpu.make_async_copy(weights_hbm.at[q], weights_ref.at[q], sems.at[0, q])
+        for q in range(groups)
+    ]
+    for load in small + loads:
+        load.start()
+    for load in small:
+        load.wait()
+    gate, up, back = gate_ref[...], up_ref[...], back_ref[...].astype(F32)
     sigmoid = 1.0 / (1.0 + jnp.exp(-gate))
     silu = gate * sigmoid
     gate_delta = (back * up * sigmoid * (1.0 + gate * (1.0 - sigmoid))).astype(BF)
@@ -149,6 +172,7 @@
     for j in range(pieces, MAIN):
         packed[:, j, :] = jnp.zeros((m, LANES), F32)
     for q in range(groups):
+        loads[q].wait()
         out = dot(gate_delta, weights_ref[q, :, :ffw], CONTRACT_LAST)
         out = out + dot(up_delta, weights_ref[q, :, ffw:], CONTRACT_LAST)
         out_back_ref[q, :, :quarter] = out[:n, :].astype(BF)
@@ -192,12 +216,15 @@
     down_ref[...] = total.astype(BF)
 
 
-def combine_kernel(ids_ref, rows_ref, out_ref, packed):
+def combine_kernel(ids_ref, rows_hbm, out_ref, packed, rows_ref, sem):
+    load = pltpu.make_async_copy(rows_hbm, rows_ref, sem)
+    load.start()
     experts = rows_ref.shape[0] // MAIN
     quarter = out_ref.shape[1]
     slot, _ = routing(ids_ref, experts)
     here = jnp.where(main_slots(slot), 1.0, 0.0).astype(BF)
     last = jnp.where(slot == float(MAIN), 1.0, 0.0).astype(BF)
+    load.wait()
     packed[...] = rows_ref[:, quarter:].astype(F32).reshape(experts, MAIN, LANES)
     total = dot(here, rows_ref[:, :quarter], CONTRACT_FIRST)
     for j in range(quarter // LANES):
@@ -255,19 +282,34 @@
     )
     back_sums = lax.psum_scatter(back_parts, "rep", scatter_dimension=0, tiled=True)
     wide_rows = exchange(token_rows.reshape(groups, n, -1), "rep")
+    gate, up = kernel_call(
+        token_products_kernel,
+        (shape((n + m, ffw), F32), shape((n + m, ffw), F32)),
+        (wide_rows, weights),
+        4 * (n + m) * groups * quarter * ffw,
+        (
+            pltpu.VMEM((groups, n, quarter + LANES), BF),
+            pltpu.VMEM((groups, quarter, 2 * ffw), BF),
+            pltpu.VMEM((m, MAIN, LANES), F32),
+            pltpu.SemaphoreType.DMA((2, groups)),
+        ),
+        in_hbm=(0, 1),
+        vmem=60,
+    )
     terms, back = kernel_call(
         expert_kernel,
         (shape((n + m, 3 * ffw), BF), shape((groups, n, quarter + LANES), BF)),
-        (wide_rows, weights, back_sums),
-        8 * (n + m) * groups * quarter * ffw,
+        (weights, gate, up, back_sums),
+        4 * (n + m) * groups * quarter * ffw,
         (
-            pltpu.VMEM((groups, n, quarter + LANES), BF),
             pltpu.VMEM((groups, quarter, 2 * ffw), BF),
+            pltpu.VMEM((n + m, ffw), F32),
+            pltpu.VMEM((n + m, ffw), F32),
             pltpu.VMEM((n + m, ffw), BF),
             pltpu.VMEM((m, MAIN, LANES), F32),
-            pltpu.SemaphoreType.DMA((2, groups + 1)),
+            pltpu.SemaphoreType.DMA((2, groups)),
         ),
-        in_hbm=(0, 1, 2),
+        in_hbm=(0, 1, 2, 3),
         vmem=60,
     )
     terms = lax.all_gather(terms, "rep", axis=0, tiled=True)
@@ -295,7 +337,9 @@
         shape((count, quarter), BF),
         (ids, returned),
         2 * main * count * quarter,
-        (packed,),
+        (packed, pltpu.VMEM((main, quarter + LANES), BF), pltpu.SemaphoreType.DMA),
+        in_hbm=(1,),
+        vmem=60,
     )
     return token_grad, grad_gate[None], grad_up[None], grad_down[None]
 

time: 220 us -> 223 us (1.014)
  starting transfers between devices: 11.2 us -> 24.8 us
  blocking collectives: 130 us -> 120 us
  waiting for transfers between devices: 34.4 us -> 29.1 us
  Pallas kernels: 27.1 us -> 31.4 us
    all_to_all x1, starting transfers between devices: 11.1 us -> 24.6 us  [exchange(): return lax.all_to_all(blocks, axis, split_axis=0, concat_axis=0, tiled=True)]
    all_to_all x3, blocking collectives: 130 us -> 120 us  [exchange(): return lax.all_to_all(blocks, axis, split_axis=0, concat_axis=0, tiled=True)]
    reduce_scatter x1, waiting for transfers between devices: 9.43 us -> 4.07 us  [body(): lax.psum_scatter(back_parts, 'rep', scatter_dimension=0, tiled=True)]
    pallas_call x7 -> x8, Pallas kernels: 27.1 us -> 31.4 us  [kernel_call(): pl.pallas_call(body, out_shape=out_shape, in_specs=[pl.BlockSpec(memory_s...]
    all_to_all x1, waiting for transfers between devices: 6.35 us -> 9.95 us  [exchange(): return lax.all_to_all(blocks, axis, split_axis=0, concat_axis=0, tiled=True)]
    all_gather x1, waiting for transfers between devices: 18.6 us -> 15 us  [body(): terms = lax.all_gather(terms, 'rep', axis=0, tiled=True)]
  transfers between devices with their start and end apart: 4 -> 4, of which waited for: 3 -> 3; matrix products, arithmetic and copies ran while one was open for 1% -> 1% of each run, Pallas kernels for 7% -> 9%
where the time goes in v7:
time: 223 us; the launch traced here: 222 us
  blocking collectives  120 us (54%)
  Pallas kernels  31.4 us (14%)
  waiting for transfers between devices  29.1 us (13%)
  starting transfers between devices  24.8 us (11%)
  between operations  13.8 us (6%)
  local copies, waits for them, and re-layouts  3.32 us (1%)
    all_to_all x3, blocking collectives, exchange(): return lax.all_to_all(blocks, axis, split_axis=0, concat_axis=0, tiled=True)  120 us
    pallas_call x8, Pallas kernels, kernel_call(): pl.pallas_call(body, out_shape=out_shape, in_specs=[pl.BlockSpec(memory_s...  31.4 us
    all_to_all x1, starting transfers between devices, exchange(): return lax.all_to_all(blocks, axis, split_axis=0, concat_axis=0, tiled=True)  24.6 us
    all_gather x1, waiting for transfers between devices, body(): terms = lax.all_gather(terms, 'rep', axis=0, tiled=True)  15 us
    all_to_all x1, waiting for transfers between devices, exchange(): return lax.all_to_all(blocks, axis, split_axis=0, concat_axis=0, tiled=True)  9.95 us
  transfers between devices with their start and end apart: 4, of which 3 were waited for; matrix products, arithmetic and copies ran while one was open for 1% of the time, Pallas kernels for 9%

profile of v7, /device:TPU:1, one launch (start us, length us, event | category | flops | bytes accessed | tf_op | source)
XLA Modules:
  0.0 221.9 jit_solution(5055950880424004885)
XLA Ops:
  7.2 0.0 all-gather.6.cloned.1.call-start
  7.2 2.6 %shard_map.104 = bf16[512,1280]{1,0:T(8,128)(2,1)} custom-call(bf16[512,640]{1,0:T(8,128)(2,1)} %bitcast.27, bf16[512,640]{1,0:T(8,128)(2,1)} %bitcast.28), custom_call_target="tpu_custom_call" | custom-call | bytes 2621440 | tf_op jit(solution)/shard_map/pallas_call | solution.py:24
  9.8 0.0 copy-start.2
  9.8 0.0 copy-start.3
  9.8 0.0 copy-start.4
  9.8 0.0 copy-start.5
  9.8 0.0 all-gather.6.cloned.1.call-update
  9.8 0.0 reduce-scatter.2.cloned.1.call-start
  9.9 0.8 copy-done.2
  10.7 0.1 copy-done.3
  10.7 0.0 copy-done.4
  10.7 0.0 copy-done.5
  10.7 1.8 shard_map.102
  12.6 75.0 %all_to_all.20 = bf16[128,8,1152]{2,1,0:T(8,128)(2,1)S(1)} all-to-all(bf16[128,8,1152]{2,1,0:T(8,128)(2,1)S(1)} %bitcast.18), channel_id=1, replica_groups=mesh['rep'=4,'ep'=128] {'ep'}, dimensions={0} | all-to-all | bytes 4718592 | tf_op jit(solution)/shard_map/all_to_all | solution.py:237
  87.6 0.0 copy-start.1
  87.6 1.2 slice.4
  88.7 0.1 copy-done.1
  88.8 1.7 shard_map.103
  90.5 0.0 copy-start
  90.5 1.2 copy-done
  91.7 0.0 all-gather.6.cloned.1.call-done
  91.7 0.0 reduce-scatter.2.cloned.1.call-update
  91.7 0.0 all-gather.4.cloned.1.call-start
  91.8 26.0 %all_to_all.21.rows_hbm = bf16[4,256,640]{2,1,0:T(8,128)(2,1)} all-to-all(bf16[4,256,640]{2,1,0:T(8,128)(2,1)} %bitcast.26), channel_id=1, replica_groups=mesh['rep'=4,'ep'=128] {'rep'}, dimensions={0} | all-to-all | bytes 2621440 | tf_op jit(solution)/shard_map/all_to_all | solution.py:237
  117.7 5.3 %shard_map.105 = (f32[288,640]{1,0:T(8,128)}, f32[288,640]{1,0:T(8,128)}) custom-call(bf16[4,256,640]{2,1,0:T(8,128)(2,1)} %all_to_all.21.rows_hbm, bf16[4,512,1280]{2,1,0:T(8,128)(2,1)} %bitcast.23), custom_call_target="tpu_custom_call" | custom-call | flops 1509949440 | bytes 8028160 | tf_op jit(solution)/shard_map/pallas_call | solution.py:24
  123.0 4.1 %reduce-scatter.2.cloned.1.call-done.back_hbm = bf16[288,640]{1,0:T(8,128)(2,1)} async-done(((bf16[1152,640]{1,0:T(8,128)(2,1)}), bf16[288,640]{1,0:T(8,128)(2,1)}) %reduce-scatter.2.cloned.1.call-update) | async-done | bytes 368656 | tf_op jit(solution)/shard_map/reduce_scatter | solution.py:283
  127.1 6.0 %shard_map.106 = (bf16[288,1920]{1,0:T(8,128)(2,1)}, bf16[4,256,640]{2,1,0:T(8,128)(2,1)}) custom-call(bf16[4,512,1280]{2,1,0:T(8,128)(2,1)} %bitcast.24, f32[288,640]{1,0:T(8,128)} %get-tuple-element.19.gate_hbm, f32[288,640]{1,0:T(8,128)} %get-tuple-element.20.up_hbm, bf16[288,640]{1,0:T(8,128)(2,1)} %reduce-scatter.2.cloned.1.call-done.back_hbm), custom_call_target="tpu_custom_call" | custom-call | flops 1509949440 | bytes 9502720 | tf_op jit(solution)/shard_map/pallas_call | solution.py:24
  133.1 0.0 all-gather.4.cloned.1.call-update
  133.1 18.7 %all_to_all.22 = bf16[4,256,640]{2,1,0:T(8,128)(2,1)} all-to-all(bf16[4,256,640]{2,1,0:T(8,128)(2,1)} %get-tuple-element.26), channel_id=1, replica_groups=mesh['rep'=4,'ep'=128] {'rep'}, dimensions={0} | all-to-all | bytes 2621440 | tf_op jit(solution)/shard_map/all_to_all | solution.py:237
  151.8 24.6 %all-to-all-start.3 = ((bf16[128,8,640]{2,1,0:T(8,128)(2,1)}), bf16[128,8,640]{2,1,0:T(8,128)(2,1)}, u32[]{:S(2)}, u32[]{:S(2)}) async-start(bf16[128,8,640]{2,1,0:T(8,128)(2,1)} %bitcast.25), calls=%async_computation.4 | async-start | bytes 2621440 | tf_op jit(solution)/shard_map/all_to_all | solution.py:237
  176.4 15.0 %all-gather.4.cloned.1.call-done.terms_ref = bf16[1152,1920]{1,0:T(8,128)(2,1)} async-done(((bf16[288,1920]{1,0:T(8,128)(2,1)}), bf16[1152,1920]{1,0:T(8,128)(2,1)}) %all-gather.4.cloned.1.call-update) | async-done | bytes 4423696 | tf_op jit(solution)/shard_map/all_gather | solution.py:315
  191.4 4.7 %shard_map.108 = bf16[640,512]{1,0:T(8,128)(2,1)} custom-call(bf16[1024,1152]{1,0:T(8,128)(2,1)S(1)} %bitcast.16, bf16[1152,1920]{1,0:T(8,128)(2,1)} %all-gather.4.cloned.1.call-done.terms_ref), custom_call_target="tpu_custom_call" | custom-call | flops 754974720 | bytes 7438336 | tf_op jit(solution)/shard_map/pallas_call | solution.py:24
  196.1 6.1 %shard_map.107 = (bf16[512,640]{1,0:T(8,128)(2,1)}, bf16[512,640]{1,0:T(8,128)(2,1)}) custom-call(bf16[1024,1152]{1,0:T(8,128)(2,1)S(1)} %bitcast.17, bf16[1152,1920]{1,0:T(8,128)(2,1)} %all-gather.4.cloned.1.call-done.terms_ref), custom_call_target="tpu_custom_call" | custom-call | flops 1509949440 | bytes 8093696 | tf_op jit(solution)/shard_map/pallas_call | solution.py:24
  202.2 9.9 %all-to-all-done.3 = bf16[128,8,640]{2,1,0:T(8,128)(2,1)} async-done(((bf16[128,8,640]{2,1,0:T(8,128)(2,1)}), bf16[128,8,640]{2,1,0:T(8,128)(2,1)}, u32[]{:S(2)}, u32[]{:S(2)}) %all-to-all-start.3) | async-done | bytes 1310752 | tf_op jit(solution)/shard_map/all_to_all | solution.py:237
  212.2 3.2 %shard_map.109 = bf16[128,512]{1,0:T(8,128)(2,1)} custom-call(s32[8,128]{1,0:T(8,128)} %bitcast.20, bf16[1024,640]{1,0:T(8,128)(2,1)} %bitcast.10.rows_hbm), custom_call_target="tpu_custom_call" | custom-call | flops 134217728 | bytes 1445888 | tf_op jit(solution)/shard_map/pallas_call | solution.py:24
Async XLA Ops:
  7.2 84.5 %all-gather.6.cloned.1.call-start = ((), (), s32[]{:S(2)}) async-start(), calls=%async_computation.7 | async-start | bytes 6553600 | tf_op jit(solution)/shard_map/all_gather | solution.py:257
  9.8 0.9 copy-start.2
  9.8 1.0 copy-start.3
  9.8 1.0 copy-start.4
  9.8 1.0 copy-start.5
  9.8 117.3 %reduce-scatter.2.cloned.1.call-start = ((), (), s32[]{:S(2)}) async-start(), calls=%async_computation.5 | async-start | bytes 1843200 | tf_op jit(solution)/shard_map/reduce_scatter | solution.py:283
  87.6 1.3 copy-start.1
  90.5 1.2 copy-start
  91.7 99.7 %all-gather.4.cloned.1.call-start = ((), (), s32[]{:S(2)}) async-start(), calls=%async_computation.6 | async-start | bytes 5529600 | tf_op jit(solution)/shard_map/all_gather | solution.py:315
  151.8 60.4 %all-to-all-start.3 = ((bf16[128,8,640]{2,1,0:T(8,128)(2,1)}), bf16[128,8,640]{2,1,0:T(8,128)(2,1)}, u32[]{:S(2)}, u32[]{:S(2)}) async-start(bf16[128,8,640]{2,1,0:T(8,128)(2,1)} %bitcast.25), calls=%async_computation.4 | async-start | bytes 2621440 | tf_op jit(solution)/shard_map/all_to_all | solution.py:237
Sparse Core Ops, SparseCore 0:
  10.1 67.7 all-gather.5
  91.8 35.2 reduce-scatter.1
  133.2 58.1 all-gather.3

commit v8 on v7

--- a/solution.py
+++ b/solution.py
@@ -17,7 +17,7 @@
     return lax.dot_general(a, b, dims, preferred_element_type=F32)
 
 
-def kernel_call(body, out_shape, args, flops, scratch=(), in_hbm=(), vmem=48):
+def kernel_call(body, out_shape, args, flops, scratch=(), in_hbm=(), in_smem=(), vmem=48):
     moved = sum(a.size * a.dtype.itemsize for a in args)
     outs = out_shape if isinstance(out_shape, tuple) else (out_shape,)
     moved += sum(o.size * o.dtype.itemsize for o in outs)
@@ -25,7 +25,9 @@
         body,
         out_shape=out_shape,
         in_specs=[
-            pl.BlockSpec(memory_space=pl.ANY if i in in_hbm else pltpu.VMEM)
+            pl.BlockSpec(
+                memory_space=pl.ANY if i in in_hbm else pltpu.SMEM if i in in_smem else pltpu.VMEM
+            )
             for i in range(len(args))
         ],
         out_specs=jax.tree.map(lambda _: pl.BlockSpec(memory_space=pltpu.VMEM), out_shape),
@@ -99,16 +101,24 @@
     )
 
 
-def grad_products_kernel(rows_ref, down_ref, out_ref, packed):
+def grad_products_kernel(rank_ref, rows_ref, down_ref, out_ref, *refs):
+    *token_refs, packed = refs
     quarter = down_ref.shape[1]
+    groups, count = len(token_refs), token_refs[0].shape[0]
+    for k, token_ref in enumerate(token_refs):
+        first = pl.multiple_of(away(rank_ref, k, groups) * count, count)
+        token_ref[...] = rows_ref[pl.ds(first, count), : quarter + LANES]
     for at, n, m, rows, extra in row_blocks(rows_ref, packed, quarter, 1):
         out_ref[at : at + n, :] = dot(rows, down_ref[...], CONTRACT_LAST).astype(BF)
         out_ref[at + n : at + n + m, :] = dot(extra, down_ref[...], CONTRACT_LAST).astype(BF)
 
 
-def token_products_kernel(
-    rows_hbm, weights_hbm, gate_ref, up_ref, rows_ref, weights_ref, packed, sems
-):
+def away(rank_ref, k, groups):
+    return lax.rem(rank_ref[0] + (k + groups), groups)
+
+
+def token_products_kernel(rank_ref, weights_hbm, *refs):
+    *rows_hbm, gate_ref, up_ref, rows_ref, weights_ref, packed, sems = refs
     groups, n, _ = rows_ref.shape
     quarter = weights_ref.shape[1]
     ffw = weights_ref.shape[2] // 2
@@ -117,8 +127,10 @@
     loads = []
     for q in range(groups):
         load = (
-            pltpu.make_async_copy(rows_hbm.at[q], rows_ref.at[q], sems.at[0, q]),
-            pltpu.make_async_copy(weights_hbm.at[q], weights_ref.at[q], sems.at[1, q]),
+            pltpu.make_async_copy(rows_hbm[q], rows_ref.at[q], sems.at[0, q]),
+            pltpu.make_async_copy(
+                weights_hbm.at[away(rank_ref, -q, groups)], weights_ref.at[q], sems.at[1, q]
+            ),
         )
         load[0].start()
         load[1].start()
@@ -138,11 +150,15 @@
     up_ref[...] = up
 
 
-def expert_kernel(
-    weights_hbm, gate_hbm, up_hbm, back_hbm, terms_ref, out_back_ref, *scratch
-):
-    weights_ref, gate_ref, up_ref, back_ref, packed, sems = scratch
-    groups, n, _ = out_back_ref.shape
+def place_kernel(rank_ref, *refs):
+    *blocks, out_ref = refs
+    for k, block in enumerate(blocks):
+        out_ref[away(rank_ref, -k, len(blocks))] = block[...]
+
+
+def expert_kernel(rank_ref, weights_hbm, gate_hbm, up_hbm, back_hbm, terms_ref, *refs):
+    *out_back_refs, weights_ref, gate_ref, up_ref, back_ref, packed, sems = refs
+    groups, n = len(out_back_refs), out_back_refs[0].shape[0]
     quarter = weights_ref.shape[1]
     ffw = weights_ref.shape[2] // 2
     m = n // MAIN
@@ -154,7 +170,9 @@
         )
     ]
     loads = [
-        pltpu.make_async_copy(weights_hbm.at[q], weights_ref.at[q], sems.at[0, q])
+        pltpu.make_async_copy(
+            weights_hbm.at[away(rank_ref, q, groups)], weights_ref.at[q], sems.at[0, q]
+        )
         for q in range(groups)
     ]
     for load in small + loads:
@@ -175,10 +193,10 @@
         loads[q].wait()
         out = dot(gate_delta, weights_ref[q, :, :ffw], CONTRACT_LAST)
         out = out + dot(up_delta, weights_ref[q, :, ffw:], CONTRACT_LAST)
-        out_back_ref[q, :, :quarter] = out[:n, :].astype(BF)
+        out_back_refs[q][:, :quarter] = out[:n, :].astype(BF)
         for j in range(pieces):
             packed[:, j, :] = out[n:, j * LANES : (j + 1) * LANES]
-        out_back_ref[q, :, quarter:] = packed[...].reshape(n, LANES).astype(BF)
+        out_back_refs[q][:, quarter:] = packed[...].reshape(n, LANES).astype(BF)
 
 
 def row_blocks(rows_ref, packed, quarter, which):
@@ -216,15 +234,12 @@
     down_ref[...] = total.astype(BF)
 
 
-def combine_kernel(ids_ref, rows_hbm, out_ref, packed, rows_ref, sem):
-    load = pltpu.make_async_copy(rows_hbm, rows_ref, sem)
-    load.start()
+def combine_kernel(ids_ref, rows_ref, out_ref, packed):
     experts = rows_ref.shape[0] // MAIN
     quarter = out_ref.shape[1]
     slot, _ = routing(ids_ref, experts)
     here = jnp.where(main_slots(slot), 1.0, 0.0).astype(BF)
     last = jnp.where(slot == float(MAIN), 1.0, 0.0).astype(BF)
-    load.wait()
     packed[...] = rows_ref[:, quarter:].astype(F32).reshape(experts, MAIN, LANES)
     total = dot(here, rows_ref[:, :quarter], CONTRACT_FIRST)
     for j in range(quarter // LANES):
@@ -235,6 +250,14 @@
 
 def exchange(blocks, axis):
     return lax.all_to_all(blocks, axis, split_axis=0, concat_axis=0, tiled=True)
+
+
+def swap(blocks, axis):
+    groups = len(blocks)
+    return blocks[:1] + [
+        lax.ppermute(blocks[k], axis, [(i, (i + k) % groups) for i in range(groups)])
+        for k in range(1, groups)
+    ]
 
 
 def body(tokens, out_grad, expert_ids, route_weight, w_gate, w_up, w_down):
@@ -255,7 +278,8 @@
         vmem=60,
     )
     weights = lax.all_gather(weights, "rep", axis=0)
-    ids = expert_ids.T
+    at_rank = lax.axis_index("rep").astype(jnp.int32).reshape(1)
+    ids, at_rank = lax.optimization_barrier((expert_ids.T, at_rank))
     sent = kernel_call(
         dispatch_kernel,
         shape((main, 2 * quarter + LANES), BF),
@@ -270,22 +294,21 @@
         in_hbm=(2, 3),
     )
     rows = exchange(sent.reshape(experts, MAIN, -1), "ep").reshape(main, -1)
-    back_parts = kernel_call(
+    back_parts, *token_rows = kernel_call(
         grad_products_kernel,
-        shape((main + experts, ffw), BF),
-        (rows, w_down[0]),
+        (shape((main + experts, ffw), BF),) + (shape((n, quarter + LANES), BF),) * groups,
+        (at_rank, rows, w_down[0]),
         2 * (main + experts) * quarter * ffw,
         (packed,),
-    )
-    token_rows, back_parts, weights = lax.optimization_barrier(
-        (rows[:, : quarter + LANES], back_parts, weights)
-    )
+        in_smem=(0,),
+    )
+    back_parts, weights = lax.optimization_barrier((back_parts, weights))
     back_sums = lax.psum_scatter(back_parts, "rep", scatter_dimension=0, tiled=True)
-    wide_rows = exchange(token_rows.reshape(groups, n, -1), "rep")
+    wide_rows = swap(token_rows, "rep")
     gate, up = kernel_call(
         token_products_kernel,
         (shape((n + m, ffw), F32), shape((n + m, ffw), F32)),
-        (wide_rows, weights),
+        (at_rank, weights, *wide_rows),
         4 * (n + m) * groups * quarter * ffw,
         (
             pltpu.VMEM((groups, n, quarter + LANES), BF),
@@ -293,13 +316,14 @@
             pltpu.VMEM((m, MAIN, LANES), F32),
             pltpu.SemaphoreType.DMA((2, groups)),
         ),
-        in_hbm=(0, 1),
+        in_smem=(0,),
+        in_hbm=range(1, 2 + groups),
         vmem=60,
     )
-    terms, back = kernel_call(
+    terms, *back = kernel_call(
         expert_kernel,
-        (shape((n + m, 3 * ffw), BF), shape((groups, n, quarter + LANES), BF)),
-        (weights, gate, up, back_sums),
+        (shape((n + m, 3 * ffw), BF),) + (shape((n, quarter + LANES), BF),) * groups,
+        (at_rank, weights, gate, up, back_sums),
         4 * (n + m) * groups * quarter * ffw,
         (
             pltpu.VMEM((groups, quarter, 2 * ffw), BF),
@@ -309,11 +333,18 @@
             pltpu.VMEM((m, MAIN, LANES), F32),
             pltpu.SemaphoreType.DMA((2, groups)),
         ),
-        in_hbm=(0, 1, 2, 3),
+        in_smem=(0,),
+        in_hbm=(1, 2, 3, 4),
         vmem=60,
     )
     terms = lax.all_gather(terms, "rep", axis=0, tiled=True)
-    back = exchange(back, "rep")
+    back = kernel_call(
+        place_kernel,
+        shape((groups, n, quarter + LANES), BF),
+        (at_rank, *swap(back, "rep")),
+        0,
+        in_smem=(0,),
+    )
     returned = exchange(back.reshape(experts, MAIN, -1), "ep").reshape(main, -1)
     grad_gate, grad_up = kernel_call(
         token_weights_kernel,
@@ -337,9 +368,7 @@
         shape((count, quarter), BF),
         (ids, returned),
         2 * main * count * quarter,
-        (packed, pltpu.VMEM((main, quarter + LANES), BF), pltpu.SemaphoreType.DMA),
-        in_hbm=(1,),
-        vmem=60,
+        (packed,),
     )
     return token_grad, grad_gate[None], grad_up[None], grad_down[None]
 

time: 223 us -> 223 us (level)
  blocking collectives: 120 us -> 75.1 us
  waiting for transfers between devices: 29.1 us -> 51.4 us
  starting transfers between devices: 24.8 us -> 44.2 us
    all_to_all x3 -> x1, blocking collectives: 120 us -> 75.1 us  [exchange(): return lax.all_to_all(blocks, axis, split_axis=0, concat_axis=0, tiled=True)]
    ppermute x0 -> x6, waiting for transfers between devices: none -> 24.8 us  [swap(): lax.ppermute(blocks[k], axis, [(i, (i + k) % groups) for i in range(group...]
    ppermute x0 -> x6, starting transfers between devices: none -> 21 us  [swap(): lax.ppermute(blocks[k], axis, [(i, (i + k) % groups) for i in range(group...]
    unnamed x12 -> x24, local copies, waits for them, and re-layouts: 2.14 us -> 4.78 us
    reduce_scatter x1, waiting for transfers between devices: 4.07 us -> 1.59 us  [body(): lax.psum_scatter(back_parts, 'rep', scatter_dimension=0, tiled=True)]
    pallas_call x8 -> x9, Pallas kernels: 31.4 us -> 30.7 us  [kernel_call(): pl.pallas_call(body, out_shape=out_shape, in_specs=[pl.BlockSpec(memory_s...]
  transfers between devices with their start and end apart: 4 -> 10, of which waited for: 3 -> 7; matrix products, arithmetic and copies ran while one was open for 1% -> 0% of each run, Pallas kernels for 9% -> 9%
where the time goes in v8:
time: 223 us; the launch traced here: 220 us
  blocking collectives  75.1 us (34%)
  waiting for transfers between devices  51.4 us (23%)
  starting transfers between devices  44.2 us (20%)
  Pallas kernels  30.7 us (14%)
  between operations  13.9 us (6%)
  local copies, waits for them, and re-layouts  4.78 us (2%)
    all_to_all x1, blocking collectives, exchange(): return lax.all_to_all(blocks, axis, split_axis=0, concat_axis=0, tiled=True)  75.1 us
    pallas_call x9, Pallas kernels, kernel_call(): pl.pallas_call(body, out_shape=out_shape, in_specs=[pl.BlockSpec(memory_s...  30.7 us
    ppermute x6, waiting for transfers between devices, swap(): lax.ppermute(blocks[k], axis, [(i, (i + k) % groups) for i in range(group...  24.8 us
    all_to_all x1, starting transfers between devices, exchange(): return lax.all_to_all(blocks, axis, split_axis=0, concat_axis=0, tiled=True)  23.1 us
    ppermute x6, starting transfers between devices, swap(): lax.ppermute(blocks[k], axis, [(i, (i + k) % groups) for i in range(group...  21 us
    all_gather x1, waiting for transfers between devices, body(): terms = lax.all_gather(terms, 'rep', axis=0, tiled=True)  14.8 us
    all_to_all x1, waiting for transfers between devices, exchange(): return lax.all_to_all(blocks, axis, split_axis=0, concat_axis=0, tiled=True)  10.2 us
    unnamed x24, local copies, waits for them, and re-layouts  4.78 us
  transfers between devices with their start and end apart: 10, of which 7 were waited for; matrix products, arithmetic and copies ran while one was open for 0% of the time, Pallas kernels for 9%

profile of v8, /device:TPU:1, one launch (start us, length us, event | category | flops | bytes accessed | tf_op | source)
XLA Modules:
  0.0 220.2 jit_solution(9312831423775262050)
XLA Ops:
  7.2 0.0 all-gather.6.cloned.1.call-start
  7.2 0.0 copy-start.5
  7.2 0.0 copy-start.6
  7.2 0.0 copy-start.7
  7.2 0.0 copy-start.8
  7.3 2.5 %shard_map.104 = bf16[512,1280]{1,0:T(8,128)(2,1)} custom-call(bf16[512,640]{1,0:T(8,128)(2,1)} %bitcast.25, bf16[512,640]{1,0:T(8,128)(2,1)} %bitcast.26), custom_call_target="tpu_custom_call" | custom-call | bytes 2621440 | tf_op jit(solution)/shard_map/pallas_call | solution.py:24
  9.8 0.0 all-gather.6.cloned.1.call-update
  9.8 0.0 reduce-scatter.2.cloned.1.call-start
  9.8 0.0 copy-done.5
  9.9 0.0 copy-done.6
  9.9 0.0 copy-done.7
  9.9 0.0 copy-done.8
  9.9 1.9 shard_map.102
  11.8 0.0 copy-start.2
  11.8 75.1 %all_to_all.10 = bf16[128,8,1152]{2,1,0:T(8,128)(2,1)S(1)} all-to-all(bf16[128,8,1152]{2,1,0:T(8,128)(2,1)S(1)} %bitcast.17), channel_id=1, replica_groups=mesh['rep'=4,'ep'=128] {'ep'}, dimensions={0} | all-to-all | bytes 4718592 | tf_op jit(solution)/shard_map/all_to_all | solution.py:252
  86.8 0.0 copy-done.2
  86.9 1.8 shard_map.103
  88.7 1.2 copy-done.1
  89.8 0.7 copy-done.3
  90.6 0.0 reduce-scatter.2.cloned.1.call-update
  90.6 0.0 all-gather.4.cloned.1.call-start
  90.6 3.1 %collective-permute-start = (bf16[256,640]{1,0:T(8,128)(2,1)S(1)}, bf16[256,640]{1,0:T(8,128)(2,1)S(1)}, u32[]{:S(2)}, u32[]{:S(2)}) collective-permute-start(bf16[256,640]{1,0:T(8,128)(2,1)S(1)} %get-tuple-element.31), channel_id=1, source_target_pairs={{0,128},{128,256},{256,384},{384,0},{1,129},{129,257},{257,385},{3... | collective-permute-start | bytes 983048 | tf_op jit(solution)/shard_map/ppermute | solution.py:258
  93.8 4.3 %collective-permute-start.1 = (bf16[256,640]{1,0:T(8,128)(2,1)S(1)}, bf16[256,640]{1,0:T(8,128)(2,1)S(1)}, u32[]{:S(2)}, u32[]{:S(2)}) collective-permute-start(bf16[256,640]{1,0:T(8,128)(2,1)S(1)} %get-tuple-element.32), channel_id=1, source_target_pairs={{0,256},{128,384},{256,0},{384,128},{1,257},{129,385},{257,1},{385... | collective-permute-start | bytes 983048 | tf_op jit(solution)/shard_map/ppermute | solution.py:258
  98.1 3.1 %collective-permute-start.2 = (bf16[256,640]{1,0:T(8,128)(2,1)S(1)}, bf16[256,640]{1,0:T(8,128)(2,1)S(1)}, u32[]{:S(2)}, u32[]{:S(2)}) collective-permute-start(bf16[256,640]{1,0:T(8,128)(2,1)S(1)} %get-tuple-element.33), channel_id=1, source_target_pairs={{0,384},{128,0},{256,128},{384,256},{1,385},{129,1},{257,129},{385... | collective-permute-start | bytes 983048 | tf_op jit(solution)/shard_map/ppermute | solution.py:258
  101.2 0.0 collective-permute-done.refs_1_
  101.2 0.0 copy-start.9
  101.3 11.7 %collective-permute-done.1.refs_2_ = bf16[256,640]{1,0:T(8,128)(2,1)S(1)} collective-permute-done((bf16[256,640]{1,0:T(8,128)(2,1)S(1)}, bf16[256,640]{1,0:T(8,128)(2,1)S(1)}, u32[]{:S(2)}, u32[]{:S(2)}) %collective-permute-start.1) | collective-permute-done | bytes 327712 | tf_op jit(solution)/shard_map/ppermute | solution.py:258
  113.0 5.1 %collective-permute-done.2.refs_3_ = bf16[256,640]{1,0:T(8,128)(2,1)S(1)} collective-permute-done((bf16[256,640]{1,0:T(8,128)(2,1)S(1)}, bf16[256,640]{1,0:T(8,128)(2,1)S(1)}, u32[]{:S(2)}, u32[]{:S(2)}) %collective-permute-start.2) | collective-permute-done | bytes 327712 | tf_op jit(solution)/shard_map/ppermute | solution.py:258
  118.1 0.7 copy-done.11
  118.8 5.3 %shard_map.105 = (f32[288,640]{1,0:T(8,128)}, f32[288,640]{1,0:T(8,128)}) custom-call(s32[1]{0:T(128)} %bitcast.1.rank_ref, bf16[4,512,1280]{2,1,0:T(8,128)(2,1)} %bitcast.23, bf16[256,640]{1,0:T(8,128)(2,1)} %copy-done.3, bf16[256,640]{1,0:T(8,128)(2,1)} %copy-done.9, bf16[256,640]{1,0:T(8,128)(2,1)} %copy-done.10, bf16[256,640]{1,0:T(8,128)(2,1)} %copy-done.11), custom_call_target="tpu_custom_call" | custom-call | flops 1509949440 | bytes 8028164 | tf_op jit(solution)/shard_map/pallas_call | solution.py:24
  124.2 1.6 reduce-scatter.2.cloned.1.call-done.back_hbm
  125.8 5.6 %shard_map.106 = (bf16[288,1920]{1,0:T(8,128)(2,1)}, bf16[256,640]{1,0:T(8,128)(2,1)}, bf16[256,640]{1,0:T(8,128)(2,1)}, bf16[256,640]{1,0:T(8,128)(2,1)}, bf16[256,640]{1,0:T(8,128)(2,1)}) custom-call(s32[1]{0:T(128)} %bitcast.1.rank_ref, bf16[4,512,1280]{2,1,0:T(8,128)(2,1)} %bitcast.24, f32[288,640]{1,0:T(8,128)} %get-tuple-element.34.gate_hbm, ...), custom_call_target="tpu_custom_call" | custom-call | flops 1509949440 | bytes 9502724 | tf_op jit(solution)/shard_map/pallas_call | solution.py:24
  131.4 0.0 all-gather.4.cloned.1.call-update
  131.4 4.2 %collective-permute-start.3 = (bf16[256,640]{1,0:T(8,128)(2,1)}, bf16[256,640]{1,0:T(8,128)(2,1)S(1)}, u32[]{:S(2)}, u32[]{:S(2)}) collective-permute-start(bf16[256,640]{1,0:T(8,128)(2,1)} %get-tuple-element.42), channel_id=1, source_target_pairs={{0,128},{128,256},{256,384},{384,0},{1,129},{129,257},{257,385},{3... | collective-permute-start | bytes 983048 | tf_op jit(solution)/shard_map/ppermute | solution.py:258
  135.6 3.0 %collective-permute-start.4 = (bf16[256,640]{1,0:T(8,128)(2,1)}, bf16[256,640]{1,0:T(8,128)(2,1)S(1)}, u32[]{:S(2)}, u32[]{:S(2)}) collective-permute-start(bf16[256,640]{1,0:T(8,128)(2,1)} %get-tuple-element.43), channel_id=1, source_target_pairs={{0,256},{128,384},{256,0},{384,128},{1,257},{129,385},{257,1},{385... | collective-permute-start | bytes 983048 | tf_op jit(solution)/shard_map/ppermute | solution.py:258
  138.7 3.2 %collective-permute-start.5 = (bf16[256,640]{1,0:T(8,128)(2,1)}, bf16[256,640]{1,0:T(8,128)(2,1)S(1)}, u32[]{:S(2)}, u32[]{:S(2)}) collective-permute-start(bf16[256,640]{1,0:T(8,128)(2,1)} %get-tuple-element.44), channel_id=1, source_target_pairs={{0,384},{128,0},{256,128},{384,256},{1,385},{129,1},{257,129},{385... | collective-permute-start | bytes 983048 | tf_op jit(solution)/shard_map/ppermute | solution.py:258
  141.9 0.5 collective-permute-done.3.refs_1_
  142.4 7.5 %collective-permute-done.4.refs_2_ = bf16[256,640]{1,0:T(8,128)(2,1)S(1)} collective-permute-done((bf16[256,640]{1,0:T(8,128)(2,1)}, bf16[256,640]{1,0:T(8,128)(2,1)S(1)}, u32[]{:S(2)}, u32[]{:S(2)}) %collective-permute-start.4) | collective-permute-done | bytes 327712 | tf_op jit(solution)/shard_map/ppermute | solution.py:258
  149.9 0.0 collective-permute-done.5.refs_3_
  149.9 1.0 copy-done.4
  150.8 0.1 shard_map.109
  151.0 1.1 copy-done
  152.1 23.1 %all-to-all-start.1 = ((bf16[128,8,640]{2,1,0:T(8,128)(2,1)}), bf16[128,8,640]{2,1,0:T(8,128)(2,1)}, u32[]{:S(2)}, u32[]{:S(2)}) async-start(bf16[128,8,640]{2,1,0:T(8,128)(2,1)} %bitcast.18), calls=%async_computation.2 | async-start | bytes 2621440 | tf_op jit(solution)/shard_map/all_to_all | solution.py:252
  175.2 14.8 %all-gather.4.cloned.1.call-done.terms_ref = bf16[1152,1920]{1,0:T(8,128)(2,1)} async-done(((bf16[288,1920]{1,0:T(8,128)(2,1)}), bf16[1152,1920]{1,0:T(8,128)(2,1)}) %all-gather.4.cloned.1.call-update) | async-done | bytes 4423696 | tf_op jit(solution)/shard_map/all_gather | solution.py:340
  189.9 4.7 %shard_map.108 = bf16[640,512]{1,0:T(8,128)(2,1)} custom-call(bf16[1024,1152]{1,0:T(8,128)(2,1)S(1)} %bitcast.15, bf16[1152,1920]{1,0:T(8,128)(2,1)} %all-gather.4.cloned.1.call-done.terms_ref), custom_call_target="tpu_custom_call" | custom-call | flops 754974720 | bytes 7438336 | tf_op jit(solution)/shard_map/pallas_call | solution.py:24
  194.6 6.1 %shard_map.107 = (bf16[512,640]{1,0:T(8,128)(2,1)}, bf16[512,640]{1,0:T(8,128)(2,1)}) custom-call(bf16[1024,1152]{1,0:T(8,128)(2,1)S(1)} %bitcast.16, bf16[1152,1920]{1,0:T(8,128)(2,1)} %all-gather.4.cloned.1.call-done.terms_ref), custom_call_target="tpu_custom_call" | custom-call | flops 1509949440 | bytes 8093696 | tf_op jit(solution)/shard_map/pallas_call | solution.py:24
  200.7 10.2 %all-to-all-done.1 = bf16[128,8,640]{2,1,0:T(8,128)(2,1)} async-done(((bf16[128,8,640]{2,1,0:T(8,128)(2,1)}), bf16[128,8,640]{2,1,0:T(8,128)(2,1)}, u32[]{:S(2)}, u32[]{:S(2)}) %all-to-all-start.1) | async-done | bytes 1310752 | tf_op jit(solution)/shard_map/all_to_all | solution.py:252
  211.0 2.7 %shard_map.110 = bf16[128,512]{1,0:T(8,128)(2,1)} custom-call(s32[8,128]{1,0:T(8,128)S(1)} %bitcast.21, bf16[1024,640]{1,0:T(8,128)(2,1)} %bitcast.10.rows_ref), custom_call_target="tpu_custom_call" | custom-call | flops 134217728 | bytes 1445888 | tf_op jit(solution)/shard_map/pallas_call | solution.py:24
  (9 shorter events, 0.0 us)
Async XLA Ops:
  7.2 83.4 %all-gather.6.cloned.1.call-start = ((), (), s32[]{:S(2)}) async-start(), calls=%async_computation.5 | async-start | bytes 6553600 | tf_op jit(solution)/shard_map/all_gather | solution.py:280
  7.2 2.6 %copy-start.5 = (bf16[128,512]{1,0:T(8,128)(2,1)S(1)}, bf16[128,512]{1,0:T(8,128)(2,1)}, u32[]{:S(2)}) copy-start(bf16[128,512]{1,0:T(8,128)(2,1)} %tokens_hbm.1) | copy-start | bytes 393220
  7.2 2.6 %copy-start.6 = (bf16[128,512]{1,0:T(8,128)(2,1)S(1)}, bf16[128,512]{1,0:T(8,128)(2,1)}, u32[]{:S(2)}) copy-start(bf16[128,512]{1,0:T(8,128)(2,1)} %grads_hbm.1) | copy-start | bytes 393220
  7.2 2.6 %copy-start.7 = (s32[128,8]{0,1:T(8,128)S(1)}, s32[128,8]{0,1:T(8,128)}, u32[]{:S(2)}) copy-start(s32[128,8]{0,1:T(8,128)} %param.9) | copy-start | bytes 12292
  7.2 2.6 %copy-start.8 = (bf16[128,8]{0,1:T(8,128)(2,1)S(1)}, bf16[128,8]{0,1:T(8,128)(2,1)}, u32[]{:S(2)}) copy-start(bf16[128,8]{0,1:T(8,128)(2,1)} %param.10) | copy-start | bytes 6148
  9.8 116.0 %reduce-scatter.2.cloned.1.call-start = ((), (), s32[]{:S(2)}) async-start(), calls=%async_computation.3 | async-start | bytes 1843200 | tf_op jit(solution)/shard_map/reduce_scatter | solution.py:306
  11.8 75.1 %copy-start.2 = (bf16[1,640,512]{2,1,0:T(8,128)(2,1)S(1)}, bf16[1,640,512]{2,1,0:T(8,128)(2,1)}, u32[]{:S(2)}) copy-start(bf16[1,640,512]{2,1,0:T(8,128)(2,1)} %param.13) | copy-start | bytes 1966084
  88.7 1.2 copy-start.1
  89.8 0.7 copy-start.3
  90.6 99.3 %all-gather.4.cloned.1.call-start = ((), (), s32[]{:S(2)}) async-start(), calls=%async_computation.4 | async-start | bytes 5529600 | tf_op jit(solution)/shard_map/all_gather | solution.py:340
  90.6 10.6 %collective-permute-start = (bf16[256,640]{1,0:T(8,128)(2,1)S(1)}, bf16[256,640]{1,0:T(8,128)(2,1)S(1)}, u32[]{:S(2)}, u32[]{:S(2)}) collective-permute-start(bf16[256,640]{1,0:T(8,128)(2,1)S(1)} %get-tuple-element.31), channel_id=1, source_target_pairs={{0,128},{128,256},{256,384},{384,0},{1,129},{129,257},{257,385},{3... | collective-permute-start | bytes 983048 | tf_op jit(solution)/shard_map/ppermute | solution.py:258
  93.8 19.2 %collective-permute-start.1 = (bf16[256,640]{1,0:T(8,128)(2,1)S(1)}, bf16[256,640]{1,0:T(8,128)(2,1)S(1)}, u32[]{:S(2)}, u32[]{:S(2)}) collective-permute-start(bf16[256,640]{1,0:T(8,128)(2,1)S(1)} %get-tuple-element.32), channel_id=1, source_target_pairs={{0,256},{128,384},{256,0},{384,128},{1,257},{129,385},{257,1},{385... | collective-permute-start | bytes 983048 | tf_op jit(solution)/shard_map/ppermute | solution.py:258
  98.1 19.9 %collective-permute-start.2 = (bf16[256,640]{1,0:T(8,128)(2,1)S(1)}, bf16[256,640]{1,0:T(8,128)(2,1)S(1)}, u32[]{:S(2)}, u32[]{:S(2)}) collective-permute-start(bf16[256,640]{1,0:T(8,128)(2,1)S(1)} %get-tuple-element.33), channel_id=1, source_target_pairs={{0,384},{128,0},{256,128},{384,256},{1,385},{129,1},{257,129},{385... | collective-permute-start | bytes 983048 | tf_op jit(solution)/shard_map/ppermute | solution.py:258
  101.2 17.6 %copy-start.9 = (bf16[256,640]{1,0:T(8,128)(2,1)}, bf16[256,640]{1,0:T(8,128)(2,1)S(1)}, u32[]{:S(2)}) copy-start(bf16[256,640]{1,0:T(8,128)(2,1)S(1)} %collective-permute-done.refs_1_) | copy-start | bytes 983044
  113.0 5.1 %copy-start.10 = (bf16[256,640]{1,0:T(8,128)(2,1)}, bf16[256,640]{1,0:T(8,128)(2,1)S(1)}, u32[]{:S(2)}) copy-start(bf16[256,640]{1,0:T(8,128)(2,1)S(1)} %collective-permute-done.1.refs_2_) | copy-start | bytes 983044
  118.1 0.7 copy-start.11
  131.4 11.0 %collective-permute-start.3 = (bf16[256,640]{1,0:T(8,128)(2,1)}, bf16[256,640]{1,0:T(8,128)(2,1)S(1)}, u32[]{:S(2)}, u32[]{:S(2)}) collective-permute-start(bf16[256,640]{1,0:T(8,128)(2,1)} %get-tuple-element.42), channel_id=1, source_target_pairs={{0,128},{128,256},{256,384},{384,0},{1,129},{129,257},{257,385},{3... | collective-permute-start | bytes 983048 | tf_op jit(solution)/shard_map/ppermute | solution.py:258
  135.6 14.2 %collective-permute-start.4 = (bf16[256,640]{1,0:T(8,128)(2,1)}, bf16[256,640]{1,0:T(8,128)(2,1)S(1)}, u32[]{:S(2)}, u32[]{:S(2)}) collective-permute-start(bf16[256,640]{1,0:T(8,128)(2,1)} %get-tuple-element.43), channel_id=1, source_target_pairs={{0,256},{128,384},{256,0},{384,128},{1,257},{129,385},{257,1},{385... | collective-permute-start | bytes 983048 | tf_op jit(solution)/shard_map/ppermute | solution.py:258
  138.7 11.2 %collective-permute-start.5 = (bf16[256,640]{1,0:T(8,128)(2,1)}, bf16[256,640]{1,0:T(8,128)(2,1)S(1)}, u32[]{:S(2)}, u32[]{:S(2)}) collective-permute-start(bf16[256,640]{1,0:T(8,128)(2,1)} %get-tuple-element.44), channel_id=1, source_target_pairs={{0,384},{128,0},{256,128},{384,256},{1,385},{129,1},{257,129},{385... | collective-permute-start | bytes 983048 | tf_op jit(solution)/shard_map/ppermute | solution.py:258
  149.9 1.0 copy-start.4
  151.0 1.2 copy-start
  152.1 58.8 %all-to-all-start.1 = ((bf16[128,8,640]{2,1,0:T(8,128)(2,1)}), bf16[128,8,640]{2,1,0:T(8,128)(2,1)}, u32[]{:S(2)}, u32[]{:S(2)}) async-start(bf16[128,8,640]{2,1,0:T(8,128)(2,1)} %bitcast.18), calls=%async_computation.2 | async-start | bytes 2621440 | tf_op jit(solution)/shard_map/all_to_all | solution.py:252
Sparse Core Ops, SparseCore 0:
  10.1 67.7 all-gather.5
  90.7 34.9 reduce-scatter.1
  131.5 58.3 all-gather.3

commit v9 on v6

--- a/solution.py
+++ b/solution.py
@@ -99,8 +99,9 @@
     )
 
 
-def grad_products_kernel(rows_ref, down_ref, out_ref, packed):
+def grad_products_kernel(rows_ref, down_ref, out_ref, token_ref, packed):
     quarter = down_ref.shape[1]
+    token_ref[...] = rows_ref[:, : quarter + LANES]
     for at, n, m, rows, extra in row_blocks(rows_ref, packed, quarter, 1):
         out_ref[at : at + n, :] = dot(rows, down_ref[...], CONTRACT_LAST).astype(BF)
         out_ref[at + n : at + n + m, :] = dot(extra, down_ref[...], CONTRACT_LAST).astype(BF)
@@ -243,15 +244,15 @@
         in_hbm=(2, 3),
     )
     rows = exchange(sent.reshape(experts, MAIN, -1), "ep").reshape(main, -1)
-    back_parts = kernel_call(
+    back_parts, token_rows = kernel_call(
         grad_products_kernel,
-        shape((main + experts, ffw), BF),
+        (shape((main + experts, ffw), BF), shape((main, quarter + LANES), BF)),
         (rows, w_down[0]),
         2 * (main + experts) * quarter * ffw,
         (packed,),
     )
     token_rows, back_parts, weights = lax.optimization_barrier(
-        (rows[:, : quarter + LANES], back_parts, weights)
+        (token_rows, back_parts, weights)
     )
     back_sums = lax.psum_scatter(back_parts, "rep", scatter_dimension=0, tiled=True)
     wide_rows = exchange(token_rows.reshape(groups, n, -1), "rep")

time: 220 us -> 220 us (level)
  transfers between devices with their start and end apart: 4 -> 4, of which waited for: 3 -> 3; matrix products, arithmetic and copies ran while one was open for 1% -> 0% of each run, Pallas kernels for 7% -> 7%
where the time goes in v9:
time: 220 us; the launch traced here: 219 us
  blocking collectives  130 us (59%)
  waiting for transfers between devices  34.5 us (16%)
  Pallas kernels  27.2 us (12%)
  between operations  13.8 us (6%)
  starting transfers between devices  11.3 us (5%)
  local copies, waits for them, and re-layouts  3.22 us (1%)
    all_to_all x3, blocking collectives, exchange(): return lax.all_to_all(blocks, axis, split_axis=0, concat_axis=0, tiled=True)  130 us
    pallas_call x7, Pallas kernels, kernel_call(): pl.pallas_call(body, out_shape=out_shape, in_specs=[pl.BlockSpec(memory_s...  27.2 us
    all_gather x1, waiting for transfers between devices, body(): terms = lax.all_gather(terms, 'rep', axis=0, tiled=True)  18.6 us
    all_to_all x1, starting transfers between devices, exchange(): return lax.all_to_all(blocks, axis, split_axis=0, concat_axis=0, tiled=True)  11.1 us
    reduce_scatter x1, waiting for transfers between devices, body(): lax.psum_scatter(back_parts, 'rep', scatter_dimension=0, tiled=True)  9.47 us
    all_to_all x1, waiting for transfers between devices, exchange(): return lax.all_to_all(blocks, axis, split_axis=0, concat_axis=0, tiled=True)  6.33 us
  transfers between devices with their start and end apart: 4, of which 3 were waited for; matrix products, arithmetic and copies ran while one was open for 0% of the time, Pallas kernels for 7%

profile of v9, /device:TPU:1, one launch (start us, length us, event | category | flops | bytes accessed | tf_op | source)
XLA Modules:
  0.0 219.4 jit_solution(14873690560067232261)
XLA Ops:
  7.2 0.0 all-gather.6.cloned.1.call-start
  7.2 2.5 %shard_map.104 = bf16[512,1280]{1,0:T(8,128)(2,1)} custom-call(bf16[512,640]{1,0:T(8,128)(2,1)} %bitcast.24, bf16[512,640]{1,0:T(8,128)(2,1)} %bitcast.25), custom_call_target="tpu_custom_call" | custom-call | bytes 2621440 | tf_op jit(solution)/shard_map/pallas_call | solution.py:24
  9.7 0.0 copy-start.3
  9.7 0.0 copy-start.4
  9.7 0.0 copy-start.5
  9.7 0.0 copy-start.6
  9.7 0.0 all-gather.6.cloned.1.call-update
  9.7 0.0 reduce-scatter.2.cloned.1.call-start
  9.8 0.8 copy-done.3
  10.6 0.1 copy-done.4
  10.6 0.0 copy-done.5
  10.6 0.0 copy-done.6
  10.7 1.8 shard_map.102
  12.5 0.0 copy-start.2
  12.5 75.1 %all_to_all.20 = bf16[128,8,1152]{2,1,0:T(8,128)(2,1)S(1)} all-to-all(bf16[128,8,1152]{2,1,0:T(8,128)(2,1)S(1)} %bitcast.17), channel_id=1, replica_groups=mesh['rep'=4,'ep'=128] {'ep'}, dimensions={0} | all-to-all | bytes 4718592 | tf_op jit(solution)/shard_map/all_to_all | solution.py:211
  87.6 0.0 copy-done.2
  87.6 1.8 shard_map.103
  89.4 0.0 copy-start
  89.4 1.2 copy-done
  90.6 0.0 copy-start.1
  90.6 1.2 copy-done.1
  91.7 0.0 all-gather.6.cloned.1.call-done
  91.7 0.0 reduce-scatter.2.cloned.1.call-update
  91.7 0.0 all-gather.4.cloned.1.call-start
  91.8 25.8 %all_to_all.21.rows_hbm = bf16[4,256,640]{2,1,0:T(8,128)(2,1)} all-to-all(bf16[4,256,640]{2,1,0:T(8,128)(2,1)} %bitcast.18), channel_id=1, replica_groups=mesh['rep'=4,'ep'=128] {'rep'}, dimensions={0} | all-to-all | bytes 2621440 | tf_op jit(solution)/shard_map/all_to_all | solution.py:211
  117.6 9.5 %reduce-scatter.2.cloned.1.call-done.back_hbm = bf16[288,640]{1,0:T(8,128)(2,1)} async-done(((bf16[1152,640]{1,0:T(8,128)(2,1)}), bf16[288,640]{1,0:T(8,128)(2,1)}) %reduce-scatter.2.cloned.1.call-update) | async-done | bytes 368656 | tf_op jit(solution)/shard_map/reduce_scatter | solution.py:257
  127.1 7.6 %shard_map.105 = (bf16[288,1920]{1,0:T(8,128)(2,1)}, bf16[4,256,640]{2,1,0:T(8,128)(2,1)}) custom-call(bf16[4,256,640]{2,1,0:T(8,128)(2,1)} %all_to_all.21.rows_hbm, bf16[4,512,1280]{2,1,0:T(8,128)(2,1)} %bitcast.27, bf16[288,640]{1,0:T(8,128)(2,1)} %reduce-scatter.2.cloned.1.call-done.back_hbm), custom_call_target="tpu_custom_call" | custom-call | flops 3019898880 | bytes 9338880 | tf_op jit(solution)/shard_map/pallas_call | solution.py:24
  134.7 0.0 all-gather.4.cloned.1.call-update
  134.7 28.6 %all_to_all.22 = bf16[4,256,640]{2,1,0:T(8,128)(2,1)} all-to-all(bf16[4,256,640]{2,1,0:T(8,128)(2,1)} %get-tuple-element.26), channel_id=1, replica_groups=mesh['rep'=4,'ep'=128] {'rep'}, dimensions={0} | all-to-all | bytes 2621440 | tf_op jit(solution)/shard_map/all_to_all | solution.py:211
  163.3 11.1 %all-to-all-start.3 = ((bf16[128,8,640]{2,1,0:T(8,128)(2,1)}), bf16[128,8,640]{2,1,0:T(8,128)(2,1)}, u32[]{:S(2)}, u32[]{:S(2)}) async-start(bf16[128,8,640]{2,1,0:T(8,128)(2,1)} %bitcast.23), calls=%async_computation.4 | async-start | bytes 2621440 | tf_op jit(solution)/shard_map/all_to_all | solution.py:211
  174.4 18.6 %all-gather.4.cloned.1.call-done.terms_ref = bf16[1152,1920]{1,0:T(8,128)(2,1)} async-done(((bf16[288,1920]{1,0:T(8,128)(2,1)}), bf16[1152,1920]{1,0:T(8,128)(2,1)}) %all-gather.4.cloned.1.call-update) | async-done | bytes 4423696 | tf_op jit(solution)/shard_map/all_gather | solution.py:274
  193.0 4.7 %shard_map.107 = bf16[640,512]{1,0:T(8,128)(2,1)} custom-call(bf16[1024,1152]{1,0:T(8,128)(2,1)S(1)} %bitcast.15, bf16[1152,1920]{1,0:T(8,128)(2,1)} %all-gather.4.cloned.1.call-done.terms_ref), custom_call_target="tpu_custom_call" | custom-call | flops 754974720 | bytes 7438336 | tf_op jit(solution)/shard_map/pallas_call | solution.py:24
  197.7 6.1 %shard_map.106 = (bf16[512,640]{1,0:T(8,128)(2,1)}, bf16[512,640]{1,0:T(8,128)(2,1)}) custom-call(bf16[1024,1152]{1,0:T(8,128)(2,1)S(1)} %bitcast.16, bf16[1152,1920]{1,0:T(8,128)(2,1)} %all-gather.4.cloned.1.call-done.terms_ref), custom_call_target="tpu_custom_call" | custom-call | flops 1509949440 | bytes 8093696 | tf_op jit(solution)/shard_map/pallas_call | solution.py:24
  203.8 6.3 %all-to-all-done.3 = bf16[128,8,640]{2,1,0:T(8,128)(2,1)} async-done(((bf16[128,8,640]{2,1,0:T(8,128)(2,1)}), bf16[128,8,640]{2,1,0:T(8,128)(2,1)}, u32[]{:S(2)}, u32[]{:S(2)}) %all-to-all-start.3) | async-done | bytes 1310752 | tf_op jit(solution)/shard_map/all_to_all | solution.py:211
  210.2 2.7 %shard_map.108 = bf16[128,512]{1,0:T(8,128)(2,1)} custom-call(s32[8,128]{1,0:T(8,128)S(1)} %bitcast.21, bf16[1024,640]{1,0:T(8,128)(2,1)} %bitcast.10.rows_ref), custom_call_target="tpu_custom_call" | custom-call | flops 134217728 | bytes 1445888 | tf_op jit(solution)/shard_map/pallas_call | solution.py:24
Async XLA Ops:
  7.2 84.5 %all-gather.6.cloned.1.call-start = ((), (), s32[]{:S(2)}) async-start(), calls=%async_computation.7 | async-start | bytes 6553600 | tf_op jit(solution)/shard_map/all_gather | solution.py:231
  9.7 0.9 copy-start.3
  9.7 1.0 copy-start.4
  9.7 1.0 copy-start.5
  9.7 1.0 copy-start.6
  9.7 117.4 %reduce-scatter.2.cloned.1.call-start = ((), (), s32[]{:S(2)}) async-start(), calls=%async_computation.5 | async-start | bytes 1843200 | tf_op jit(solution)/shard_map/reduce_scatter | solution.py:257
  12.5 75.1 %copy-start.2 = (bf16[1,640,512]{2,1,0:T(8,128)(2,1)S(1)}, bf16[1,640,512]{2,1,0:T(8,128)(2,1)}, u32[]{:S(2)}) copy-start(bf16[1,640,512]{2,1,0:T(8,128)(2,1)} %param.13) | copy-start | bytes 1966084
  89.4 1.2 copy-start
  90.6 1.2 copy-start.1
  91.7 101.3 %all-gather.4.cloned.1.call-start = ((), (), s32[]{:S(2)}) async-start(), calls=%async_computation.6 | async-start | bytes 5529600 | tf_op jit(solution)/shard_map/all_gather | solution.py:274
  163.3 46.9 %all-to-all-start.3 = ((bf16[128,8,640]{2,1,0:T(8,128)(2,1)}), bf16[128,8,640]{2,1,0:T(8,128)(2,1)}, u32[]{:S(2)}, u32[]{:S(2)}) async-start(bf16[128,8,640]{2,1,0:T(8,128)(2,1)} %bitcast.23), calls=%async_computation.4 | async-start | bytes 2621440 | tf_op jit(solution)/shard_map/all_to_all | solution.py:211
Sparse Core Ops, SparseCore 0:
  10.1 67.7 all-gather.5
  91.9 35.1 reduce-scatter.1
  134.8 58.1 all-gather.3
